TPU v7x, 32 devices: a whole 2x2x4 slice. The times are simulated.
32 devices in a mesh: grp: 2 (over y), pos: 4 (over z), read: 2 (over x), head: 2 (over core).
Axes of the slice: x: 2, y: 2, z: 4, core: 2. Of those that a mesh axis runs over, the one named last changes fastest.
Arguments:
- latents: bfloat16 [32, 128, 512], P(('grp', 'pos')), parts along dimension 0, may hold values from -6 to 6
- read_tokens: bfloat16 [32, 8, 512, 512], P(('grp', 'pos'), 'read'), parts along dimension 0, may hold values from -166.1 to 166.1
- band_start: int32 [32, 8], P(('grp', 'pos'), 'read'), parts along dimension 0, may hold values from 0 to 511
- coverage: int32 [32, 8], P(('grp', 'pos'), 'read'), parts along dimension 0, may hold values from 1 to 512, as said below
- present: int32 [32, 8], P(('grp', 'pos'), 'read'), parts along dimension 0, may hold values from 0 to 1, as said below
- pattern: int32 [32, 16], P(('grp', 'pos')), parts along dimension 0, may hold values from 0 to 1, as said below
- cross_query: bfloat16 [512, 512], P(None, 'head'), may hold values from -0.25 to 0.25
- cross_key: bfloat16 [512, 512], P(None, 'head'), may hold values from -0.25 to 0.25
- cross_value: bfloat16 [512, 512], P(None, 'head'), may hold values from -0.25 to 0.25
- cross_out: bfloat16 [512, 512], P('head'), may hold values from -0.25 to 0.25
- self_query: bfloat16 [512, 512], P(None, 'head'), may hold values from -3.1 to 3.1
- self_key: bfloat16 [512, 512], P(None, 'head'), may hold values from -0.25 to 0.25
- self_value: bfloat16 [512, 512], P(None, 'head'), may hold values from -0.25 to 0.25
- self_out: bfloat16 [512, 512], P('head'), may hold values from -0.25 to 0.25
Outputs:
- latents_out: bfloat16 [32, 128, 512], P(('grp', 'pos'), 'read', 'head'), parts along dimension 0
There are 2 independent parts, one for each index of `grp`. A program takes and returns all parts, laid end to end along the dimension named above; an argument that names none is the same for every part. Nothing has to cross between parts.
Inputs may be any that keep to these rules, and one draw needn't show every extreme that they name: band_start + coverage <= 512 everywhere. Read 0 is present in every segment. pattern[s, s] = 1; pattern[s, t] may be 1 only where the distance of s and t is a power of two.
All inputs are finite; a program needn't handle non-finite values.
Results may differ from a plain program's by a relative error of at most 0.015.
The roundings to bfloat16 on the way count: a program that leaves them out, or rounds other values in their place, can miss the bound.
Values may be sent and summed in bfloat16 or wider, within the bound.
No kernel may reach another device: no remote copies, remote signals or barrier semaphores. Data moves between devices by JAX's collectives and lax.ppermute only.
A program may use at most 64 MiB of HBM per device.

v0:
```python
import jax
import jax.numpy as jnp
from jax import lax
from jax.sharding import PartitionSpec as P

HD = 64


EPSILON = 1e-06
NEGATIVE_FILL = -1e30


def from_behind(value, axis, steps):
    count = lax.axis_size(axis)
    leading, last = (max(0, -steps), min(count, count - steps))
    return lax.ppermute(value, axis, [(source, source + steps) for source in range(leading, last)])


def rms_rows(values):
    return values * lax.rsqrt(jnp.mean(values * values, axis=-1, keepdims=True) + EPSILON)


def project(input_rows, weight):
    flat_rows = input_rows.reshape(-1, input_rows.shape[-1])
    product = jnp.dot(flat_rows, weight, preferred_element_type=jnp.float32)
    return product.reshape(input_rows.shape[:-1] + (weight.shape[1],))


def pull_block(packed, device_steps, sent_blocks):
    if device_steps == 0:
        return packed
    if device_steps not in sent_blocks:
        sent_blocks[device_steps] = from_behind(packed, "pos", device_steps)
    return sent_blocks[device_steps]


def partner_block(packed, offset, sent_blocks):
    seg_rows = packed.shape[0]
    whole_steps = offset // seg_rows
    remainder = offset % seg_rows
    nearer = pull_block(packed, whole_steps, sent_blocks)
    if remainder == 0:
        return nearer
    farther = pull_block(packed, whole_steps + 1, sent_blocks)
    joined = jnp.concatenate([farther, nearer], axis=0)
    return joined[seg_rows - remainder : 2 * seg_rows - remainder]


def per_device(
    latents,
    read_tokens,
    band_start,
    coverage,
    present,
    pattern,
    cross_query,
    cross_key,
    cross_value,
    cross_out,
    self_query,
    self_key,
    self_value,
    self_out,
):
    seg_local, lat_rows, width = latents.shape
    local_width = cross_query.shape[1]
    local_heads = local_width // HD
    score_scale = HD ** (-0.5)
    latent_float = latents.astype(jnp.float32)
    normed = rms_rows(latent_float).astype(jnp.bfloat16)
    query_rows = (project(normed, cross_query) * score_scale).astype(jnp.bfloat16)
    query_rows = query_rows.reshape(seg_local, lat_rows, local_heads, HD)
    cross_pair = jnp.concatenate([cross_key, cross_value], axis=1)
    positions = jnp.arange(read_tokens.shape[2], dtype=jnp.int32)

    def cross_block(segment_query, current, tokens, first_pos, length, present_flag):
        row_max, row_total, weighted = current
        packed = jnp.dot(tokens, cross_pair, preferred_element_type=jnp.float32).astype(
            jnp.bfloat16
        )
        key_rows = packed[:, :local_width].reshape(-1, local_heads, HD)
        value_rows = packed[:, local_width:].reshape(-1, local_heads, HD)
        live_mask = (
            (positions >= first_pos) & (positions < first_pos + length) & (present_flag > 0)
        )[None, None, :]
        scores = jnp.einsum(
            "qhd,khd->qhk", segment_query, key_rows, preferred_element_type=jnp.float32
        )
        scores = jnp.where(live_mask, scores, NEGATIVE_FILL)
        new_max = jnp.maximum(row_max, jnp.max(scores, axis=-1))
        weights = jnp.where(live_mask, jnp.exp(scores - new_max[..., None]), 0.0)
        factor = jnp.exp(row_max - new_max)
        new_total = row_total * factor + jnp.sum(weights, axis=-1)
        update = jnp.einsum(
            "qhk,khd->qhd",
            weights.astype(jnp.bfloat16),
            value_rows,
            preferred_element_type=jnp.float32,
        )
        return (new_max, new_total, weighted * factor[..., None] + update)

    maxima_list = []
    totals_list = []
    weighted_list = []
    for segment in range(seg_local):
        segment_query = query_rows[segment]

        def read_step(current, block_item):
            tokens, first_pos, length, present_flag = block_item
            return (
                cross_block(segment_query, current, tokens, first_pos, length, present_flag),
                None,
            )

        initial = (
            jnp.full((lat_rows, local_heads), NEGATIVE_FILL, jnp.float32),
            jnp.zeros((lat_rows, local_heads), jnp.float32),
            jnp.zeros((lat_rows, local_heads, HD), jnp.float32),
        )
        final_state, unused = lax.scan(
            read_step,
            initial,
            (read_tokens[segment], band_start[segment], coverage[segment], present[segment]),
        )
        maxima_list.append(final_state[0])
        totals_list.append(final_state[1])
        weighted_list.append(final_state[2])
    local_max = jnp.stack(maxima_list, axis=0)
    local_total = jnp.stack(totals_list, axis=0)
    local_weighted = jnp.stack(weighted_list, axis=0)
    joint_max = lax.pmax(local_max, "read")
    factor = jnp.exp(local_max - joint_max)
    joint_total, joint_weighted = (
        lax.psum((local_total * factor).astype(jnp.bfloat16), "read").astype(jnp.float32),
        lax.psum((local_weighted * factor[..., None]).astype(jnp.bfloat16), "read").astype(
            jnp.float32
        ),
    )
    attended = (
        (joint_weighted / joint_total[..., None])
        .astype(jnp.bfloat16)
        .reshape(seg_local, lat_rows, local_width)
    )
    cross_delta = lax.psum(project(attended, cross_out).astype(jnp.bfloat16), "head").astype(
        jnp.float32
    )
    hidden_state = latent_float + cross_delta
    second_normed = rms_rows(hidden_state).astype(jnp.bfloat16)
    self_pair = jnp.concatenate([self_key, self_value], axis=1)
    self_packed = project(second_normed, self_pair).astype(jnp.bfloat16)
    quarter = lat_rows // lax.axis_size("read")
    first_row = lax.axis_index("read") * quarter
    own_rows = lax.dynamic_slice_in_dim(second_normed, first_row, quarter, 1)
    self_rows = (project(own_rows, self_query) * score_scale).astype(jnp.bfloat16)
    self_rows = self_rows.reshape(seg_local, quarter, local_heads, HD)
    seg_total = pattern.shape[1]
    global_index = lax.axis_index("pos") * seg_local + jnp.arange(seg_local, dtype=jnp.int32)
    offsets = [0]
    distance = 1
    while distance < seg_total:
        offsets.append(distance)
        offsets.append(-distance)
        distance = distance * 2
    columns = jnp.arange(seg_total, dtype=jnp.int32)
    sent_blocks = {}
    block_list = []
    flag_list = []
    for offset in offsets:
        block_list.append(partner_block(self_packed, offset, sent_blocks))
        target = global_index - offset
        flag_list.append(
            jnp.sum(jnp.where(columns[None, :] == target[:, None], pattern, 0), axis=1)
        )
    gathered = jnp.stack(block_list, axis=1).reshape(
        seg_local, len(offsets) * lat_rows, 2 * local_width
    )
    live_mask = jnp.repeat(jnp.stack(flag_list, axis=1) > 0, lat_rows, axis=1)[:, None, None, :]
    key_rows = gathered[..., :local_width].reshape(seg_local, -1, local_heads, HD)
    value_rows = gathered[..., local_width:].reshape(seg_local, -1, local_heads, HD)
    scores = jnp.einsum("sqhd,skhd->sqhk", self_rows, key_rows, preferred_element_type=jnp.float32)
    scores = jnp.where(live_mask, scores, NEGATIVE_FILL)
    self_max = jnp.max(scores, axis=-1)
    weights = jnp.where(live_mask, jnp.exp(scores - self_max[..., None]), 0.0)
    self_total = jnp.sum(weights, axis=-1)
    self_weighted = jnp.einsum(
        "sqhk,skhd->sqhd",
        weights.astype(jnp.bfloat16),
        value_rows,
        preferred_element_type=jnp.float32,
    )
    self_mixed = (
        (self_weighted / self_total[..., None])
        .astype(jnp.bfloat16)
        .reshape(seg_local, quarter, local_width)
    )
    partial_out = project(self_mixed, self_out)
    shared = lax.psum_scatter(
        partial_out.astype(jnp.bfloat16), "head", scatter_dimension=2, tiled=True
    ).astype(jnp.float32)
    share_width = shared.shape[2]
    residual = lax.dynamic_slice(
        hidden_state,
        (0, first_row, lax.axis_index("head") * share_width),
        (seg_local, quarter, share_width),
    )
    return (residual + shared).astype(jnp.bfloat16)


def solution(mesh):
    placed = (
        P(("grp", "pos"), None, None),
        P(("grp", "pos"), "read", None, None),
        P(("grp", "pos"), "read"),
        P(("grp", "pos"), "read"),
        P(("grp", "pos"), "read"),
        P(("grp", "pos"), None),
        P(None, "head"),
        P(None, "head"),
        P(None, "head"),
        P("head", None),
        P(None, "head"),
        P(None, "head"),
        P(None, "head"),
        P("head", None),
    )
    return jax.shard_map(
        per_device,
        mesh=mesh,
        in_specs=placed,
        out_specs=P(("grp", "pos"), "read", "head"),
        check_vma=False,
    )
```

profile of v0, /device:TPU:9, one launch (start us, length us, event | category | flops | bytes accessed | tf_op | source)
XLA Modules:
  0.0 260.3 jit_solution(12135016930209422298)
XLA Ops:
  6.7 6.1 %slice_bitcast_fusion.3 = (bf16[4,512,512]{2,1,0:T(8,128)(2,1)}, bf16[4,512,512]{2,1,0:T(8,128)(2,1)}, bf16[4,512,512]{2,1,0:T(8,128)(2,1)}, bf16[4,512,512]{2,1,0:T(8,128)(2,1)}) fusion(bf16[4,4,512,512]{3,2,1,0:T(8,128)(2,1)} %param.23), kind=kLoop, calls=%fused_computation.111 | loop fusion | bytes 16777216 | tf_op jit(solution)/shard_map/squeeze | solution.py:123
  13.7 27.6 %while.64 = (s32[]{:T(128)}, f32[128,4]{0,1:T(4,128)S(1)}, f32[128,4]{0,1:T(4,128)S(1)}, f32[128,4,64]{0,2,1:T(8,128)S(1)}, s32[4]{0:T(128)S(1)}, /*index=5*/s32...) while((s32[]{:T(128)}, f32[128,4]{0,1:T(4,128)S(1)}, ...), condition=%wide.region_4.5_spmd.clone.clone, body=%wide.region_1.4_spmd.clone.clone.sunk | while | flops 338006528 | bytes 6654667 | solution.py:120
  41.4 27.6 %while.65 = (s32[]{:T(128)}, f32[128,4]{0,1:T(4,128)S(1)}, f32[128,4]{0,1:T(4,128)S(1)}, f32[128,4,64]{0,2,1:T(8,128)S(1)}, s32[4]{0:T(128)S(1)}, /*index=5*/s32...) while((s32[]{:T(128)}, f32[128,4]{0,1:T(4,128)S(1)}, ...), condition=%wide.region_8.9_spmd.clone.clone, body=%wide.region_5.8_spmd.clone.clone.sunk | while | flops 338006528 | bytes 6654667 | solution.py:120
  69.1 28.1 %while.66 = (s32[]{:T(128)}, f32[128,4]{0,1:T(4,128)S(1)}, f32[128,4]{0,1:T(4,128)S(1)}, f32[128,4,64]{0,2,1:T(8,128)S(1)}, s32[4]{0:T(128)S(1)}, /*index=5*/s32...) while((s32[]{:T(128)}, f32[128,4]{0,1:T(4,128)S(1)}, ...), condition=%wide.region_12.13_spmd.clone.clone, body=%wide.region_9.12_spmd.clone.clone.sunk | while | flops 338006528 | bytes 6654667 | solution.py:120
  97.4 27.6 %while.67 = (s32[]{:T(128)}, f32[128,4]{0,1:T(4,128)S(1)}, f32[128,4]{0,1:T(4,128)S(1)}, f32[128,4,64]{0,2,1:T(8,128)S(1)}, s32[4]{0:T(128)S(1)}, /*index=5*/s32...) while((s32[]{:T(128)}, f32[128,4]{0,1:T(4,128)S(1)}, ...), condition=%wide.region_16.17_spmd.clone.clone, body=%wide.region_13.16_spmd.clone.clone.sunk | while | flops 338006528 | bytes 6654667 | solution.py:120
  125.0 4.0 %pmax.7 = f32[4,128,4]{1,2,0:T(4,128)S(1)} all-reduce(f32[4,128,4]{1,2,0:T(4,128)S(1)} %pad_maximum_fusion.2), channel_id=1, replica_groups=mesh['grp'=2,'pos'=4,'read'=2,'head'=2] {'read'}, use_global_device_ids=true, to_apply=%region_17.18 | all-reduce | flops 2048 | bytes 16384 | tf_op jit(solution)/shard_map/pmax | solution.py:131
  129.8 3.8 %psum.22 = bf16[4,128,4]{1,2,0:T(4,128)(2,1)S(1)} all-reduce(bf16[4,128,4]{1,2,0:T(4,128)(2,1)S(1)} %get-tuple-element.646), channel_id=1, replica_groups=mesh['grp'=2,'pos'=4,'read'=2,'head'=2] {'read'}, use_global_device_ids=true, to_apply=%region_19.20 | all-reduce | flops 2048 | bytes 8192 | tf_op jit(solution)/shard_map/psum | solution.py:134
  133.6 21.4 %all-reduce.3.cloned.1.call-done = bf16[4,128,4,64]{1,3,2,0:T(8,128)(2,1)} async-done(((bf16[4,128,4,64]{1,3,2,0:T(8,128)(2,1)}), bf16[4,128,4,64]{1,3,2,0:T(8,128)(2,1)}) %all-reduce.3.cloned.1.call-update) | async-done | bytes 262160 | tf_op jit(solution)/shard_map/psum | solution.py:135
  158.6 18.7 %all-reduce.5.cloned.1.call-done = bf16[4,128,512]{2,1,0:T(8,128)(2,1)} async-done(((bf16[4,128,512]{2,1,0:T(8,128)(2,1)}), bf16[4,128,512]{2,1,0:T(8,128)(2,1)}) %all-reduce.5.cloned.1.call-update) | async-done | bytes 524304 | tf_op jit(solution)/shard_map/psum | solution.py:144
  177.3 2.2 convert_add_fusion
  181.9 3.1 %collective-permute-start = (bf16[4,128,512]{2,1,0:T(8,128)(2,1)S(1)}, bf16[4,128,512]{2,1,0:T(8,128)(2,1)S(1)}, u32[]{:S(2)}, u32[]{:S(2)}) collective-permute-start(bf16[4,128,512]{2,1,0:T(8,128)(2,1)S(1)} %get-tuple-element.689), channel_id=1, source_target_pairs={{0,4},{4,8},{8,12},{1,5},{5,9},{9,13},{2,6},{6,10},{10,14},{3,7},{... | collective-permute-start | bytes 1572872 | tf_op jit(solution)/shard_map/ppermute | solution.py:16
  185.0 2.2 collective-permute-start.1
  187.3 4.9 %collective-permute-start.2 = (bf16[4,128,512]{2,1,0:T(8,128)(2,1)S(1)}, bf16[4,128,512]{2,1,0:T(8,128)(2,1)}, u32[]{:S(2)}, u32[]{:S(2)}) collective-permute-start(bf16[4,128,512]{2,1,0:T(8,128)(2,1)S(1)} %get-tuple-element.689), channel_id=1, source_target_pairs={{0,8},{4,12},{1,9},{5,13},{2,10},{6,14},{3,11},{7,15},{16,24},{20,... | collective-permute-start | bytes 1572872 | tf_op jit(solution)/shard_map/ppermute | solution.py:16
  194.1 3.0 %collective-permute-done = bf16[4,128,512]{2,1,0:T(8,128)(2,1)S(1)} collective-permute-done((bf16[4,128,512]{2,1,0:T(8,128)(2,1)S(1)}, bf16[4,128,512]{2,1,0:T(8,128)(2,1)S(1)}, u32[]{:S(2)}, u32[]{:S(2)}) %collective-permute-start) | collective-permute-done | bytes 524320 | tf_op jit(solution)/shard_map/ppermute | solution.py:16
  197.9 2.0 collective-permute-done.1
  204.1 14.4 %collective-permute-done.2 = bf16[4,128,512]{2,1,0:T(8,128)(2,1)} collective-permute-done((bf16[4,128,512]{2,1,0:T(8,128)(2,1)S(1)}, bf16[4,128,512]{2,1,0:T(8,128)(2,1)}, u32[]{:S(2)}, u32[]{:S(2)}) %collective-permute-start.2) | collective-permute-done | bytes 524320 | tf_op jit(solution)/shard_map/ppermute | solution.py:16
  218.5 1.9 bitcast_dynamic-update-slice_fusion.1
  221.2 2.6 %copy.51 = bf16[4,9,128,512]{3,2,1,0:T(8,128)(2,1)S(1)} copy(bf16[4,9,128,512]{3,2,0,1:T(8,128)(2,1)} %bitcast_dynamic-update-slice_fusion) | data formatting | bytes 9437184 | tf_op jit(solution)/shard_map/stack | solution.py:174
  223.9 1.7 fusion.127
  225.6 4.3 %copy.62 = bf16[4,1152,256]{1,2,0:T(8,128)(2,1)} copy(bf16[4,1152,256]{2,1,0:T(8,128)(2,1)} %get-tuple-element.668) | data formatting | bytes 4718592 | tf_op jit(solution)/shard_map/slice | solution.py:178
  229.9 2.6 copy.52
  232.5 5.0 %fusion.129 = (f32[4,64,4]{1,2,0:T(4,128)S(1)}, bf16[4,64,4,1152]{3,1,2,0:T(8,128)(2,1)}) fusion(bf16[4,1152,4,64]{1,3,2,0:T(8,128)(2,1)} %bitcast.307, bf16[4,64,4,64]{3,2,1,0:T(4,128)(2,1)S(1)} %reshape.155, pred[4,1152]{1,0:T(4,128)(4,1)S(1)} %bitcast.323), kind=kOutput, calls=%fused_computation.227 | convolution fusion | flops 156894336 | bytes 4858368 | tf_op jit(solution)/shard_map/sub | solution.py:183
  237.5 2.5 fusion.82
  241.1 11.0 %reduce-scatter.2.cloned.1.call-done = bf16[4,64,256]{2,1,0:T(8,128)(2,1)} async-done(((bf16[4,64,512]{2,1,0:T(8,128)(2,1)}), bf16[4,64,256]{2,1,0:T(8,128)(2,1)}) %reduce-scatter.2.cloned.1.call-update) | async-done | bytes 131088 | tf_op jit(solution)/shard_map/reduce_scatter | solution.py:197
  (291 shorter events, 98.3 us)
Async XLA Ops:
  6.5 149.5 %copy-start = (bf16[256,512]{1,0:T(8,128)(2,1)S(1)}, bf16[256,512]{1,0:T(8,128)(2,1)}, u32[]{:S(2)}) copy-start(bf16[256,512]{1,0:T(8,128)(2,1)} %param.31) | copy-start | bytes 786436
  6.5 148.5 %all-reduce.3.cloned.1.call-start = ((), (), s32[]{:S(2)}) async-start(), calls=%async_computation.1 | async-start | bytes 524288 | tf_op jit(solution)/shard_map/psum | solution.py:135
  6.6 6.2 %copy-start.4 = (bf16[512,256]{1,0:T(8,128)(2,1)S(1)}, bf16[512,256]{1,0:T(8,128)(2,1)}, u32[]{:S(2)}) copy-start(bf16[512,256]{1,0:T(8,128)(2,1)} %param.29) | copy-start | bytes 786436
  6.6 6.2 %copy-start.1 = (bf16[4,128,512]{2,1,0:T(8,128)(2,1)S(1)}, bf16[4,128,512]{2,1,0:T(8,128)(2,1)}, u32[]{:S(2)}) copy-start(bf16[4,128,512]{2,1,0:T(8,128)(2,1)} %param.22) | copy-start | bytes 1572868
  6.6 6.4 %copy-start.11 = (bf16[512,256]{1,0:T(8,128)(2,1)S(1)}, bf16[512,256]{1,0:T(8,128)(2,1)}, u32[]{:S(2)}) copy-start(bf16[512,256]{1,0:T(8,128)(2,1)} %param.28) | copy-start | bytes 786436
  6.7 6.9 %copy-start.7 = (s32[4,4]{1,0:T(4,128)S(1)}, s32[4,4]{1,0:T(4,128)}, u32[]{:S(2)}) copy-start(s32[4,4]{1,0:T(4,128)} %param.24) | copy-start | bytes 196
  6.7 6.9 %copy-start.8 = (s32[4,4]{1,0:T(4,128)S(1)}, s32[4,4]{1,0:T(4,128)}, u32[]{:S(2)}) copy-start(s32[4,4]{1,0:T(4,128)} %param.26) | copy-start | bytes 196
  6.7 6.9 %copy-start.9 = (s32[4,4]{1,0:T(4,128)S(1)}, s32[4,4]{1,0:T(4,128)}, u32[]{:S(2)}) copy-start(s32[4,4]{1,0:T(4,128)} %param.25) | copy-start | bytes 196
  6.7 6.9 %copy-start.5 = (bf16[512,256]{1,0:T(8,128)(2,1)S(1)}, bf16[512,256]{1,0:T(8,128)(2,1)}, u32[]{:S(2)}) copy-start(bf16[512,256]{1,0:T(8,128)(2,1)} %param.30) | copy-start | bytes 786436
  97.3 60.0 %copy-start.10 = (s32[4,16]{1,0:T(4,128)S(1)}, s32[4,16]{1,0:T(4,128)}, u32[]{:S(2)}) copy-start(s32[4,16]{1,0:T(4,128)} %param.27) | copy-start | bytes 772
  124.9 55.7 %copy-start.12 = (bf16[512,256]{1,0:T(8,128)(2,1)S(1)}, bf16[512,256]{1,0:T(8,128)(2,1)}, u32[]{:S(2)}) copy-start(bf16[512,256]{1,0:T(8,128)(2,1)} %param.34) | copy-start | bytes 786436
  124.9 55.7 %copy-start.13 = (bf16[512,256]{1,0:T(8,128)(2,1)S(1)}, bf16[512,256]{1,0:T(8,128)(2,1)}, u32[]{:S(2)}) copy-start(bf16[512,256]{1,0:T(8,128)(2,1)} %param.33) | copy-start | bytes 786436
  129.0 64.7 %copy-start.6 = (bf16[512,256]{1,0:T(8,128)(2,1)S(1)}, bf16[512,256]{1,0:T(8,128)(2,1)}, u32[]{:S(2)}) copy-start(bf16[512,256]{1,0:T(8,128)(2,1)} %param.32) | copy-start | bytes 786436
  129.8 47.5 %all-reduce.5.cloned.1.call-start = ((), (), s32[]{:S(2)}) async-start(), calls=%async_computation.2 | async-start | bytes 1048576 | tf_op jit(solution)/shard_map/psum | solution.py:144
  157.2 94.9 %reduce-scatter.2.cloned.1.call-start = ((), (), s32[]{:S(2)}) async-start(), calls=%async_computation.3 | async-start | bytes 393216 | tf_op jit(solution)/shard_map/reduce_scatter | solution.py:197
  181.9 15.1 %collective-permute-start = (bf16[4,128,512]{2,1,0:T(8,128)(2,1)S(1)}, bf16[4,128,512]{2,1,0:T(8,128)(2,1)S(1)}, u32[]{:S(2)}, u32[]{:S(2)}) collective-permute-start(bf16[4,128,512]{2,1,0:T(8,128)(2,1)S(1)} %get-tuple-element.689), channel_id=1, source_target_pairs={{0,4},{4,8},{8,12},{1,5},{5,9},{9,13},{2,6},{6,10},{10,14},{3,7},{... | collective-permute-start | bytes 1572872 | tf_op jit(solution)/shard_map/ppermute | solution.py:16
  185.0 14.8 %collective-permute-start.1 = (bf16[4,128,512]{2,1,0:T(8,128)(2,1)S(1)}, bf16[4,128,512]{2,1,0:T(8,128)(2,1)S(1)}, u32[]{:S(2)}, u32[]{:S(2)}) collective-permute-start(bf16[4,128,512]{2,1,0:T(8,128)(2,1)S(1)} %get-tuple-element.689), channel_id=1, source_target_pairs={{4,0},{8,4},{12,8},{5,1},{9,5},{13,9},{6,2},{10,6},{14,10},{7,3},{... | collective-permute-start | bytes 1572872 | tf_op jit(solution)/shard_map/ppermute | solution.py:16
  187.3 31.2 %collective-permute-start.2 = (bf16[4,128,512]{2,1,0:T(8,128)(2,1)S(1)}, bf16[4,128,512]{2,1,0:T(8,128)(2,1)}, u32[]{:S(2)}, u32[]{:S(2)}) collective-permute-start(bf16[4,128,512]{2,1,0:T(8,128)(2,1)S(1)} %get-tuple-element.689), channel_id=1, source_target_pairs={{0,8},{4,12},{1,9},{5,13},{2,10},{6,14},{3,11},{7,15},{16,24},{20,... | collective-permute-start | bytes 1572872 | tf_op jit(solution)/shard_map/ppermute | solution.py:16
  192.2 28.2 %collective-permute-start.3 = (bf16[4,128,512]{2,1,0:T(8,128)(2,1)S(1)}, bf16[4,128,512]{2,1,0:T(8,128)(2,1)S(1)}, u32[]{:S(2)}, u32[]{:S(2)}) collective-permute-start(bf16[4,128,512]{2,1,0:T(8,128)(2,1)S(1)} %get-tuple-element.689), channel_id=1, source_target_pairs={{8,0},{12,4},{9,1},{13,5},{10,2},{14,6},{11,3},{15,7},{24,16},{28,... | collective-permute-start | bytes 1572872 | tf_op jit(solution)/shard_map/ppermute | solution.py:16
  232.5 5.0 %copy-start.2 = (bf16[4,1152,256]{1,2,0:T(8,128)(2,1)S(1)}, bf16[4,1152,256]{1,2,0:T(8,128)(2,1)}, u32[]{:S(2)}) copy-start(bf16[4,1152,256]{1,2,0:T(8,128)(2,1)} %copy.52) | copy-start | bytes 7077892
  237.5 2.6 copy-start.3
Sparse Core Ops, SparseCore 0:
  129.9 25.0 all-reduce.2
  157.4 19.8 all-reduce.4
  241.2 10.8 reduce-scatter.1
where the time goes:
time: 263 us; the launch traced here: 260 us
  waiting for transfers between devices  70.5 us (27%)
  local copies, waits for them, and re-layouts  53.5 us (20%)
  matrix products  47.9 us (18%)
  loops' own time  31 us (12%)
  other arithmetic  24.4 us (9%)
  between operations  13.6 us (5%)
  starting transfers between devices  11.7 us (4%)
  blocking collectives  7.77 us (3%)
    another operation x4, loops' own time, per_device(): lax.scan(read_step, initial, (read_tokens[segment], band_start[segment],...  31 us
    dynamic_slice x48, local copies, waits for them, and re-layouts, per_device(): lax.scan(read_step, initial, (read_tokens[segment], band_start[segment],...  29.3 us
    dot_general x16, matrix products, cross_block(): jnp.dot(tokens, cross_pair, preferred_element_type=jnp.float32)  24.5 us
    psum x1, waiting for transfers between devices, per_device(): lax.psum((local_weighted * factor[..., None]).astype(jnp.bfloat16), 'read')  21.4 us
    ppermute x4, waiting for transfers between devices, from_behind(): lax.ppermute(value, axis, [(source, source + steps) for source in range(l...  19.4 us
    psum x1, waiting for transfers between devices, per_device(): lax.psum(project(attended, cross_out).astype(jnp.bfloat16), 'head')  18.7 us
    ppermute x4, starting transfers between devices, from_behind(): lax.ppermute(value, axis, [(source, source + steps) for source in range(l...  11.6 us
    reduce_scatter x1, waiting for transfers between devices, per_device(): lax.psum_scatter(partial_out.astype(jnp.bfloat16), 'head', scatter_dimens...  11 us
  transfers between devices with their start and end apart: 7, of which 6 were waited for; matrix products, arithmetic and copies ran while one was open for 3% of the time, Pallas kernels for 0%

commit v1 on v0

v1 whole, which is shorter than its diff:
```python
import functools

import jax
import jax.numpy as jnp
from jax import lax
from jax.experimental import pallas as pl
from jax.experimental.pallas import tpu as pltpu
from jax.sharding import PartitionSpec as P

HD = 64
EPSILON = 1e-06
NEG = -1e30
CHUNK = 256
STATS = 128
ROWS = 16
F32 = jnp.float32
BF16 = jnp.bfloat16


def nt_dot(left, right):
    return lax.dot_general(left, right, (((1,), (1,)), ((), ())), preferred_element_type=F32)


def mm(left, right):
    return jnp.dot(left, right, preferred_element_type=F32)


def rms_rows(values):
    return values * lax.rsqrt(jnp.mean(values * values, axis=-1, keepdims=True) + EPSILON)


def spread_queries(query, heads, target):
    rows, width = query.shape
    column_head = lax.broadcasted_iota(jnp.int32, (rows, width), 1) // HD
    for head in range(heads):
        target[head * rows : (head + 1) * rows, :] = jnp.where(
            column_head == head, query.astype(F32), 0.0
        ).astype(BF16)


def tile_fold(values, combine):
    folded = values[:, :128]
    for tile in range(1, values.shape[1] // 128):
        folded = combine(folded, values[:, tile * 128 : (tile + 1) * 128])
    return folded


def attend(chunks, chunk_scores, value_of, scratch):
    score_buf, max_buf, total_buf, acc = scratch
    max_buf[...] = jnp.full(max_buf.shape, NEG, F32)
    total_buf[...] = jnp.zeros(total_buf.shape, F32)
    acc[...] = jnp.zeros(acc.shape, F32)

    def first(chunk, carry):
        scores = chunk_scores(chunk)
        score_buf[chunk] = scores
        max_buf[...] = jnp.maximum(max_buf[...], tile_fold(scores, jnp.maximum))
        return carry

    lax.fori_loop(0, chunks, first, 0)
    row_max = jnp.max(max_buf[...], axis=1, keepdims=True)

    def second(chunk, carry):
        weights = jnp.exp(score_buf[chunk] - row_max)
        total_buf[...] += tile_fold(weights, jnp.add)
        acc[...] += mm(weights.astype(BF16), value_of(chunk))
        return carry

    lax.fori_loop(0, chunks, second, 0)
    return row_max, jnp.sum(total_buf[...], axis=1, keepdims=True)


def emit(segment, row_max, row_total, acc, heads, full, stat_full, own_ref, own_stat_ref, sends):
    readers = len(sends) + 1
    rows, width = full.shape
    part = rows // readers
    lane = lax.broadcasted_iota(jnp.int32, (rows, 128), 1)
    for tile in range(width // 128):
        low, high = 2 * tile, 2 * tile + 1
        cols = slice(tile * 128, (tile + 1) * 128)
        full[:, cols] = jnp.where(
            lane < HD,
            acc[low * rows : (low + 1) * rows, cols],
            acc[high * rows : (high + 1) * rows, cols],
        )
    stats = jnp.zeros((rows, STATS), F32)
    place = 0
    for source in (row_max, row_total):
        for head in range(heads):
            left = source[head * rows : (head + 1) * rows]
            for step in range(3):
                piece = left.astype(BF16).astype(F32)
                stats = jnp.where(lane == place, piece, stats)
                left = left - piece
                place += 1
    stat_full[...] = stats
    reader = lax.axis_index("read")
    for step in range(readers):
        first = pl.multiple_of(lax.rem(reader + step, readers) * part, part)
        if step == 0:
            own_ref[segment] = full[pl.ds(first, part), :]
            own_stat_ref[segment] = stat_full[pl.ds(first, part), :].astype(BF16)
        else:
            sends[step - 1][segment, :, :width] = full[pl.ds(first, part), :].astype(BF16)
            sends[step - 1][segment, :, width:] = stat_full[pl.ds(first, part), :].astype(BF16)


def cross_kernel(
    readers, start_ref, cov_ref, present_ref, lat_ref, tok_ref, wq_ref, wk_ref, wv_ref, *rest
):
    own_ref, own_stat_ref = rest[:2]
    sends = rest[2 : 1 + readers]
    (token_buf, query_buf, spread, score_buf, value_buf, max_buf, total_buf, acc, full, stat_full,
     sems) = rest[1 + readers :]
    segs, lat_rows, width = lat_ref.shape
    reads = tok_ref.shape[1]
    local = wq_ref.shape[1]
    heads = local // HD

    def span(segment, read):
        start = start_ref[segment, read]
        length = cov_ref[segment, read]
        first = (start // ROWS) * ROWS
        last = ((start + length + ROWS - 1) // ROWS) * ROWS
        live = present_ref[segment, read] > 0
        return start - first, jnp.where(live, length, 0), first, jnp.where(live, last - first, 0)

    for segment in range(segs):
        offset = jnp.int32(0)
        for read in range(reads):
            lead, length, first, rows = span(segment, read)

            @pl.when(rows > 0)
            def _(segment=segment, read=read, offset=offset, first=first, rows=rows):
                pltpu.make_async_copy(
                    tok_ref.at[segment, read, pl.ds(pl.multiple_of(first, ROWS), rows), :],
                    token_buf.at[segment, pl.ds(pl.multiple_of(offset, ROWS), rows), :],
                    sems.at[segment],
                ).start()

            offset = offset + rows
        blocks = (((offset + CHUNK - 1) // CHUNK) * CHUNK - offset) // ROWS

        def clear(step, carry, segment=segment, offset=offset):
            token_buf[segment, pl.ds(pl.multiple_of(offset + step * ROWS, ROWS), ROWS), :] = (
                jnp.zeros((ROWS, width), BF16)
            )
            return carry

        lax.fori_loop(0, blocks, clear, 0)

    for segment in range(segs):
        normed = rms_rows(lat_ref[segment].astype(F32)).astype(BF16)
        query_buf[segment] = (mm(normed, wq_ref[...]) * (HD ** (-0.5))).astype(BF16)

    def one_segment(segment, carry):
        spread_queries(query_buf[segment], heads, spread)
        offset = jnp.int32(0)
        bounds = []
        for read in range(reads):
            lead, length, first, rows = span(segment, read)
            bounds.append((offset + lead, offset + lead + length))
            offset = offset + rows

        @pl.when(offset > 0)
        def _():
            landed = token_buf.at[segment, pl.ds(0, offset), :]
            pltpu.make_async_copy(landed, landed, sems.at[segment]).wait()

        def chunk_scores(chunk):
            base = pl.multiple_of(chunk * CHUNK, CHUNK)
            tokens = token_buf[segment, pl.ds(base, CHUNK), :]
            keys = mm(tokens, wk_ref[...]).astype(BF16)
            value_buf[pl.ds(base, CHUNK), :] = mm(tokens, wv_ref[...]).astype(BF16)
            place = base + lax.broadcasted_iota(jnp.int32, (1, CHUNK), 1)
            live = jnp.zeros((1, CHUNK), jnp.bool_)
            for low, high in bounds:
                live = live | ((place >= low) & (place < high))
            return jnp.where(live, nt_dot(spread[...], keys), NEG)

        def value_of(chunk):
            return value_buf[pl.ds(pl.multiple_of(chunk * CHUNK, CHUNK), CHUNK), :]

        chunks = (offset + CHUNK - 1) // CHUNK
        row_max, row_total = attend(
            chunks, chunk_scores, value_of, (score_buf, max_buf, total_buf, acc)
        )
        emit(
            segment, row_max, row_total, acc, heads, full, stat_full, own_ref, own_stat_ref, sends
        )
        return carry

    lax.fori_loop(0, segs, one_segment, 0)


def combine_kernel(own_ref, stat_ref, *rest):
    received, out_ref = rest[:-1], rest[-1]
    width = own_ref.shape[1]
    heads = width // HD
    lane = lax.broadcasted_iota(jnp.int32, (STATS, width), 0)
    head = lax.broadcasted_iota(jnp.int32, (STATS, width), 1) // HD
    pick_max = ((lane // 3) == head).astype(F32).astype(BF16)
    pick_total = ((lane // 3) == head + heads).astype(F32).astype(BF16)
    parts = [(own_ref[...], stat_ref[...])]
    for ref in received:
        parts.append((ref[:, :width].astype(F32), ref[:, width:]))
    maxima = [mm(stat, pick_max) for _, stat in parts]
    totals = [mm(stat, pick_total) for _, stat in parts]
    joint = functools.reduce(jnp.maximum, maxima)
    factors = [jnp.exp(value - joint) for value in maxima]
    total = sum(value * factor for value, factor in zip(totals, factors))
    mixed = sum(part[0] * factor for part, factor in zip(parts, factors))
    out_ref[...] = (mixed / total).astype(BF16)


def hidden_kernel(
    lat_ref, own_ref, other_ref, wo_ref, wp_ref, wq_ref, hid_ref, norm_ref, query_ref
):
    segs, lat_rows, width = lat_ref.shape
    part = own_ref.shape[0] // segs
    first = pl.multiple_of(lax.axis_index("read") * part, part)
    delta = mm(own_ref[...], wo_ref[...]) + mm(other_ref[...], wp_ref[...])
    for segment in range(segs):
        rows = slice(segment * part, (segment + 1) * part)
        hid_ref[rows, :] = lat_ref[segment, pl.ds(first, part), :].astype(F32) + delta[rows]
    normed = rms_rows(hid_ref[...]).astype(BF16)
    norm_ref[...] = normed
    query_ref[...] = (mm(normed, wq_ref[...]) * (HD ** (-0.5))).astype(BF16)


def self_kernel(readers, steps, offsets, pattern_ref, wk_ref, wv_ref, *rest):
    queries = rest[:readers]
    count = 1 + 2 * len(steps)
    blocks = rest[readers : readers + count]
    rest = rest[readers + count :]
    own_ref, own_stat_ref = rest[:2]
    sends = rest[2 : 1 + readers]
    (query_buf, spread, key_all, value_all, key_buf, value_buf, score_buf, max_buf, total_buf, acc,
     full, stat_full) = rest[1 + readers :]
    segs = own_ref.shape[0]
    part = own_ref.shape[1]
    local = wk_ref.shape[1]
    heads = local // HD
    seg_total = pattern_ref.shape[1]
    reader = lax.axis_index("read")
    core = lax.axis_index("head")
    group = lax.axis_index("pos")
    size = segs * part

    key_buf[...] = jnp.zeros(key_buf.shape, BF16)
    value_buf[...] = jnp.zeros(value_buf.shape, BF16)
    for index, block in enumerate(blocks):
        if index == 0:
            slot = 0
        else:
            pair = (index - 1) // 2
            slot = 1 + 2 * pair + (core if index % 2 == 1 else 1 - core)
        place = pl.ds(pl.multiple_of(slot * size, size), size)
        key_all[place, :] = mm(block[...], wk_ref[...]).astype(BF16)
        value_all[place, :] = mm(block[...], wv_ref[...]).astype(BF16)
    for step in range(readers):
        first = pl.multiple_of(lax.rem(reader + readers - step, readers) * part, part)
        for segment in range(segs):
            query_buf[segment, pl.ds(first, part), :] = queries[step][
                segment * part : (segment + 1) * part, :
            ]

    for segment in range(segs):
        spread_queries(query_buf[segment], heads, spread)
        live = jnp.int32(0)
        for offset in offsets:
            block_step = (segment + offset) // segs
            inner = (segment + offset) % segs
            if block_step == 0:
                slot = 0
            else:
                slot = 1 + 2 * steps.index(abs(block_step)) + (1 if block_step > 0 else 0)
            target = group * segs + segment + offset
            inside = (target >= 0) & (target < seg_total)
            flag = pattern_ref[segment, jnp.clip(target, 0, seg_total - 1)]
            chosen = inside & (flag > 0)
            source = (slot * segs + inner) * part

            @pl.when(chosen)
            def _(live=live, source=source):
                place = pl.ds(pl.multiple_of(live * part, part), part)
                key_buf[place, :] = key_all[source : source + part, :]
                value_buf[place, :] = value_all[source : source + part, :]

            live = live + chosen.astype(jnp.int32)

        def chunk_scores(chunk, live=live):
            base = pl.multiple_of(chunk * CHUNK, CHUNK)
            keys = key_buf[pl.ds(base, CHUNK), :]
            place = base + lax.broadcasted_iota(jnp.int32, (1, CHUNK), 1)
            return jnp.where(place < live * part, nt_dot(spread[...], keys), NEG)

        def value_of(chunk):
            return value_buf[pl.ds(pl.multiple_of(chunk * CHUNK, CHUNK), CHUNK), :]

        chunks = (live * part + CHUNK - 1) // CHUNK
        row_max, row_total = attend(
            chunks, chunk_scores, value_of, (score_buf, max_buf, total_buf, acc)
        )
        emit(
            segment, row_max, row_total, acc, heads, full, stat_full, own_ref, own_stat_ref, sends
        )


def out_kernel(hid_ref, own_ref, other_ref, wo_ref, wp_ref, out_ref):
    segs, part, share = out_ref.shape
    cols = pl.ds(pl.multiple_of(lax.axis_index("head") * share, 128), share)
    result = (
        hid_ref[:, cols] + mm(own_ref[...], wo_ref[:, cols]) + mm(other_ref[...], wp_ref[:, cols])
    )
    for segment in range(segs):
        out_ref[segment] = result[segment * part : (segment + 1) * part].astype(BF16)


def cost(flops, moved, exps=0):
    return pl.CostEstimate(flops=int(flops), bytes_accessed=int(moved), transcendentals=int(exps))


def vmem():
    return pl.BlockSpec(memory_space=pltpu.VMEM)


def smem():
    return pl.BlockSpec(memory_space=pltpu.SMEM)


def call(kernel, inputs, outputs, specs=None, scratch=(), estimate=None, limit=None, name=None):
    return pl.pallas_call(
        kernel,
        out_shape=[jax.ShapeDtypeStruct(shape, kind) for shape, kind in outputs],
        in_specs=specs or [vmem() for _ in inputs],
        out_specs=[vmem() for _ in outputs],
        scratch_shapes=list(scratch),
        cost_estimate=estimate,
        compiler_params=pltpu.CompilerParams(vmem_limit_bytes=limit),
        name=name,
    )(*inputs)


def swap_cores(value):
    return lax.ppermute(value, "head", [(0, 1), (1, 0)])


def to_reader(value, step):
    readers = lax.axis_size("read")
    return lax.ppermute(value, "read", [(i, (i + step) % readers) for i in range(readers)])


def both_ways(value, step):
    count = lax.axis_size("pos")
    moves = []
    for place in range(count):
        if place + step < count:
            moves.append((2 * place, 2 * (place + step)))
        if place - step >= 0:
            moves.append((2 * place + 1, 2 * (place - step) + 1))
    return lax.ppermute(value, ("pos", "head"), moves)


def per_device(
    latents, read_tokens, band_start, coverage, present, pattern, cross_query, cross_key,
    cross_value, cross_out, self_query, self_key, self_value, self_out,
):
    segs, lat_rows, width = latents.shape
    reads, length = read_tokens.shape[1:3]
    local = cross_query.shape[1]
    heads = local // HD
    readers = lax.axis_size("read")
    part = lat_rows // readers
    size = segs * part
    seg_total = pattern.shape[1]
    share = width // lax.axis_size("head")
    spread_rows = heads * lat_rows

    offsets = [0]
    distance = 1
    while distance < seg_total:
        offsets += [distance, -distance]
        distance *= 2
    steps = sorted(
        {abs((seg + off) // segs) for off in offsets for seg in range(segs)} - {0}
    )

    cross_out_other = swap_cores(cross_out)
    self_out_other = swap_cores(self_out)

    part_outputs = [((segs, part, local), F32), ((segs, part, STATS), BF16)] + [
        ((segs, part, local + STATS), BF16)
    ] * (readers - 1)
    work = [
        pltpu.VMEM((spread_rows, 128), F32),
        pltpu.VMEM((spread_rows, 128), F32),
        pltpu.VMEM((spread_rows, local), F32),
        pltpu.VMEM((lat_rows, local), F32),
        pltpu.VMEM((lat_rows, STATS), F32),
    ]
    most = reads * length
    produced = call(
        functools.partial(cross_kernel, readers),
        (band_start, coverage, present, latents, read_tokens, cross_query, cross_key, cross_value),
        part_outputs,
        specs=[smem()] * 3
        + [vmem(), pl.BlockSpec(memory_space=pl.ANY), vmem(), vmem(), vmem()],
        scratch=[
            pltpu.VMEM((segs, most, width), BF16),
            pltpu.VMEM((segs, lat_rows, local), BF16),
            pltpu.VMEM((spread_rows, local), BF16),
            pltpu.VMEM((most // CHUNK, spread_rows, CHUNK), F32),
            pltpu.VMEM((most, local), BF16),
        ]
        + work
        + [pltpu.SemaphoreType.DMA((segs,))],
        estimate=cost(
            2 * segs * most * local * (2 * width + 2 * spread_rows),
            2 * segs * most * width,
            segs * most * spread_rows,
        ),
        limit=48 << 20,
        name="cross",
    )

    def combine(parts, name):
        own, own_stat, sends = parts[0], parts[1], parts[2:]
        received = [to_reader(value, step + 1) for step, value in enumerate(sends)]
        inputs = [own.reshape(size, local), own_stat.reshape(size, STATS)] + [
            value.reshape(size, local + STATS) for value in received
        ]
        return call(
            combine_kernel, inputs, [((size, local), BF16)], name=name,
            estimate=cost(8 * size * STATS * local, 8 * size * local),
        )[0]

    attended = combine(produced, "join_reads")
    attended_other = swap_cores(attended)
    hidden, normed, query = call(
        hidden_kernel,
        (latents, attended, attended_other, cross_out, cross_out_other, self_query),
        [((size, width), F32), ((size, width), BF16), ((size, local), BF16)],
        name="hidden",
        estimate=cost(2 * size * width * (width + local), 8 * size * width),
    )
    queries = [query] + [to_reader(query, step) for step in range(1, readers)]
    blocks = [normed]
    direct = {0: normed}
    for step in steps:
        half = step // 2
        source = direct[half] if half and half * 2 == step and half in direct else normed
        direct[step] = both_ways(source, step - half if half in direct and half else step)
    for step in steps:
        blocks += [direct[step], swap_cores(direct[step])]
    keys_most = -(-len(offsets) * part // CHUNK) * CHUNK
    produced = call(
        functools.partial(self_kernel, readers, tuple(steps), tuple(offsets)),
        (pattern, self_key, self_value, *queries, *blocks),
        part_outputs,
        specs=[smem()] + [vmem()] * (2 + len(queries) + len(blocks)),
        scratch=[
            pltpu.VMEM((segs, lat_rows, local), BF16),
            pltpu.VMEM((spread_rows, local), BF16),
            pltpu.VMEM((len(blocks) * size, local), BF16),
            pltpu.VMEM((len(blocks) * size, local), BF16),
            pltpu.VMEM((keys_most, local), BF16),
            pltpu.VMEM((keys_most, local), BF16),
            pltpu.VMEM((keys_most // CHUNK, spread_rows, CHUNK), F32),
        ]
        + work,
        estimate=cost(4 * segs * keys_most * local * spread_rows, 4 * len(blocks) * size * width),
        limit=48 << 20,
        name="within",
    )
    mixed = combine(produced, "join_keys")
    mixed_other = swap_cores(mixed)
    return call(
        out_kernel,
        (hidden, mixed, mixed_other, self_out, self_out_other),
        [((segs, part, share), BF16)],
        name="out",
        estimate=cost(2 * size * width * share, 8 * size * width),
    )[0]


def solution(mesh):
    placed = (
        P(("grp", "pos"), None, None),
        P(("grp", "pos"), "read", None, None),
        P(("grp", "pos"), "read"),
        P(("grp", "pos"), "read"),
        P(("grp", "pos"), "read"),
        P(("grp", "pos"), None),
        P(None, "head"),
        P(None, "head"),
        P(None, "head"),
        P("head", None),
        P(None, "head"),
        P(None, "head"),
        P(None, "head"),
        P("head", None),
    )
    return jax.shard_map(
        per_device,
        mesh=mesh,
        in_specs=placed,
        out_specs=P(("grp", "pos"), "read", "head"),
        check_vma=False,
    )
```

time: 263 us -> 87.8 us (0.33)
  matrix products: 47.9 us -> 0 us
  waiting for transfers between devices: 70.5 us -> 26 us
  local copies, waits for them, and re-layouts: 53.5 us -> 13.1 us
  Pallas kernels: 0 us -> 33.6 us
  loops' own time: 31 us -> 0 us
  other arithmetic: 24.4 us -> 0 us
  between operations: 13.6 us -> 0.12 us
  blocking collectives: 7.77 us -> 0 us
    dot_general x54 -> x0, matrix products: 42.8 us -> none  [the longest x16 24.5 us: cross_block(): jnp.dot(tokens, cross_pair, preferred_element_type=jnp.float32)]
    psum x2 -> x0, waiting for transfers between devices: 40.1 us -> none  [the longest x1 21.4 us: per_device(): lax.psum((local_weighted * factor[..., None]).astype(jnp.bfloat16), 'read')]
    pallas_call x0 -> x6, Pallas kernels: none -> 33.6 us  [call(): pl.pallas_call(kernel, out_shape=[jax.ShapeDtypeStruct(shape, kind) for s...]
    another operation x4 -> x0, loops' own time: 31 us -> none  [per_device(): lax.scan(read_step, initial, (read_tokens[segment], band_start[segment],...]
    dynamic_slice x48 -> x0, local copies, waits for them, and re-layouts: 29.3 us -> none  [per_device(): lax.scan(read_step, initial, (read_tokens[segment], band_start[segment],...]
    reduce_scatter x1 -> x0, waiting for transfers between devices: 11 us -> none  [per_device(): lax.psum_scatter(partial_out.astype(jnp.bfloat16), 'head', scatter_dimens...]
    and x16 -> x0, other arithmetic: 9.8 us -> none  [cross_block(): (positions >= first_pos) & (positions < first_pos + length)]
    slice x24 -> x0, local copies, waits for them, and re-layouts: 9.69 us -> none  [the longest x2 6.06 us: per_device(): gathered[..., :local_width].reshape(seg_local, -1, local_heads, HD)]
  transfers between devices with their start and end apart: 7 -> 11, of which waited for: 6 -> 7; matrix products, arithmetic and copies ran while one was open for 3% -> 0% of each run, Pallas kernels for 0% -> 5%
where the time goes in v1:
time: 87.8 us; the launch traced here: 86.5 us
  Pallas kernels  33.6 us (38%)
  waiting for transfers between devices  26 us (30%)
  starting transfers between devices  13.8 us (16%)
  local copies, waits for them, and re-layouts  13.1 us (15%)
    pallas_call x6, Pallas kernels, call(): pl.pallas_call(kernel, out_shape=[jax.ShapeDtypeStruct(shape, kind) for s...  33.6 us
    ppermute x3, waiting for transfers between devices, to_reader(): lax.ppermute(value, 'read', [(i, (i + step) % readers) for i in range(rea...  14.8 us
    unnamed x48, local copies, waits for them, and re-layouts  13.1 us
    ppermute x6, starting transfers between devices, swap_cores(): return lax.ppermute(value, 'head', [(0, 1), (1, 0)])  9.94 us
    ppermute x2, waiting for transfers between devices, both_ways(): return lax.ppermute(value, ('pos', 'head'), moves)  8.77 us
    ppermute x2, starting transfers between devices, both_ways(): return lax.ppermute(value, ('pos', 'head'), moves)  3.82 us
    ppermute x6, waiting for transfers between devices, swap_cores(): return lax.ppermute(value, 'head', [(0, 1), (1, 0)])  2.39 us
  transfers between devices with their start and end apart: 11, of which 7 were waited for; matrix products, arithmetic and copies ran while one was open for 0% of the time, Pallas kernels for 5%

profile of v1, /device:TPU:9, one launch (start us, length us, event | category | flops | bytes accessed | tf_op | source)
XLA Modules:
  0.0 86.5 jit_solution(7368357310282372442)
XLA Ops:
  0.0 1.0 %copy-done = bf16[4,128,512]{2,1,0:T(8,128)(2,1)S(1)} copy-done((bf16[4,128,512]{2,1,0:T(8,128)(2,1)S(1)}, bf16[4,128,512]{2,1,0:T(8,128)(2,1)}, u32[]{:S(2)}) %copy-start) | copy-done | bytes 524312
  1.0 0.9 %copy-done.5 = bf16[512,256]{1,0:T(8,128)(2,1)S(1)} copy-done((bf16[512,256]{1,0:T(8,128)(2,1)S(1)}, bf16[512,256]{1,0:T(8,128)(2,1)}, u32[]{:S(2)}) %copy-start.5) | copy-done | bytes 262168
  2.0 0.9 %copy-done.6 = bf16[512,256]{1,0:T(8,128)(2,1)S(1)} copy-done((bf16[512,256]{1,0:T(8,128)(2,1)S(1)}, bf16[512,256]{1,0:T(8,128)(2,1)}, u32[]{:S(2)}) %copy-start.6) | copy-done | bytes 262168
  2.9 0.9 %copy-done.7 = bf16[512,256]{1,0:T(8,128)(2,1)S(1)} copy-done((bf16[512,256]{1,0:T(8,128)(2,1)S(1)}, bf16[512,256]{1,0:T(8,128)(2,1)}, u32[]{:S(2)}) %copy-start.7) | copy-done | bytes 262168
  6.0 17.0 %cross.1 = (f32[4,64,256]{2,1,0:T(8,128)S(1)}, bf16[4,64,128]{2,1,0:T(8,128)(2,1)S(1)}, bf16[4,64,384]{2,1,0:T(8,128)(2,1)S(1)}) custom-call(s32[4,4]{1,0:T(4,128)S(1)} %copy-done.12, s32[4,4]{1,0:T(4,128)S(1)} %copy-done.13, s32[4,4]{1,0:T(4,128)S(1)} %copy-done.14, bf16[4,128,512]{2,1,0:T(8,128)(2,1)S(1)} %copy-done, bf16[4,4,512,512]{3,2,1,0:T(8,128)(2,1)} %tok_ref.1, ...), custom_call_target="tpu_custom_call" | custom-call | flops 8589934592 | bytes 8388608 | tf_op jit(solution)/shard_map/cross/pallas_call | solution.py:333
  25.0 5.1 %collective-permute-done = bf16[4,64,384]{2,1,0:T(8,128)(2,1)S(1)} collective-permute-done((bf16[4,64,384]{2,1,0:T(8,128)(2,1)S(1)}, bf16[4,64,384]{2,1,0:T(8,128)(2,1)S(1)}, u32[]{:S(2)}, u32[]{:S(2)}) %collective-permute-start) | collective-permute-done | bytes 196640 | tf_op jit(solution)/shard_map/ppermute | solution.py:351
  30.8 2.0 %join_reads.1.own_ref = bf16[256,256]{1,0:T(8,128)(2,1)} custom-call(f32[256,256]{1,0:T(8,128)} %bitcast.7, bf16[256,128]{1,0:T(8,128)(2,1)} %bitcast.9, bf16[256,384]{1,0:T(8,128)(2,1)} %bitcast.10), custom_call_target="tpu_custom_call" | custom-call | flops 67108864 | bytes 524288 | tf_op jit(solution)/shard_map/join_reads/pallas_call | solution.py:333
  32.8 1.5 %collective-permute-start.1 = (bf16[256,256]{1,0:T(8,128)(2,1)}, bf16[256,256]{1,0:T(8,128)(2,1)S(1)}, u32[]{:S(2)}, u32[]{:S(2)}) collective-permute-start(bf16[256,256]{1,0:T(8,128)(2,1)} %join_reads.1.own_ref), channel_id=1, source_target_pairs={{0,1},{1,0},{2,3},{3,2},{4,5},{5,4},{6,7},{7,6},{8,9},{9,8},{10,11... | collective-permute-start | bytes 393224 | tf_op jit(solution)/shard_map/ppermute | solution.py:346
  34.3 1.2 %collective-permute-done.1.other_ref = bf16[256,256]{1,0:T(8,128)(2,1)S(1)} collective-permute-done((bf16[256,256]{1,0:T(8,128)(2,1)}, bf16[256,256]{1,0:T(8,128)(2,1)S(1)}, u32[]{:S(2)}, u32[]{:S(2)}) %collective-permute-start.1) | collective-permute-done | bytes 131104 | tf_op jit(solution)/shard_map/ppermute | solution.py:346
  36.1 2.7 %hidden.1 = (f32[256,512]{1,0:T(8,128)}, bf16[256,512]{1,0:T(8,128)(2,1)}, bf16[256,256]{1,0:T(8,128)(2,1)}) custom-call(bf16[4,128,512]{2,1,0:T(8,128)(2,1)} %lat_ref.3, bf16[256,256]{1,0:T(8,128)(2,1)} %join_reads.1.own_ref, bf16[256,256]{1,0:T(8,128)(2,1)} %copy-done.22, bf16[256,512]{1,0:T(8,128)(2,1)} %wo_ref.2, bf16[256,512]{1,0:T(8,128)(2,1)} %copy-done.18, ...), custom_call_target="tpu_custom_call" | custom-call | flops 201326592 | bytes 1048576 | tf_op jit(solution)/shard_map/hidden/pallas_call | solution.py:333
  38.8 1.9 %collective-permute-start.4 = (bf16[256,512]{1,0:T(8,128)(2,1)}, bf16[256,512]{1,0:T(8,128)(2,1)S(1)}, u32[]{:S(2)}, u32[]{:S(2)}) collective-permute-start(bf16[256,512]{1,0:T(8,128)(2,1)} %get-tuple-element.19.rest_2_), channel_id=1, source_target_pairs={{0,4},{4,8},{5,1},{8,12},{9,5},{13,9},{2,6},{6,10},{7,3},{10,14},{... | collective-permute-start | bytes 786440 | tf_op jit(solution)/shard_map/ppermute | solution.py:362
  40.7 6.3 %collective-permute-done.4.rest_3_ = bf16[256,512]{1,0:T(8,128)(2,1)S(1)} collective-permute-done((bf16[256,512]{1,0:T(8,128)(2,1)}, bf16[256,512]{1,0:T(8,128)(2,1)S(1)}, u32[]{:S(2)}, u32[]{:S(2)}) %collective-permute-start.4) | collective-permute-done | bytes 262176 | tf_op jit(solution)/shard_map/ppermute | solution.py:362
  47.0 1.9 %collective-permute-start.6 = (bf16[256,512]{1,0:T(8,128)(2,1)S(1)}, bf16[256,512]{1,0:T(8,128)(2,1)S(1)}, u32[]{:S(2)}, u32[]{:S(2)}) collective-permute-start(bf16[256,512]{1,0:T(8,128)(2,1)S(1)} %collective-permute-done.4.rest_3_), channel_id=1, source_target_pairs={{0,4},{4,8},{5,1},{8,12},{9,5},{13,9},{2,6},{6,10},{7,3},{10,14},{... | collective-permute-start | bytes 786440 | tf_op jit(solution)/shard_map/ppermute | solution.py:362
  48.9 3.6 %collective-permute-start.5 = (bf16[256,512]{1,0:T(8,128)(2,1)S(1)}, bf16[256,512]{1,0:T(8,128)(2,1)S(1)}, u32[]{:S(2)}, u32[]{:S(2)}) collective-permute-start(bf16[256,512]{1,0:T(8,128)(2,1)S(1)} %collective-permute-done.4.rest_3_), channel_id=1, source_target_pairs={{0,1},{1,0},{2,3},{3,2},{4,5},{5,4},{6,7},{7,6},{8,9},{9,8},{10,11... | collective-permute-start | bytes 786440 | tf_op jit(solution)/shard_map/ppermute | solution.py:346
  52.5 2.5 %collective-permute-done.6.rest_5_ = bf16[256,512]{1,0:T(8,128)(2,1)S(1)} collective-permute-done((bf16[256,512]{1,0:T(8,128)(2,1)S(1)}, bf16[256,512]{1,0:T(8,128)(2,1)S(1)}, u32[]{:S(2)}, u32[]{:S(2)}) %collective-permute-start.6) | collective-permute-done | bytes 262176 | tf_op jit(solution)/shard_map/ppermute | solution.py:362
  55.0 1.3 %collective-permute-start.7 = (bf16[256,512]{1,0:T(8,128)(2,1)S(1)}, bf16[256,512]{1,0:T(8,128)(2,1)S(1)}, u32[]{:S(2)}, u32[]{:S(2)}) collective-permute-start(bf16[256,512]{1,0:T(8,128)(2,1)S(1)} %collective-permute-done.6.rest_5_), channel_id=1, source_target_pairs={{0,1},{1,0},{2,3},{3,2},{4,5},{5,4},{6,7},{7,6},{8,9},{9,8},{10,11... | collective-permute-start | bytes 786440 | tf_op jit(solution)/shard_map/ppermute | solution.py:346
  56.3 5.3 %collective-permute-done.3.rest_1_ = bf16[256,256]{1,0:T(8,128)(2,1)S(1)} collective-permute-done((bf16[256,256]{1,0:T(8,128)(2,1)}, bf16[256,256]{1,0:T(8,128)(2,1)S(1)}, u32[]{:S(2)}, u32[]{:S(2)}) %collective-permute-start.3) | collective-permute-done | bytes 131104 | tf_op jit(solution)/shard_map/ppermute | solution.py:351
  63.4 7.7 %within.1 = (f32[4,64,256]{2,1,0:T(8,128)S(1)}, bf16[4,64,128]{2,1,0:T(8,128)(2,1)S(1)}, bf16[4,64,384]{2,1,0:T(8,128)(2,1)S(1)}) custom-call(s32[4,16]{1,0:T(4,128)S(1)} %copy-done.15, bf16[512,256]{1,0:T(8,128)(2,1)S(1)} %copy-done.8, bf16[512,256]{1,0:T(8,128)(2,1)S(1)} %copy-done.9, bf16[256,256]{1,0:T(8,128)(2,1)S(1)} %copy-done.11, ...), custom_call_target="tpu_custom_call" | custom-call | flops 1610612736 | bytes 2621440 | tf_op jit(solution)/shard_map/within/pallas_call | solution.py:333
  72.5 1.2 %collective-permute-start.10 = (bf16[256,512]{1,0:T(8,128)(2,1)S(1)}, bf16[256,512]{1,0:T(8,128)(2,1)S(1)}, u32[]{:S(2)}, u32[]{:S(2)}) collective-permute-start(bf16[256,512]{1,0:T(8,128)(2,1)S(1)} %copy-done.17), channel_id=1, source_target_pairs={{0,1},{1,0},{2,3},{3,2},{4,5},{5,4},{6,7},{7,6},{8,9},{9,8},{10,11... | collective-permute-start | bytes 786440 | tf_op jit(solution)/shard_map/ppermute | solution.py:346
  73.6 4.4 %collective-permute-done.8 = bf16[4,64,384]{2,1,0:T(8,128)(2,1)S(1)} collective-permute-done((bf16[4,64,384]{2,1,0:T(8,128)(2,1)S(1)}, bf16[4,64,384]{2,1,0:T(8,128)(2,1)S(1)}, u32[]{:S(2)}, u32[]{:S(2)}) %collective-permute-start.8) | collective-permute-done | bytes 196640 | tf_op jit(solution)/shard_map/ppermute | solution.py:351
  78.7 2.0 %join_keys.1.own_ref = bf16[256,256]{1,0:T(8,128)(2,1)} custom-call(f32[256,256]{1,0:T(8,128)} %bitcast.6, bf16[256,128]{1,0:T(8,128)(2,1)} %bitcast.8, bf16[256,384]{1,0:T(8,128)(2,1)} %bitcast.11), custom_call_target="tpu_custom_call" | custom-call | flops 67108864 | bytes 524288 | tf_op jit(solution)/shard_map/join_keys/pallas_call | solution.py:333
  80.7 1.7 %collective-permute-start.9 = (bf16[256,256]{1,0:T(8,128)(2,1)}, bf16[256,256]{1,0:T(8,128)(2,1)S(1)}, u32[]{:S(2)}, u32[]{:S(2)}) collective-permute-start(bf16[256,256]{1,0:T(8,128)(2,1)} %join_keys.1.own_ref), channel_id=1, source_target_pairs={{0,1},{1,0},{2,3},{3,2},{4,5},{5,4},{6,7},{7,6},{8,9},{9,8},{10,11... | collective-permute-start | bytes 393224 | tf_op jit(solution)/shard_map/ppermute | solution.py:346
  82.5 1.2 %collective-permute-done.9.other_ref = bf16[256,256]{1,0:T(8,128)(2,1)S(1)} collective-permute-done((bf16[256,256]{1,0:T(8,128)(2,1)}, bf16[256,256]{1,0:T(8,128)(2,1)S(1)}, u32[]{:S(2)}, u32[]{:S(2)}) %collective-permute-start.9) | collective-permute-done | bytes 131104 | tf_op jit(solution)/shard_map/ppermute | solution.py:346
  84.3 2.2 %out.1 = bf16[4,64,256]{2,1,0:T(8,128)(2,1)} custom-call(f32[256,512]{1,0:T(8,128)} %get-tuple-element.17.hid_ref, bf16[256,256]{1,0:T(8,128)(2,1)} %join_keys.1.own_ref, bf16[256,256]{1,0:T(8,128)(2,1)} %copy-done.23, bf16[256,512]{1,0:T(8,128)(2,1)} %wo_ref.3, bf16[256,512]{1,0:T(8,128)(2,1)} %copy-done.19), custom_call_target="tpu_custom_call" | custom-call | flops 67108864 | bytes 1048576 | tf_op jit(solution)/shard_map/out/pallas_call | solution.py:333
  (52 shorter events, 9.9 us)
Async XLA Ops:
  0.0 1.0 %copy-start = (bf16[4,128,512]{2,1,0:T(8,128)(2,1)S(1)}, bf16[4,128,512]{2,1,0:T(8,128)(2,1)}, u32[]{:S(2)}) copy-start(bf16[4,128,512]{2,1,0:T(8,128)(2,1)} %lat_ref.3) | copy-start | bytes 1572868
  1.0 0.9 %copy-start.5 = (bf16[512,256]{1,0:T(8,128)(2,1)S(1)}, bf16[512,256]{1,0:T(8,128)(2,1)}, u32[]{:S(2)}) copy-start(bf16[512,256]{1,0:T(8,128)(2,1)} %wq_ref.2) | copy-start | bytes 786436
  2.0 0.9 %copy-start.6 = (bf16[512,256]{1,0:T(8,128)(2,1)S(1)}, bf16[512,256]{1,0:T(8,128)(2,1)}, u32[]{:S(2)}) copy-start(bf16[512,256]{1,0:T(8,128)(2,1)} %wk_ref.2) | copy-start | bytes 786436
  2.9 0.9 %copy-start.7 = (bf16[512,256]{1,0:T(8,128)(2,1)S(1)}, bf16[512,256]{1,0:T(8,128)(2,1)}, u32[]{:S(2)}) copy-start(bf16[512,256]{1,0:T(8,128)(2,1)} %wv_ref.2) | copy-start | bytes 786436
  5.9 18.4 %copy-start.16 = (bf16[256,512]{1,0:T(8,128)(2,1)S(1)}, bf16[256,512]{1,0:T(8,128)(2,1)}, u32[]{:S(2)}) copy-start(bf16[256,512]{1,0:T(8,128)(2,1)} %wo_ref.2) | copy-start | bytes 786436
  5.9 55.6 %copy-start.8 = (bf16[512,256]{1,0:T(8,128)(2,1)S(1)}, bf16[512,256]{1,0:T(8,128)(2,1)}, u32[]{:S(2)}) copy-start(bf16[512,256]{1,0:T(8,128)(2,1)} %wk_ref.3) | copy-start | bytes 786436
  5.9 55.6 %copy-start.9 = (bf16[512,256]{1,0:T(8,128)(2,1)S(1)}, bf16[512,256]{1,0:T(8,128)(2,1)}, u32[]{:S(2)}) copy-start(bf16[512,256]{1,0:T(8,128)(2,1)} %wv_ref.3) | copy-start | bytes 786436
  5.9 55.6 %copy-start.15 = (s32[4,16]{1,0:T(4,128)S(1)}, s32[4,16]{1,0:T(4,128)}, u32[]{:S(2)}) copy-start(s32[4,16]{1,0:T(4,128)} %pattern_ref.1) | copy-start | bytes 772
  6.0 66.5 %copy-start.17 = (bf16[256,512]{1,0:T(8,128)(2,1)S(1)}, bf16[256,512]{1,0:T(8,128)(2,1)}, u32[]{:S(2)}) copy-start(bf16[256,512]{1,0:T(8,128)(2,1)} %wo_ref.3) | copy-start | bytes 786436
  24.3 5.8 %collective-permute-start = (bf16[4,64,384]{2,1,0:T(8,128)(2,1)S(1)}, bf16[4,64,384]{2,1,0:T(8,128)(2,1)S(1)}, u32[]{:S(2)}, u32[]{:S(2)}) collective-permute-start(bf16[4,64,384]{2,1,0:T(8,128)(2,1)S(1)} %get-tuple-element.16), channel_id=1, source_target_pairs={{0,2},{2,0},{1,3},{3,1},{4,6},{6,4},{5,7},{7,5},{8,10},{10,8},{9,1... | collective-permute-start | bytes 589832 | tf_op jit(solution)/shard_map/ppermute | solution.py:351
  24.3 10.0 %collective-permute-start.2 = (bf16[256,512]{1,0:T(8,128)(2,1)S(1)}, bf16[256,512]{1,0:T(8,128)(2,1)S(1)}, u32[]{:S(2)}, u32[]{:S(2)}) collective-permute-start(bf16[256,512]{1,0:T(8,128)(2,1)S(1)} %copy-done.16), channel_id=1, source_target_pairs={{0,1},{1,0},{2,3},{3,2},{4,5},{5,4},{6,7},{7,6},{8,9},{9,8},{10,11... | collective-permute-start | bytes 786440 | tf_op jit(solution)/shard_map/ppermute | solution.py:346
  32.8 2.7 %collective-permute-start.1 = (bf16[256,256]{1,0:T(8,128)(2,1)}, bf16[256,256]{1,0:T(8,128)(2,1)S(1)}, u32[]{:S(2)}, u32[]{:S(2)}) collective-permute-start(bf16[256,256]{1,0:T(8,128)(2,1)} %join_reads.1.own_ref), channel_id=1, source_target_pairs={{0,1},{1,0},{2,3},{3,2},{4,5},{5,4},{6,7},{7,6},{8,9},{9,8},{10,11... | collective-permute-start | bytes 393224 | tf_op jit(solution)/shard_map/ppermute | solution.py:346
  34.3 1.2 %copy-start.18 = (bf16[256,512]{1,0:T(8,128)(2,1)}, bf16[256,512]{1,0:T(8,128)(2,1)S(1)}, u32[]{:S(2)}) copy-start(bf16[256,512]{1,0:T(8,128)(2,1)S(1)} %collective-permute-done.2.wp_ref) | copy-start | bytes 786436
  38.8 8.2 %collective-permute-start.4 = (bf16[256,512]{1,0:T(8,128)(2,1)}, bf16[256,512]{1,0:T(8,128)(2,1)S(1)}, u32[]{:S(2)}, u32[]{:S(2)}) collective-permute-start(bf16[256,512]{1,0:T(8,128)(2,1)} %get-tuple-element.19.rest_2_), channel_id=1, source_target_pairs={{0,4},{4,8},{5,1},{8,12},{9,5},{13,9},{2,6},{6,10},{7,3},{10,14},{... | collective-permute-start | bytes 786440 | tf_op jit(solution)/shard_map/ppermute | solution.py:362
  47.0 8.0 %collective-permute-start.6 = (bf16[256,512]{1,0:T(8,128)(2,1)S(1)}, bf16[256,512]{1,0:T(8,128)(2,1)S(1)}, u32[]{:S(2)}, u32[]{:S(2)}) collective-permute-start(bf16[256,512]{1,0:T(8,128)(2,1)S(1)} %collective-permute-done.4.rest_3_), channel_id=1, source_target_pairs={{0,4},{4,8},{5,1},{8,12},{9,5},{13,9},{2,6},{6,10},{7,3},{10,14},{... | collective-permute-start | bytes 786440 | tf_op jit(solution)/shard_map/ppermute | solution.py:362
  48.9 12.6 %collective-permute-start.5 = (bf16[256,512]{1,0:T(8,128)(2,1)S(1)}, bf16[256,512]{1,0:T(8,128)(2,1)S(1)}, u32[]{:S(2)}, u32[]{:S(2)}) collective-permute-start(bf16[256,512]{1,0:T(8,128)(2,1)S(1)} %collective-permute-done.4.rest_3_), channel_id=1, source_target_pairs={{0,1},{1,0},{2,3},{3,2},{4,5},{5,4},{6,7},{7,6},{8,9},{9,8},{10,11... | collective-permute-start | bytes 786440 | tf_op jit(solution)/shard_map/ppermute | solution.py:346
  55.0 6.6 %collective-permute-start.7 = (bf16[256,512]{1,0:T(8,128)(2,1)S(1)}, bf16[256,512]{1,0:T(8,128)(2,1)S(1)}, u32[]{:S(2)}, u32[]{:S(2)}) collective-permute-start(bf16[256,512]{1,0:T(8,128)(2,1)S(1)} %collective-permute-done.6.rest_5_), channel_id=1, source_target_pairs={{0,1},{1,0},{2,3},{3,2},{4,5},{5,4},{6,7},{7,6},{8,9},{9,8},{10,11... | collective-permute-start | bytes 786440 | tf_op jit(solution)/shard_map/ppermute | solution.py:346
  56.3 5.3 %collective-permute-start.3 = (bf16[256,256]{1,0:T(8,128)(2,1)}, bf16[256,256]{1,0:T(8,128)(2,1)S(1)}, u32[]{:S(2)}, u32[]{:S(2)}) collective-permute-start(bf16[256,256]{1,0:T(8,128)(2,1)} %get-tuple-element.18.rest_0_), channel_id=1, source_target_pairs={{0,2},{2,0},{1,3},{3,1},{4,6},{6,4},{5,7},{7,5},{8,10},{10,8},{9,1... | collective-permute-start | bytes 393224 | tf_op jit(solution)/shard_map/ppermute | solution.py:351
  61.6 1.0 %copy-start.10 = (bf16[256,512]{1,0:T(8,128)(2,1)S(1)}, bf16[256,512]{1,0:T(8,128)(2,1)}, u32[]{:S(2)}) copy-start(bf16[256,512]{1,0:T(8,128)(2,1)} %get-tuple-element.19.rest_2_) | copy-start | bytes 786436
  62.5 0.9 %copy-start.11 = (bf16[256,256]{1,0:T(8,128)(2,1)S(1)}, bf16[256,256]{1,0:T(8,128)(2,1)}, u32[]{:S(2)}) copy-start(bf16[256,256]{1,0:T(8,128)(2,1)} %get-tuple-element.18.rest_0_) | copy-start | bytes 393220
  72.5 5.6 %collective-permute-start.8 = (bf16[4,64,384]{2,1,0:T(8,128)(2,1)S(1)}, bf16[4,64,384]{2,1,0:T(8,128)(2,1)S(1)}, u32[]{:S(2)}, u32[]{:S(2)}) collective-permute-start(bf16[4,64,384]{2,1,0:T(8,128)(2,1)S(1)} %get-tuple-element.22), channel_id=1, source_target_pairs={{0,2},{2,0},{1,3},{3,1},{4,6},{6,4},{5,7},{7,5},{8,10},{10,8},{9,1... | collective-permute-start | bytes 589832 | tf_op jit(solution)/shard_map/ppermute | solution.py:351
  72.5 10.0 %collective-permute-start.10 = (bf16[256,512]{1,0:T(8,128)(2,1)S(1)}, bf16[256,512]{1,0:T(8,128)(2,1)S(1)}, u32[]{:S(2)}, u32[]{:S(2)}) collective-permute-start(bf16[256,512]{1,0:T(8,128)(2,1)S(1)} %copy-done.17), channel_id=1, source_target_pairs={{0,1},{1,0},{2,3},{3,2},{4,5},{5,4},{6,7},{7,6},{8,9},{9,8},{10,11... | collective-permute-start | bytes 786440 | tf_op jit(solution)/shard_map/ppermute | solution.py:346
  80.7 2.9 %collective-permute-start.9 = (bf16[256,256]{1,0:T(8,128)(2,1)}, bf16[256,256]{1,0:T(8,128)(2,1)S(1)}, u32[]{:S(2)}, u32[]{:S(2)}) collective-permute-start(bf16[256,256]{1,0:T(8,128)(2,1)} %join_keys.1.own_ref), channel_id=1, source_target_pairs={{0,1},{1,0},{2,3},{3,2},{4,5},{5,4},{6,7},{7,6},{8,9},{9,8},{10,11... | collective-permute-start | bytes 393224 | tf_op jit(solution)/shard_map/ppermute | solution.py:346
  82.5 1.2 %copy-start.19 = (bf16[256,512]{1,0:T(8,128)(2,1)}, bf16[256,512]{1,0:T(8,128)(2,1)S(1)}, u32[]{:S(2)}) copy-start(bf16[256,512]{1,0:T(8,128)(2,1)S(1)} %collective-permute-done.10.wp_ref) | copy-start | bytes 786436
  (11 other events, 7.3 us)

commit v2 on v1

--- a/solution.py
+++ b/solution.py
@@ -106,12 +106,32 @@
 
 
 def cross_kernel(
-    readers, start_ref, cov_ref, present_ref, lat_ref, tok_ref, wq_ref, wk_ref, wv_ref, *rest
+    readers, start_hbm, cov_hbm, present_hbm, lat_hbm, tok_ref, wq_hbm, wk_hbm, wv_hbm, *rest
 ):
     own_ref, own_stat_ref = rest[:2]
     sends = rest[2 : 1 + readers]
-    (token_buf, query_buf, spread, score_buf, value_buf, max_buf, total_buf, acc, full, stat_full,
-     sems) = rest[1 + readers :]
+    (start_ref, cov_ref, present_ref, lat_ref, wq_ref, wk_ref, wv_ref, token_buf, query_buf, spread,
+     score_buf, value_buf, max_buf, total_buf, acc, full, stat_full, load_sems, sems) = rest[
+        1 + readers :
+    ]
+    loads = [
+        pltpu.make_async_copy(source, target, load_sems.at[index])
+        for index, (source, target) in enumerate(
+            (
+                (start_hbm, start_ref),
+                (cov_hbm, cov_ref),
+                (present_hbm, present_ref),
+                (lat_hbm, lat_ref),
+                (wq_hbm, wq_ref),
+                (wk_hbm, wk_ref),
+                (wv_hbm, wv_ref),
+            )
+        )
+    ]
+    for load in loads:
+        load.start()
+    for load in loads[:3]:
+        load.wait()
     segs, lat_rows, width = lat_ref.shape
     reads = tok_ref.shape[1]
     local = wq_ref.shape[1]
@@ -149,6 +169,8 @@
 
         lax.fori_loop(0, blocks, clear, 0)
 
+    for load in loads[3:]:
+        load.wait()
     for segment in range(segs):
         normed = rms_rows(lat_ref[segment].astype(F32)).astype(BF16)
         query_buf[segment] = (mm(normed, wq_ref[...]) * (HD ** (-0.5))).astype(BF16)
@@ -329,7 +351,7 @@
     return pl.BlockSpec(memory_space=pltpu.SMEM)
 
 
-def call(kernel, inputs, outputs, specs=None, scratch=(), estimate=None, limit=None, name=None):
+def call(kernel, inputs, outputs, specs=None, scratch=(), estimate=None, limit=8 << 20, name=None):
     return pl.pallas_call(
         kernel,
         out_shape=[jax.ShapeDtypeStruct(shape, kind) for shape, kind in outputs],
@@ -404,9 +426,15 @@
         functools.partial(cross_kernel, readers),
         (band_start, coverage, present, latents, read_tokens, cross_query, cross_key, cross_value),
         part_outputs,
-        specs=[smem()] * 3
-        + [vmem(), pl.BlockSpec(memory_space=pl.ANY), vmem(), vmem(), vmem()],
+        specs=[pl.BlockSpec(memory_space=pltpu.HBM)] * 8,
         scratch=[
+            pltpu.SMEM(band_start.shape, jnp.int32),
+            pltpu.SMEM(coverage.shape, jnp.int32),
+            pltpu.SMEM(present.shape, jnp.int32),
+            pltpu.VMEM(latents.shape, BF16),
+            pltpu.VMEM(cross_query.shape, BF16),
+            pltpu.VMEM(cross_key.shape, BF16),
+            pltpu.VMEM(cross_value.shape, BF16),
             pltpu.VMEM((segs, most, width), BF16),
             pltpu.VMEM((segs, lat_rows, local), BF16),
             pltpu.VMEM((spread_rows, local), BF16),
@@ -414,13 +442,13 @@
             pltpu.VMEM((most, local), BF16),
         ]
         + work
-        + [pltpu.SemaphoreType.DMA((segs,))],
+        + [pltpu.SemaphoreType.DMA((7,)), pltpu.SemaphoreType.DMA((segs,))],
         estimate=cost(
             2 * segs * most * local * (2 * width + 2 * spread_rows),
             2 * segs * most * width,
             segs * most * spread_rows,
         ),
-        limit=48 << 20,
+        limit=60 * 1024 * 1024,
         name="cross",
     )
 
@@ -470,7 +498,7 @@
         ]
         + work,
         estimate=cost(4 * segs * keys_most * local * spread_rows, 4 * len(blocks) * size * width),
-        limit=48 << 20,
+        limit=16 << 20,
         name="within",
     )
     mixed = combine(produced, "join_keys")

time: 87.8 us -> 69.5 us (0.79); the launches traced: 86.5 us -> 69.1 us
  local copies, waits for them, and re-layouts: 13.1 us -> 1.82 us
  Pallas kernels: 33.6 us -> 22.4 us
  starting transfers between devices: 13.8 us -> 22.8 us
  waiting for transfers between devices: 26 us -> 21.9 us
    unnamed x48 -> x18, local copies, waits for them, and re-layouts: 13.1 us -> 1.82 us
    pallas_call x6, Pallas kernels: 33.6 us -> 22.4 us  [call(): pl.pallas_call(kernel, out_shape=[jax.ShapeDtypeStruct(shape, kind) for s...]
    ppermute x3, starting transfers between devices: 0.01 us -> 10.2 us  [to_reader(): lax.ppermute(value, 'read', [(i, (i + step) % readers) for i in range(rea...]
    ppermute x3, waiting for transfers between devices: 14.8 us -> 10.5 us  [to_reader(): lax.ppermute(value, 'read', [(i, (i + step) % readers) for i in range(rea...]
    ppermute x6, starting transfers between devices: 9.94 us -> 8.53 us  [swap_cores(): return lax.ppermute(value, 'head', [(0, 1), (1, 0)])]
  transfers between devices with their start and end apart: 11 -> 11, of which waited for: 7 -> 7; matrix products, arithmetic and copies ran while one was open for 0% -> 0% of each run, Pallas kernels for 5% -> 1%
where the time goes in v2:
time: 69.5 us; the launch traced here: 69.1 us
  starting transfers between devices  22.8 us (33%)
  Pallas kernels  22.4 us (32%)
  waiting for transfers between devices  21.9 us (32%)
  local copies, waits for them, and re-layouts  1.82 us (3%)
    pallas_call x6, Pallas kernels, call(): pl.pallas_call(kernel, out_shape=[jax.ShapeDtypeStruct(shape, kind) for s...  22.4 us
    ppermute x3, waiting for transfers between devices, to_reader(): lax.ppermute(value, 'read', [(i, (i + step) % readers) for i in range(rea...  10.5 us
    ppermute x3, starting transfers between devices, to_reader(): lax.ppermute(value, 'read', [(i, (i + step) % readers) for i in range(rea...  10.2 us
    ppermute x2, waiting for transfers between devices, both_ways(): return lax.ppermute(value, ('pos', 'head'), moves)  9.47 us
    ppermute x6, starting transfers between devices, swap_cores(): return lax.ppermute(value, 'head', [(0, 1), (1, 0)])  8.53 us
    ppermute x2, starting transfers between devices, both_ways(): return lax.ppermute(value, ('pos', 'head'), moves)  4.04 us
    ppermute x6, waiting for transfers between devices, swap_cores(): return lax.ppermute(value, 'head', [(0, 1), (1, 0)])  1.98 us
    unnamed x18, local copies, waits for them, and re-layouts  1.82 us
  transfers between devices with their start and end apart: 11, of which 7 were waited for; matrix products, arithmetic and copies ran while one was open for 0% of the time, Pallas kernels for 1%

profile of v2, /device:TPU:9, one launch (start us, length us, event | category | flops | bytes accessed | tf_op | source)
XLA Modules:
  0.0 69.1 jit_solution(2665463249526245147)
XLA Ops:
  0.0 13.6 %cross.1 = (f32[4,64,256]{2,1,0:T(8,128)}, bf16[4,64,128]{2,1,0:T(8,128)(2,1)}, bf16[4,64,384]{2,1,0:T(8,128)(2,1)}) custom-call(s32[4,4]{1,0:T(4,128)} %start_hbm.1, s32[4,4]{1,0:T(4,128)} %cov_hbm.1, s32[4,4]{1,0:T(4,128)} %present_hbm.1, bf16[4,128,512]{2,1,0:T(8,128)(2,1)} %lat_ref.1, bf16[4,4,512,512]{3,2,1,0:T(8,128)(2,1)} %tok_ref.1, ...), custom_call_target="tpu_custom_call" | custom-call | flops 8589934592 | bytes 8388608 | tf_op jit(solution)/shard_map/cross/pallas_call | solution.py:355
  13.7 7.2 %collective-permute-start = (bf16[4,64,384]{2,1,0:T(8,128)(2,1)}, bf16[4,64,384]{2,1,0:T(8,128)(2,1)S(1)}, u32[]{:S(2)}, u32[]{:S(2)}) collective-permute-start(bf16[4,64,384]{2,1,0:T(8,128)(2,1)} %get-tuple-element.16), channel_id=1, source_target_pairs={{0,2},{2,0},{1,3},{3,1},{4,6},{6,4},{5,7},{7,5},{8,10},{10,8},{9,1... | collective-permute-start | bytes 589832 | tf_op jit(solution)/shard_map/ppermute | solution.py:373
  20.9 1.0 %collective-permute-start.2 = (bf16[256,512]{1,0:T(8,128)(2,1)S(1)}, bf16[256,512]{1,0:T(8,128)(2,1)S(1)}, u32[]{:S(2)}, u32[]{:S(2)}) collective-permute-start(bf16[256,512]{1,0:T(8,128)(2,1)S(1)} %copy-done.2), channel_id=1, source_target_pairs={{0,1},{1,0},{2,3},{3,2},{4,5},{5,4},{6,7},{7,6},{8,9},{9,8},{10,11... | collective-permute-start | bytes 786440 | tf_op jit(solution)/shard_map/ppermute | solution.py:368
  21.9 3.9 %collective-permute-done = bf16[4,64,384]{2,1,0:T(8,128)(2,1)S(1)} collective-permute-done((bf16[4,64,384]{2,1,0:T(8,128)(2,1)}, bf16[4,64,384]{2,1,0:T(8,128)(2,1)S(1)}, u32[]{:S(2)}, u32[]{:S(2)}) %collective-permute-start) | collective-permute-done | bytes 196640 | tf_op jit(solution)/shard_map/ppermute | solution.py:373
  25.7 0.9 %copy-done.1 = f32[4,64,256]{2,1,0:T(8,128)S(1)} copy-done((f32[4,64,256]{2,1,0:T(8,128)S(1)}, f32[4,64,256]{2,1,0:T(8,128)}, u32[]{:S(2)}) %copy-start.1) | copy-done | bytes 262168
  26.7 0.8 %copy-done.5 = bf16[4,64,128]{2,1,0:T(8,128)(2,1)S(1)} copy-done((bf16[4,64,128]{2,1,0:T(8,128)(2,1)S(1)}, bf16[4,64,128]{2,1,0:T(8,128)(2,1)}, u32[]{:S(2)}) %copy-start.5) | copy-done | bytes 65560
  27.8 1.3 %collective-permute-start.1 = (bf16[256,256]{1,0:T(8,128)(2,1)S(1)}, bf16[256,256]{1,0:T(8,128)(2,1)S(1)}, u32[]{:S(2)}, u32[]{:S(2)}) collective-permute-start(bf16[256,256]{1,0:T(8,128)(2,1)S(1)} %join_reads.1.own_ref), channel_id=1, source_target_pairs={{0,1},{1,0},{2,3},{3,2},{4,5},{5,4},{6,7},{7,6},{8,9},{9,8},{10,11... | collective-permute-start | bytes 393224 | tf_op jit(solution)/shard_map/ppermute | solution.py:368
  29.2 1.0 %collective-permute-done.1.other_ref = bf16[256,256]{1,0:T(8,128)(2,1)S(1)} collective-permute-done((bf16[256,256]{1,0:T(8,128)(2,1)S(1)}, bf16[256,256]{1,0:T(8,128)(2,1)S(1)}, u32[]{:S(2)}, u32[]{:S(2)}) %collective-permute-start.1) | collective-permute-done | bytes 131104 | tf_op jit(solution)/shard_map/ppermute | solution.py:368
  30.1 0.6 hidden.1
  30.8 2.1 %collective-permute-start.4 = (bf16[256,512]{1,0:T(8,128)(2,1)S(1)}, bf16[256,512]{1,0:T(8,128)(2,1)S(1)}, u32[]{:S(2)}, u32[]{:S(2)}) collective-permute-start(bf16[256,512]{1,0:T(8,128)(2,1)S(1)} %get-tuple-element.19.rest_2_), channel_id=1, source_target_pairs={{0,4},{4,8},{5,1},{8,12},{9,5},{13,9},{2,6},{6,10},{7,3},{10,14},{... | collective-permute-start | bytes 786440 | tf_op jit(solution)/shard_map/ppermute | solution.py:384
  32.9 5.3 %collective-permute-done.4.rest_3_ = bf16[256,512]{1,0:T(8,128)(2,1)S(1)} collective-permute-done((bf16[256,512]{1,0:T(8,128)(2,1)S(1)}, bf16[256,512]{1,0:T(8,128)(2,1)S(1)}, u32[]{:S(2)}, u32[]{:S(2)}) %collective-permute-start.4) | collective-permute-done | bytes 262176 | tf_op jit(solution)/shard_map/ppermute | solution.py:384
  38.2 1.9 %collective-permute-start.6 = (bf16[256,512]{1,0:T(8,128)(2,1)S(1)}, bf16[256,512]{1,0:T(8,128)(2,1)S(1)}, u32[]{:S(2)}, u32[]{:S(2)}) collective-permute-start(bf16[256,512]{1,0:T(8,128)(2,1)S(1)} %collective-permute-done.4.rest_3_), channel_id=1, source_target_pairs={{0,4},{4,8},{5,1},{8,12},{9,5},{13,9},{2,6},{6,10},{7,3},{10,14},{... | collective-permute-start | bytes 786440 | tf_op jit(solution)/shard_map/ppermute | solution.py:384
  40.1 1.3 %collective-permute-start.5 = (bf16[256,512]{1,0:T(8,128)(2,1)S(1)}, bf16[256,512]{1,0:T(8,128)(2,1)S(1)}, u32[]{:S(2)}, u32[]{:S(2)}) collective-permute-start(bf16[256,512]{1,0:T(8,128)(2,1)S(1)} %collective-permute-done.4.rest_3_), channel_id=1, source_target_pairs={{0,1},{1,0},{2,3},{3,2},{4,5},{5,4},{6,7},{7,6},{8,9},{9,8},{10,11... | collective-permute-start | bytes 786440 | tf_op jit(solution)/shard_map/ppermute | solution.py:368
  41.4 4.2 %collective-permute-done.6.rest_5_ = bf16[256,512]{1,0:T(8,128)(2,1)S(1)} collective-permute-done((bf16[256,512]{1,0:T(8,128)(2,1)S(1)}, bf16[256,512]{1,0:T(8,128)(2,1)S(1)}, u32[]{:S(2)}, u32[]{:S(2)}) %collective-permute-start.6) | collective-permute-done | bytes 262176 | tf_op jit(solution)/shard_map/ppermute | solution.py:384
  45.6 2.1 %collective-permute-start.7 = (bf16[256,512]{1,0:T(8,128)(2,1)S(1)}, bf16[256,512]{1,0:T(8,128)(2,1)S(1)}, u32[]{:S(2)}, u32[]{:S(2)}) collective-permute-start(bf16[256,512]{1,0:T(8,128)(2,1)S(1)} %collective-permute-done.6.rest_5_), channel_id=1, source_target_pairs={{0,1},{1,0},{2,3},{3,2},{4,5},{5,4},{6,7},{7,6},{8,9},{9,8},{10,11... | collective-permute-start | bytes 786440 | tf_op jit(solution)/shard_map/ppermute | solution.py:368
  47.7 1.5 %collective-permute-start.3 = (bf16[256,256]{1,0:T(8,128)(2,1)S(1)}, bf16[256,256]{1,0:T(8,128)(2,1)S(1)}, u32[]{:S(2)}, u32[]{:S(2)}) collective-permute-start(bf16[256,256]{1,0:T(8,128)(2,1)S(1)} %get-tuple-element.18.rest_0_), channel_id=1, source_target_pairs={{0,2},{2,0},{1,3},{3,1},{4,6},{6,4},{5,7},{7,5},{8,10},{10,8},{9,1... | collective-permute-start | bytes 393224 | tf_op jit(solution)/shard_map/ppermute | solution.py:373
  49.1 3.6 %collective-permute-done.3.rest_1_ = bf16[256,256]{1,0:T(8,128)(2,1)S(1)} collective-permute-done((bf16[256,256]{1,0:T(8,128)(2,1)S(1)}, bf16[256,256]{1,0:T(8,128)(2,1)S(1)}, u32[]{:S(2)}, u32[]{:S(2)}) %collective-permute-start.3) | collective-permute-done | bytes 131104 | tf_op jit(solution)/shard_map/ppermute | solution.py:373
  52.8 6.6 %within.1 = (f32[4,64,256]{2,1,0:T(8,128)S(1)}, bf16[4,64,128]{2,1,0:T(8,128)(2,1)S(1)}, bf16[4,64,384]{2,1,0:T(8,128)(2,1)S(1)}) custom-call(s32[4,16]{1,0:T(4,128)S(1)} %copy-done.8, bf16[512,256]{1,0:T(8,128)(2,1)S(1)} %copy-done.6, bf16[512,256]{1,0:T(8,128)(2,1)S(1)} %copy-done.7, bf16[256,256]{1,0:T(8,128)(2,1)S(1)} %get-tuple-element.18.rest_0_, ...), custom_call_target="tpu_custom_call" | custom-call | flops 1610612736 | bytes 2621440 | tf_op jit(solution)/shard_map/within/pallas_call | solution.py:355
  59.4 1.5 %collective-permute-start.8 = (bf16[4,64,384]{2,1,0:T(8,128)(2,1)S(1)}, bf16[4,64,384]{2,1,0:T(8,128)(2,1)S(1)}, u32[]{:S(2)}, u32[]{:S(2)}) collective-permute-start(bf16[4,64,384]{2,1,0:T(8,128)(2,1)S(1)} %get-tuple-element.22), channel_id=1, source_target_pairs={{0,2},{2,0},{1,3},{3,1},{4,6},{6,4},{5,7},{7,5},{8,10},{10,8},{9,1... | collective-permute-start | bytes 589832 | tf_op jit(solution)/shard_map/ppermute | solution.py:373
  61.0 1.1 %collective-permute-start.10 = (bf16[256,512]{1,0:T(8,128)(2,1)S(1)}, bf16[256,512]{1,0:T(8,128)(2,1)S(1)}, u32[]{:S(2)}, u32[]{:S(2)}) collective-permute-start(bf16[256,512]{1,0:T(8,128)(2,1)S(1)} %copy-done.4), channel_id=1, source_target_pairs={{0,1},{1,0},{2,3},{3,2},{4,5},{5,4},{6,7},{7,6},{8,9},{9,8},{10,11... | collective-permute-start | bytes 786440 | tf_op jit(solution)/shard_map/ppermute | solution.py:368
  62.1 3.0 %collective-permute-done.8 = bf16[4,64,384]{2,1,0:T(8,128)(2,1)S(1)} collective-permute-done((bf16[4,64,384]{2,1,0:T(8,128)(2,1)S(1)}, bf16[4,64,384]{2,1,0:T(8,128)(2,1)S(1)}, u32[]{:S(2)}, u32[]{:S(2)}) %collective-permute-start.8) | collective-permute-done | bytes 196640 | tf_op jit(solution)/shard_map/ppermute | solution.py:373
  65.4 1.8 %collective-permute-start.9 = (bf16[256,256]{1,0:T(8,128)(2,1)S(1)}, bf16[256,256]{1,0:T(8,128)(2,1)S(1)}, u32[]{:S(2)}, u32[]{:S(2)}) collective-permute-start(bf16[256,256]{1,0:T(8,128)(2,1)S(1)} %join_keys.1.own_ref), channel_id=1, source_target_pairs={{0,1},{1,0},{2,3},{3,2},{4,5},{5,4},{6,7},{7,6},{8,9},{9,8},{10,11... | collective-permute-start | bytes 393224 | tf_op jit(solution)/shard_map/ppermute | solution.py:368
  67.2 1.0 %collective-permute-done.9.other_ref = bf16[256,256]{1,0:T(8,128)(2,1)S(1)} collective-permute-done((bf16[256,256]{1,0:T(8,128)(2,1)S(1)}, bf16[256,256]{1,0:T(8,128)(2,1)S(1)}, u32[]{:S(2)}, u32[]{:S(2)}) %collective-permute-start.9) | collective-permute-done | bytes 131104 | tf_op jit(solution)/shard_map/ppermute | solution.py:368
  68.2 0.9 %out.1 = bf16[4,64,256]{2,1,0:T(8,128)(2,1)} custom-call(f32[256,512]{1,0:T(8,128)S(1)} %get-tuple-element.17.hid_ref, bf16[256,256]{1,0:T(8,128)(2,1)S(1)} %join_keys.1.own_ref, bf16[256,256]{1,0:T(8,128)(2,1)S(1)} %collective-permute-done.9.other_ref, bf16[256,512]{1,0:T(8,128)(2,1)S(1)} %copy-done.4, bf16[256,512]{1,0:T(8,128)(2,1)S(1)} %collective-permute-done.10.wp_ref), custom_call_target="tpu_custom_call" | custom-call | flops 67108864 | bytes 1048576 | tf_op jit(solution)/shard_map/out/pallas_call | solution.py:355
  (22 shorter events, 0.6 us)
Async XLA Ops:
  0.0 30.1 %copy-start = (bf16[4,128,512]{2,1,0:T(8,128)(2,1)S(1)}, bf16[4,128,512]{2,1,0:T(8,128)(2,1)}, u32[]{:S(2)}) copy-start(bf16[4,128,512]{2,1,0:T(8,128)(2,1)} %lat_ref.1) | copy-start | bytes 1572868
  0.0 20.9 %copy-start.2 = (bf16[256,512]{1,0:T(8,128)(2,1)S(1)}, bf16[256,512]{1,0:T(8,128)(2,1)}, u32[]{:S(2)}) copy-start(bf16[256,512]{1,0:T(8,128)(2,1)} %wo_ref.2) | copy-start | bytes 786436
  0.0 30.1 %copy-start.3 = (bf16[512,256]{1,0:T(8,128)(2,1)S(1)}, bf16[512,256]{1,0:T(8,128)(2,1)}, u32[]{:S(2)}) copy-start(bf16[512,256]{1,0:T(8,128)(2,1)} %wq_ref.1) | copy-start | bytes 786436
  0.0 52.7 %copy-start.8 = (s32[4,16]{1,0:T(4,128)S(1)}, s32[4,16]{1,0:T(4,128)}, u32[]{:S(2)}) copy-start(s32[4,16]{1,0:T(4,128)} %pattern_ref.1) | copy-start | bytes 772
  0.0 52.7 %copy-start.6 = (bf16[512,256]{1,0:T(8,128)(2,1)S(1)}, bf16[512,256]{1,0:T(8,128)(2,1)}, u32[]{:S(2)}) copy-start(bf16[512,256]{1,0:T(8,128)(2,1)} %wk_ref.1) | copy-start | bytes 786436
  0.0 52.7 %copy-start.7 = (bf16[512,256]{1,0:T(8,128)(2,1)S(1)}, bf16[512,256]{1,0:T(8,128)(2,1)}, u32[]{:S(2)}) copy-start(bf16[512,256]{1,0:T(8,128)(2,1)} %wv_ref.1) | copy-start | bytes 786436
  0.0 60.9 %copy-start.4 = (bf16[256,512]{1,0:T(8,128)(2,1)S(1)}, bf16[256,512]{1,0:T(8,128)(2,1)}, u32[]{:S(2)}) copy-start(bf16[256,512]{1,0:T(8,128)(2,1)} %wo_ref.3) | copy-start | bytes 786436
  13.7 12.0 %collective-permute-start = (bf16[4,64,384]{2,1,0:T(8,128)(2,1)}, bf16[4,64,384]{2,1,0:T(8,128)(2,1)S(1)}, u32[]{:S(2)}, u32[]{:S(2)}) collective-permute-start(bf16[4,64,384]{2,1,0:T(8,128)(2,1)} %get-tuple-element.16), channel_id=1, source_target_pairs={{0,2},{2,0},{1,3},{3,1},{4,6},{6,4},{5,7},{7,5},{8,10},{10,8},{9,1... | collective-permute-start | bytes 589832 | tf_op jit(solution)/shard_map/ppermute | solution.py:373
  20.9 8.2 %collective-permute-start.2 = (bf16[256,512]{1,0:T(8,128)(2,1)S(1)}, bf16[256,512]{1,0:T(8,128)(2,1)S(1)}, u32[]{:S(2)}, u32[]{:S(2)}) collective-permute-start(bf16[256,512]{1,0:T(8,128)(2,1)S(1)} %copy-done.2), channel_id=1, source_target_pairs={{0,1},{1,0},{2,3},{3,2},{4,5},{5,4},{6,7},{7,6},{8,9},{9,8},{10,11... | collective-permute-start | bytes 786440 | tf_op jit(solution)/shard_map/ppermute | solution.py:368
  25.7 1.0 %copy-start.1 = (f32[4,64,256]{2,1,0:T(8,128)S(1)}, f32[4,64,256]{2,1,0:T(8,128)}, u32[]{:S(2)}) copy-start(f32[4,64,256]{2,1,0:T(8,128)} %get-tuple-element.14) | copy-start | bytes 786436
  26.7 0.8 %copy-start.5 = (bf16[4,64,128]{2,1,0:T(8,128)(2,1)S(1)}, bf16[4,64,128]{2,1,0:T(8,128)(2,1)}, u32[]{:S(2)}) copy-start(bf16[4,64,128]{2,1,0:T(8,128)(2,1)} %get-tuple-element.15) | copy-start | bytes 196612
  27.8 2.3 %collective-permute-start.1 = (bf16[256,256]{1,0:T(8,128)(2,1)S(1)}, bf16[256,256]{1,0:T(8,128)(2,1)S(1)}, u32[]{:S(2)}, u32[]{:S(2)}) collective-permute-start(bf16[256,256]{1,0:T(8,128)(2,1)S(1)} %join_reads.1.own_ref), channel_id=1, source_target_pairs={{0,1},{1,0},{2,3},{3,2},{4,5},{5,4},{6,7},{7,6},{8,9},{9,8},{10,11... | collective-permute-start | bytes 393224 | tf_op jit(solution)/shard_map/ppermute | solution.py:368
  30.8 7.4 %collective-permute-start.4 = (bf16[256,512]{1,0:T(8,128)(2,1)S(1)}, bf16[256,512]{1,0:T(8,128)(2,1)S(1)}, u32[]{:S(2)}, u32[]{:S(2)}) collective-permute-start(bf16[256,512]{1,0:T(8,128)(2,1)S(1)} %get-tuple-element.19.rest_2_), channel_id=1, source_target_pairs={{0,4},{4,8},{5,1},{8,12},{9,5},{13,9},{2,6},{6,10},{7,3},{10,14},{... | collective-permute-start | bytes 786440 | tf_op jit(solution)/shard_map/ppermute | solution.py:384
  38.2 7.4 %collective-permute-start.6 = (bf16[256,512]{1,0:T(8,128)(2,1)S(1)}, bf16[256,512]{1,0:T(8,128)(2,1)S(1)}, u32[]{:S(2)}, u32[]{:S(2)}) collective-permute-start(bf16[256,512]{1,0:T(8,128)(2,1)S(1)} %collective-permute-done.4.rest_3_), channel_id=1, source_target_pairs={{0,4},{4,8},{5,1},{8,12},{9,5},{13,9},{2,6},{6,10},{7,3},{10,14},{... | collective-permute-start | bytes 786440 | tf_op jit(solution)/shard_map/ppermute | solution.py:384
  40.1 12.6 %collective-permute-start.5 = (bf16[256,512]{1,0:T(8,128)(2,1)S(1)}, bf16[256,512]{1,0:T(8,128)(2,1)S(1)}, u32[]{:S(2)}, u32[]{:S(2)}) collective-permute-start(bf16[256,512]{1,0:T(8,128)(2,1)S(1)} %collective-permute-done.4.rest_3_), channel_id=1, source_target_pairs={{0,1},{1,0},{2,3},{3,2},{4,5},{5,4},{6,7},{7,6},{8,9},{9,8},{10,11... | collective-permute-start | bytes 786440 | tf_op jit(solution)/shard_map/ppermute | solution.py:368
  45.6 7.1 %collective-permute-start.7 = (bf16[256,512]{1,0:T(8,128)(2,1)S(1)}, bf16[256,512]{1,0:T(8,128)(2,1)S(1)}, u32[]{:S(2)}, u32[]{:S(2)}) collective-permute-start(bf16[256,512]{1,0:T(8,128)(2,1)S(1)} %collective-permute-done.6.rest_5_), channel_id=1, source_target_pairs={{0,1},{1,0},{2,3},{3,2},{4,5},{5,4},{6,7},{7,6},{8,9},{9,8},{10,11... | collective-permute-start | bytes 786440 | tf_op jit(solution)/shard_map/ppermute | solution.py:368
  47.7 5.1 %collective-permute-start.3 = (bf16[256,256]{1,0:T(8,128)(2,1)S(1)}, bf16[256,256]{1,0:T(8,128)(2,1)S(1)}, u32[]{:S(2)}, u32[]{:S(2)}) collective-permute-start(bf16[256,256]{1,0:T(8,128)(2,1)S(1)} %get-tuple-element.18.rest_0_), channel_id=1, source_target_pairs={{0,2},{2,0},{1,3},{3,1},{4,6},{6,4},{5,7},{7,5},{8,10},{10,8},{9,1... | collective-permute-start | bytes 393224 | tf_op jit(solution)/shard_map/ppermute | solution.py:373
  59.4 5.7 %collective-permute-start.8 = (bf16[4,64,384]{2,1,0:T(8,128)(2,1)S(1)}, bf16[4,64,384]{2,1,0:T(8,128)(2,1)S(1)}, u32[]{:S(2)}, u32[]{:S(2)}) collective-permute-start(bf16[4,64,384]{2,1,0:T(8,128)(2,1)S(1)} %get-tuple-element.22), channel_id=1, source_target_pairs={{0,2},{2,0},{1,3},{3,1},{4,6},{6,4},{5,7},{7,5},{8,10},{10,8},{9,1... | collective-permute-start | bytes 589832 | tf_op jit(solution)/shard_map/ppermute | solution.py:373
  61.0 6.2 %collective-permute-start.10 = (bf16[256,512]{1,0:T(8,128)(2,1)S(1)}, bf16[256,512]{1,0:T(8,128)(2,1)S(1)}, u32[]{:S(2)}, u32[]{:S(2)}) collective-permute-start(bf16[256,512]{1,0:T(8,128)(2,1)S(1)} %copy-done.4), channel_id=1, source_target_pairs={{0,1},{1,0},{2,3},{3,2},{4,5},{5,4},{6,7},{7,6},{8,9},{9,8},{10,11... | collective-permute-start | bytes 786440 | tf_op jit(solution)/shard_map/ppermute | solution.py:368
  65.4 2.7 %collective-permute-start.9 = (bf16[256,256]{1,0:T(8,128)(2,1)S(1)}, bf16[256,256]{1,0:T(8,128)(2,1)S(1)}, u32[]{:S(2)}, u32[]{:S(2)}) collective-permute-start(bf16[256,256]{1,0:T(8,128)(2,1)S(1)} %join_keys.1.own_ref), channel_id=1, source_target_pairs={{0,1},{1,0},{2,3},{3,2},{4,5},{5,4},{6,7},{7,6},{8,9},{9,8},{10,11... | collective-permute-start | bytes 393224 | tf_op jit(solution)/shard_map/ppermute | solution.py:368

commit v3 on v2

--- a/solution.py
+++ b/solution.py
@@ -75,24 +75,23 @@
     rows, width = full.shape
     part = rows // readers
     lane = lax.broadcasted_iota(jnp.int32, (rows, 128), 1)
+    filled = row_total > 0
+    divisor = jnp.where(filled, row_total, 1.0)
+    level = jnp.where(filled, row_max + jnp.log(divisor), NEG)
     for tile in range(width // 128):
-        low, high = 2 * tile, 2 * tile + 1
+        low = slice(2 * tile * rows, (2 * tile + 1) * rows)
+        high = slice((2 * tile + 1) * rows, (2 * tile + 2) * rows)
         cols = slice(tile * 128, (tile + 1) * 128)
-        full[:, cols] = jnp.where(
-            lane < HD,
-            acc[low * rows : (low + 1) * rows, cols],
-            acc[high * rows : (high + 1) * rows, cols],
+        full[:, cols] = jnp.where(lane < HD, acc[low, cols], acc[high, cols]) / jnp.where(
+            lane < HD, divisor[low], divisor[high]
         )
     stats = jnp.zeros((rows, STATS), F32)
-    place = 0
-    for source in (row_max, row_total):
-        for head in range(heads):
-            left = source[head * rows : (head + 1) * rows]
-            for step in range(3):
-                piece = left.astype(BF16).astype(F32)
-                stats = jnp.where(lane == place, piece, stats)
-                left = left - piece
-                place += 1
+    for head in range(heads):
+        left = level[head * rows : (head + 1) * rows]
+        for step in range(3):
+            piece = left.astype(BF16).astype(F32)
+            stats = jnp.where(lane == 3 * head + step, piece, stats)
+            left = left - piece
     stat_full[...] = stats
     reader = lax.axis_index("read")
     for step in range(readers):
@@ -110,10 +109,9 @@
 ):
     own_ref, own_stat_ref = rest[:2]
     sends = rest[2 : 1 + readers]
-    (start_ref, cov_ref, present_ref, lat_ref, wq_ref, wk_ref, wv_ref, token_buf, query_buf, spread,
-     score_buf, value_buf, max_buf, total_buf, acc, full, stat_full, load_sems, sems) = rest[
-        1 + readers :
-    ]
+    (start_ref, cov_ref, present_ref, seg_of, low_of, high_of, lat_ref, wq_ref, wk_ref, wv_ref,
+     token_buf, spread, key_buf, score_buf, value_buf, max_buf, total_buf, acc, full, stat_full,
+     load_sems, sems) = rest[1 + readers :]
     loads = [
         pltpu.make_async_copy(source, target, load_sems.at[index])
         for index, (source, target) in enumerate(
@@ -137,102 +135,162 @@
     local = wq_ref.shape[1]
     heads = local // HD
 
-    def span(segment, read):
-        start = start_ref[segment, read]
-        length = cov_ref[segment, read]
-        first = (start // ROWS) * ROWS
-        last = ((start + length + ROWS - 1) // ROWS) * ROWS
-        live = present_ref[segment, read] > 0
-        return start - first, jnp.where(live, length, 0), first, jnp.where(live, last - first, 0)
-
+    used = jnp.int32(0)
     for segment in range(segs):
-        offset = jnp.int32(0)
+        offset = used * CHUNK
         for read in range(reads):
-            lead, length, first, rows = span(segment, read)
-
-            @pl.when(rows > 0)
+            start = start_ref[segment, read]
+            length = cov_ref[segment, read]
+            live = present_ref[segment, read] > 0
+            first = (start // ROWS) * ROWS
+            last = ((start + length + ROWS - 1) // ROWS) * ROWS
+            rows = jnp.where(live, last - first, 0)
+            low_of[segment, read] = offset + start - first
+            high_of[segment, read] = offset + jnp.where(live, start - first + length, 0)
+
+            @pl.when(live)
             def _(segment=segment, read=read, offset=offset, first=first, rows=rows):
                 pltpu.make_async_copy(
                     tok_ref.at[segment, read, pl.ds(pl.multiple_of(first, ROWS), rows), :],
-                    token_buf.at[segment, pl.ds(pl.multiple_of(offset, ROWS), rows), :],
+                    token_buf.at[pl.ds(pl.multiple_of(offset, ROWS), rows), :],
                     sems.at[segment],
                 ).start()
 
             offset = offset + rows
-        blocks = (((offset + CHUNK - 1) // CHUNK) * CHUNK - offset) // ROWS
-
-        def clear(step, carry, segment=segment, offset=offset):
-            token_buf[segment, pl.ds(pl.multiple_of(offset + step * ROWS, ROWS), ROWS), :] = (
-                jnp.zeros((ROWS, width), BF16)
+        low_of[segment, reads] = offset - used * CHUNK
+        chunks = (offset - used * CHUNK + CHUNK - 1) // CHUNK
+
+        def clear(step, carry, offset=offset):
+            token_buf[pl.ds(pl.multiple_of(offset + step * ROWS, ROWS), ROWS), :] = jnp.zeros(
+                (ROWS, width), BF16
             )
             return carry
 
-        lax.fori_loop(0, blocks, clear, 0)
-
+        lax.fori_loop(0, ((used + chunks) * CHUNK - offset) // ROWS, clear, 0)
+
+        def note(step, carry, segment=segment, used=used):
+            seg_of[used + step] = segment
+            return carry
+
+        lax.fori_loop(0, chunks, note, 0)
+        used = used + chunks
+    for step in range(3):
+        seg_of[used + step] = segs
+    for read in range(reads):
+        low_of[segs, read] = 0
+        high_of[segs, read] = 0
+
+    max_buf[...] = jnp.full(max_buf.shape, NEG, F32)
+    total_buf[...] = jnp.zeros(total_buf.shape, F32)
+    acc[...] = jnp.zeros(acc.shape, F32)
     for load in loads[3:]:
         load.wait()
     for segment in range(segs):
         normed = rms_rows(lat_ref[segment].astype(F32)).astype(BF16)
-        query_buf[segment] = (mm(normed, wq_ref[...]) * (HD ** (-0.5))).astype(BF16)
-
-    def one_segment(segment, carry):
-        spread_queries(query_buf[segment], heads, spread)
-        offset = jnp.int32(0)
-        bounds = []
-        for read in range(reads):
-            lead, length, first, rows = span(segment, read)
-            bounds.append((offset + lead, offset + lead + length))
-            offset = offset + rows
-
-        @pl.when(offset > 0)
+        query = (mm(normed, wq_ref[...]) * (HD ** (-0.5))).astype(BF16)
+        spread_queries(query, heads, spread.at[segment])
+
+    def landed(segment):
+        size = pl.multiple_of(low_of[segment, reads], ROWS)
+        whole = token_buf.at[pl.ds(0, size), :]
+        pltpu.make_async_copy(whole, whole, sems.at[segment]).wait()
+
+    def projected(pair):
+        place = pl.ds(pl.multiple_of(pair * 2 * CHUNK, 2 * CHUNK), 2 * CHUNK)
+        tokens = token_buf[place, :]
+        key_buf[lax.rem(pair, 2)] = mm(tokens, wk_ref[...]).astype(BF16)
+        value_buf[place, :] = mm(tokens, wv_ref[...]).astype(BF16)
+
+    def arrive(chunk, before):
+        upcoming = seg_of[chunk]
+
+        @pl.when((upcoming != before) & (upcoming < segs))
         def _():
-            landed = token_buf.at[segment, pl.ds(0, offset), :]
-            pltpu.make_async_copy(landed, landed, sems.at[segment]).wait()
-
-        def chunk_scores(chunk):
-            base = pl.multiple_of(chunk * CHUNK, CHUNK)
-            tokens = token_buf[segment, pl.ds(base, CHUNK), :]
-            keys = mm(tokens, wk_ref[...]).astype(BF16)
-            value_buf[pl.ds(base, CHUNK), :] = mm(tokens, wv_ref[...]).astype(BF16)
-            place = base + lax.broadcasted_iota(jnp.int32, (1, CHUNK), 1)
+            landed(upcoming)
+
+    pairs = (used + 1) // 2
+
+    @pl.when(used > 0)
+    def _():
+        arrive(0, -1)
+        arrive(1, seg_of[0])
+        projected(jnp.int32(0))
+
+    def first_pass(pair, carry):
+        chunk = 2 * pair
+        arrive(chunk + 2, seg_of[chunk + 1])
+        arrive(chunk + 3, seg_of[chunk + 2])
+        keys = key_buf[lax.rem(pair, 2)]
+        segments = [seg_of[chunk], seg_of[chunk + 1]]
+        for half in range(2):
+            segment = segments[half]
+            place = (chunk + half) * CHUNK + lax.broadcasted_iota(jnp.int32, (1, CHUNK), 1)
             live = jnp.zeros((1, CHUNK), jnp.bool_)
-            for low, high in bounds:
-                live = live | ((place >= low) & (place < high))
-            return jnp.where(live, nt_dot(spread[...], keys), NEG)
-
-        def value_of(chunk):
-            return value_buf[pl.ds(pl.multiple_of(chunk * CHUNK, CHUNK), CHUNK), :]
-
-        chunks = (offset + CHUNK - 1) // CHUNK
-        row_max, row_total = attend(
-            chunks, chunk_scores, value_of, (score_buf, max_buf, total_buf, acc)
-        )
+            for read in range(reads):
+                live = live | (
+                    (place >= low_of[segment, read]) & (place < high_of[segment, read])
+                )
+            for block in range(2):
+                size = acc.shape[1] // 2
+                rows = slice(block * size, (block + 1) * size)
+                scores = nt_dot(
+                    spread[segment, rows], keys[half * CHUNK : (half + 1) * CHUNK]
+                )
+                scores = jnp.where(live, scores, NEG)
+                score_buf[chunk + half, rows] = scores
+                max_buf[segment, rows] = jnp.maximum(
+                    max_buf[segment, rows], tile_fold(scores, jnp.maximum)
+                )
+        projected(pair + 1)
+        return carry
+
+    lax.fori_loop(0, pairs, first_pass, 0)
+    for segment in range(segs):
+        row_max = jnp.max(max_buf[segment], axis=1, keepdims=True)
+        max_buf[segment] = jnp.broadcast_to(row_max, max_buf.shape[1:])
+
+    def second_pass(pair, carry):
+        for half in range(2):
+            chunk = 2 * pair + half
+            segment = seg_of[chunk]
+            value = value_buf[pl.ds(pl.multiple_of(chunk * CHUNK, CHUNK), CHUNK), :]
+            for block in range(2):
+                rows = slice(block * acc.shape[1] // 2, (block + 1) * acc.shape[1] // 2)
+                weights = jnp.exp(
+                    score_buf[chunk, rows] - jnp.tile(max_buf[segment, rows], (1, CHUNK // 128))
+                )
+                total_buf[segment, rows] += tile_fold(weights, jnp.add)
+                acc[segment, rows] += mm(weights.astype(BF16), value)
+        return carry
+
+    lax.fori_loop(0, pairs, second_pass, 0)
+
+    def finish(segment, carry):
+        row_total = jnp.sum(total_buf[segment], axis=1, keepdims=True)
+        row_total = jnp.broadcast_to(row_total, total_buf.shape[1:])
         emit(
-            segment, row_max, row_total, acc, heads, full, stat_full, own_ref, own_stat_ref, sends
+            segment, max_buf[segment], row_total, acc.at[segment], heads, full, stat_full,
+            own_ref, own_stat_ref, sends,
         )
         return carry
 
-    lax.fori_loop(0, segs, one_segment, 0)
+    lax.fori_loop(0, segs, finish, 0)
 
 
 def combine_kernel(own_ref, stat_ref, *rest):
     received, out_ref = rest[:-1], rest[-1]
     width = own_ref.shape[1]
-    heads = width // HD
     lane = lax.broadcasted_iota(jnp.int32, (STATS, width), 0)
     head = lax.broadcasted_iota(jnp.int32, (STATS, width), 1) // HD
-    pick_max = ((lane // 3) == head).astype(F32).astype(BF16)
-    pick_total = ((lane // 3) == head + heads).astype(F32).astype(BF16)
+    pick = ((lane // 3) == head).astype(F32).astype(BF16)
     parts = [(own_ref[...], stat_ref[...])]
     for ref in received:
         parts.append((ref[:, :width].astype(F32), ref[:, width:]))
-    maxima = [mm(stat, pick_max) for _, stat in parts]
-    totals = [mm(stat, pick_total) for _, stat in parts]
-    joint = functools.reduce(jnp.maximum, maxima)
-    factors = [jnp.exp(value - joint) for value in maxima]
-    total = sum(value * factor for value, factor in zip(totals, factors))
+    levels = [mm(stat, pick) for _, stat in parts]
+    joint = functools.reduce(jnp.maximum, levels)
+    factors = [jnp.exp(level - joint) for level in levels]
     mixed = sum(part[0] * factor for part, factor in zip(parts, factors))
-    out_ref[...] = (mixed / total).astype(BF16)
+    out_ref[...] = (mixed / sum(factors)).astype(BF16)
 
 
 def hidden_kernel(
@@ -324,6 +382,8 @@
         row_max, row_total = attend(
             chunks, chunk_scores, value_of, (score_buf, max_buf, total_buf, acc)
         )
+        wide = (heads * full.shape[0], 128)
+        row_max, row_total = jnp.broadcast_to(row_max, wide), jnp.broadcast_to(row_total, wide)
         emit(
             segment, row_max, row_total, acc, heads, full, stat_full, own_ref, own_stat_ref, sends
         )
@@ -422,6 +482,8 @@
         pltpu.VMEM((lat_rows, STATS), F32),
     ]
     most = reads * length
+    tiles = -(-most // CHUNK)
+    spare = (segs * tiles + 1) // 2 * 2 + 2
     produced = call(
         functools.partial(cross_kernel, readers),
         (band_start, coverage, present, latents, read_tokens, cross_query, cross_key, cross_value),
@@ -431,17 +493,23 @@
             pltpu.SMEM(band_start.shape, jnp.int32),
             pltpu.SMEM(coverage.shape, jnp.int32),
             pltpu.SMEM(present.shape, jnp.int32),
+            pltpu.SMEM((segs * tiles + 3,), jnp.int32),
+            pltpu.SMEM((segs + 1, reads + 1), jnp.int32),
+            pltpu.SMEM((segs + 1, reads), jnp.int32),
             pltpu.VMEM(latents.shape, BF16),
             pltpu.VMEM(cross_query.shape, BF16),
             pltpu.VMEM(cross_key.shape, BF16),
             pltpu.VMEM(cross_value.shape, BF16),
-            pltpu.VMEM((segs, most, width), BF16),
-            pltpu.VMEM((segs, lat_rows, local), BF16),
-            pltpu.VMEM((spread_rows, local), BF16),
-            pltpu.VMEM((most // CHUNK, spread_rows, CHUNK), F32),
-            pltpu.VMEM((most, local), BF16),
+            pltpu.VMEM((spare * CHUNK, width), BF16),
+            pltpu.VMEM((segs + 1, spread_rows, local), BF16),
+            pltpu.VMEM((2, 2 * CHUNK, local), BF16),
+            pltpu.VMEM((segs * tiles + 1, spread_rows, CHUNK), F32),
+            pltpu.VMEM((spare * CHUNK, local), BF16),
+            pltpu.VMEM((segs + 1, spread_rows, 128), F32),
+            pltpu.VMEM((segs + 1, spread_rows, 128), F32),
+            pltpu.VMEM((segs + 1, spread_rows, local), F32),
         ]
-        + work
+        + work[3:]
         + [pltpu.SemaphoreType.DMA((7,)), pltpu.SemaphoreType.DMA((segs,))],
         estimate=cost(
             2 * segs * most * local * (2 * width + 2 * spread_rows),

time: 69.5 us -> 64.8 us (0.932)
  Pallas kernels: 22.4 us -> 19.6 us
  starting transfers between devices: 22.8 us -> 20.8 us
    pallas_call x6, Pallas kernels: 22.4 us -> 19.6 us  [call(): pl.pallas_call(kernel, out_shape=[jax.ShapeDtypeStruct(shape, kind) for s...]
    ppermute x3, starting transfers between devices: 10.2 us -> 8.25 us  [to_reader(): lax.ppermute(value, 'read', [(i, (i + step) % readers) for i in range(rea...]
where the time goes in v3:
time: 64.8 us; the launch traced here: 64.3 us
  waiting for transfers between devices  21.9 us (34%)
  starting transfers between devices  20.8 us (32%)
  Pallas kernels  19.6 us (30%)
  local copies, waits for them, and re-layouts  1.82 us (3%)
    pallas_call x6, Pallas kernels, call(): pl.pallas_call(kernel, out_shape=[jax.ShapeDtypeStruct(shape, kind) for s...  19.6 us
    ppermute x3, waiting for transfers between devices, to_reader(): lax.ppermute(value, 'read', [(i, (i + step) % readers) for i in range(rea...  10.4 us
    ppermute x2, waiting for transfers between devices, both_ways(): return lax.ppermute(value, ('pos', 'head'), moves)  9.5 us
    ppermute x6, starting transfers between devices, swap_cores(): return lax.ppermute(value, 'head', [(0, 1), (1, 0)])  8.58 us
    ppermute x3, starting transfers between devices, to_reader(): lax.ppermute(value, 'read', [(i, (i + step) % readers) for i in range(rea...  8.25 us
    ppermute x2, starting transfers between devices, both_ways(): return lax.ppermute(value, ('pos', 'head'), moves)  4.01 us
    ppermute x6, waiting for transfers between devices, swap_cores(): return lax.ppermute(value, 'head', [(0, 1), (1, 0)])  1.98 us
    unnamed x18, local copies, waits for them, and re-layouts  1.82 us
  transfers between devices with their start and end apart: 11, of which 7 were waited for; matrix products, arithmetic and copies ran while one was open for 0% of the time, Pallas kernels for 1%

profile of v3, /device:TPU:9, one launch (start us, length us, event | category | flops | bytes accessed | tf_op | source)
XLA Modules:
  0.0 64.3 jit_solution(4794263458277339046)
XLA Ops:
  0.0 10.6 %cross.1 = (f32[4,64,256]{2,1,0:T(8,128)}, bf16[4,64,128]{2,1,0:T(8,128)(2,1)}, bf16[4,64,384]{2,1,0:T(8,128)(2,1)}) custom-call(s32[4,4]{1,0:T(4,128)} %start_hbm.1, s32[4,4]{1,0:T(4,128)} %cov_hbm.1, s32[4,4]{1,0:T(4,128)} %present_hbm.1, bf16[4,128,512]{2,1,0:T(8,128)(2,1)} %lat_ref.1, bf16[4,4,512,512]{3,2,1,0:T(8,128)(2,1)} %tok_ref.1, ...), custom_call_target="tpu_custom_call" | custom-call | flops 8589934592 | bytes 8388608 | tf_op jit(solution)/shard_map/cross/pallas_call | solution.py:415
  10.7 5.2 %collective-permute-start = (bf16[4,64,384]{2,1,0:T(8,128)(2,1)}, bf16[4,64,384]{2,1,0:T(8,128)(2,1)S(1)}, u32[]{:S(2)}, u32[]{:S(2)}) collective-permute-start(bf16[4,64,384]{2,1,0:T(8,128)(2,1)} %get-tuple-element.16), channel_id=1, source_target_pairs={{0,2},{2,0},{1,3},{3,1},{4,6},{6,4},{5,7},{7,5},{8,10},{10,8},{9,1... | collective-permute-start | bytes 589832 | tf_op jit(solution)/shard_map/ppermute | solution.py:433
  15.9 1.0 %collective-permute-start.2 = (bf16[256,512]{1,0:T(8,128)(2,1)S(1)}, bf16[256,512]{1,0:T(8,128)(2,1)S(1)}, u32[]{:S(2)}, u32[]{:S(2)}) collective-permute-start(bf16[256,512]{1,0:T(8,128)(2,1)S(1)} %copy-done.2), channel_id=1, source_target_pairs={{0,1},{1,0},{2,3},{3,2},{4,5},{5,4},{6,7},{7,6},{8,9},{9,8},{10,11... | collective-permute-start | bytes 786440 | tf_op jit(solution)/shard_map/ppermute | solution.py:428
  16.9 3.9 %collective-permute-done = bf16[4,64,384]{2,1,0:T(8,128)(2,1)S(1)} collective-permute-done((bf16[4,64,384]{2,1,0:T(8,128)(2,1)}, bf16[4,64,384]{2,1,0:T(8,128)(2,1)S(1)}, u32[]{:S(2)}, u32[]{:S(2)}) %collective-permute-start) | collective-permute-done | bytes 196640 | tf_op jit(solution)/shard_map/ppermute | solution.py:433
  20.8 0.9 %copy-done.1 = f32[4,64,256]{2,1,0:T(8,128)S(1)} copy-done((f32[4,64,256]{2,1,0:T(8,128)S(1)}, f32[4,64,256]{2,1,0:T(8,128)}, u32[]{:S(2)}) %copy-start.1) | copy-done | bytes 262168
  21.7 0.8 %copy-done.5 = bf16[4,64,128]{2,1,0:T(8,128)(2,1)S(1)} copy-done((bf16[4,64,128]{2,1,0:T(8,128)(2,1)S(1)}, bf16[4,64,128]{2,1,0:T(8,128)(2,1)}, u32[]{:S(2)}) %copy-start.5) | copy-done | bytes 65560
  22.8 1.3 %collective-permute-start.1 = (bf16[256,256]{1,0:T(8,128)(2,1)S(1)}, bf16[256,256]{1,0:T(8,128)(2,1)S(1)}, u32[]{:S(2)}, u32[]{:S(2)}) collective-permute-start(bf16[256,256]{1,0:T(8,128)(2,1)S(1)} %join_reads.1.own_ref), channel_id=1, source_target_pairs={{0,1},{1,0},{2,3},{3,2},{4,5},{5,4},{6,7},{7,6},{8,9},{9,8},{10,11... | collective-permute-start | bytes 393224 | tf_op jit(solution)/shard_map/ppermute | solution.py:428
  24.1 1.0 %collective-permute-done.1.other_ref = bf16[256,256]{1,0:T(8,128)(2,1)S(1)} collective-permute-done((bf16[256,256]{1,0:T(8,128)(2,1)S(1)}, bf16[256,256]{1,0:T(8,128)(2,1)S(1)}, u32[]{:S(2)}, u32[]{:S(2)}) %collective-permute-start.1) | collective-permute-done | bytes 131104 | tf_op jit(solution)/shard_map/ppermute | solution.py:428
  25.1 0.6 %hidden.1 = (f32[256,512]{1,0:T(8,128)S(1)}, bf16[256,512]{1,0:T(8,128)(2,1)S(1)}, bf16[256,256]{1,0:T(8,128)(2,1)S(1)}) custom-call(bf16[4,128,512]{2,1,0:T(8,128)(2,1)S(1)} %copy-done, bf16[256,256]{1,0:T(8,128)(2,1)S(1)} %join_reads.1.own_ref, bf16[256,256]{1,0:T(8,128)(2,1)S(1)} %collective-permute-done.1.other_ref, bf16[256,512]{1,0:T(8,128)(2,1)S(1)} %copy-done.2, ...), custom_call_target="tpu_custom_call" | custom-call | flops 201326592 | bytes 1048576 | tf_op jit(solution)/shard_map/hidden/pallas_call | solution.py:415
  25.8 2.1 %collective-permute-start.4 = (bf16[256,512]{1,0:T(8,128)(2,1)S(1)}, bf16[256,512]{1,0:T(8,128)(2,1)S(1)}, u32[]{:S(2)}, u32[]{:S(2)}) collective-permute-start(bf16[256,512]{1,0:T(8,128)(2,1)S(1)} %get-tuple-element.19.rest_2_), channel_id=1, source_target_pairs={{0,4},{4,8},{5,1},{8,12},{9,5},{13,9},{2,6},{6,10},{7,3},{10,14},{... | collective-permute-start | bytes 786440 | tf_op jit(solution)/shard_map/ppermute | solution.py:444
  27.9 5.3 %collective-permute-done.4.rest_3_ = bf16[256,512]{1,0:T(8,128)(2,1)S(1)} collective-permute-done((bf16[256,512]{1,0:T(8,128)(2,1)S(1)}, bf16[256,512]{1,0:T(8,128)(2,1)S(1)}, u32[]{:S(2)}, u32[]{:S(2)}) %collective-permute-start.4) | collective-permute-done | bytes 262176 | tf_op jit(solution)/shard_map/ppermute | solution.py:444
  33.2 1.9 %collective-permute-start.6 = (bf16[256,512]{1,0:T(8,128)(2,1)S(1)}, bf16[256,512]{1,0:T(8,128)(2,1)S(1)}, u32[]{:S(2)}, u32[]{:S(2)}) collective-permute-start(bf16[256,512]{1,0:T(8,128)(2,1)S(1)} %collective-permute-done.4.rest_3_), channel_id=1, source_target_pairs={{0,4},{4,8},{5,1},{8,12},{9,5},{13,9},{2,6},{6,10},{7,3},{10,14},{... | collective-permute-start | bytes 786440 | tf_op jit(solution)/shard_map/ppermute | solution.py:444
  35.1 1.3 %collective-permute-start.5 = (bf16[256,512]{1,0:T(8,128)(2,1)S(1)}, bf16[256,512]{1,0:T(8,128)(2,1)S(1)}, u32[]{:S(2)}, u32[]{:S(2)}) collective-permute-start(bf16[256,512]{1,0:T(8,128)(2,1)S(1)} %collective-permute-done.4.rest_3_), channel_id=1, source_target_pairs={{0,1},{1,0},{2,3},{3,2},{4,5},{5,4},{6,7},{7,6},{8,9},{9,8},{10,11... | collective-permute-start | bytes 786440 | tf_op jit(solution)/shard_map/ppermute | solution.py:428
  36.4 4.2 %collective-permute-done.6.rest_5_ = bf16[256,512]{1,0:T(8,128)(2,1)S(1)} collective-permute-done((bf16[256,512]{1,0:T(8,128)(2,1)S(1)}, bf16[256,512]{1,0:T(8,128)(2,1)S(1)}, u32[]{:S(2)}, u32[]{:S(2)}) %collective-permute-start.6) | collective-permute-done | bytes 262176 | tf_op jit(solution)/shard_map/ppermute | solution.py:444
  40.6 2.1 %collective-permute-start.7 = (bf16[256,512]{1,0:T(8,128)(2,1)S(1)}, bf16[256,512]{1,0:T(8,128)(2,1)S(1)}, u32[]{:S(2)}, u32[]{:S(2)}) collective-permute-start(bf16[256,512]{1,0:T(8,128)(2,1)S(1)} %collective-permute-done.6.rest_5_), channel_id=1, source_target_pairs={{0,1},{1,0},{2,3},{3,2},{4,5},{5,4},{6,7},{7,6},{8,9},{9,8},{10,11... | collective-permute-start | bytes 786440 | tf_op jit(solution)/shard_map/ppermute | solution.py:428
  42.7 1.5 %collective-permute-start.3 = (bf16[256,256]{1,0:T(8,128)(2,1)S(1)}, bf16[256,256]{1,0:T(8,128)(2,1)S(1)}, u32[]{:S(2)}, u32[]{:S(2)}) collective-permute-start(bf16[256,256]{1,0:T(8,128)(2,1)S(1)} %get-tuple-element.18.rest_0_), channel_id=1, source_target_pairs={{0,2},{2,0},{1,3},{3,1},{4,6},{6,4},{5,7},{7,5},{8,10},{10,8},{9,1... | collective-permute-start | bytes 393224 | tf_op jit(solution)/shard_map/ppermute | solution.py:433
  44.1 3.6 %collective-permute-done.3.rest_1_ = bf16[256,256]{1,0:T(8,128)(2,1)S(1)} collective-permute-done((bf16[256,256]{1,0:T(8,128)(2,1)S(1)}, bf16[256,256]{1,0:T(8,128)(2,1)S(1)}, u32[]{:S(2)}, u32[]{:S(2)}) %collective-permute-start.3) | collective-permute-done | bytes 131104 | tf_op jit(solution)/shard_map/ppermute | solution.py:433
  47.8 6.9 %within.1 = (f32[4,64,256]{2,1,0:T(8,128)S(1)}, bf16[4,64,128]{2,1,0:T(8,128)(2,1)S(1)}, bf16[4,64,384]{2,1,0:T(8,128)(2,1)S(1)}) custom-call(s32[4,16]{1,0:T(4,128)S(1)} %copy-done.8, bf16[512,256]{1,0:T(8,128)(2,1)S(1)} %copy-done.6, bf16[512,256]{1,0:T(8,128)(2,1)S(1)} %copy-done.7, bf16[256,256]{1,0:T(8,128)(2,1)S(1)} %get-tuple-element.18.rest_0_, ...), custom_call_target="tpu_custom_call" | custom-call | flops 1610612736 | bytes 2621440 | tf_op jit(solution)/shard_map/within/pallas_call | solution.py:415
  54.6 1.5 %collective-permute-start.8 = (bf16[4,64,384]{2,1,0:T(8,128)(2,1)S(1)}, bf16[4,64,384]{2,1,0:T(8,128)(2,1)S(1)}, u32[]{:S(2)}, u32[]{:S(2)}) collective-permute-start(bf16[4,64,384]{2,1,0:T(8,128)(2,1)S(1)} %get-tuple-element.22), channel_id=1, source_target_pairs={{0,2},{2,0},{1,3},{3,1},{4,6},{6,4},{5,7},{7,5},{8,10},{10,8},{9,1... | collective-permute-start | bytes 589832 | tf_op jit(solution)/shard_map/ppermute | solution.py:433
  56.2 1.2 %collective-permute-start.10 = (bf16[256,512]{1,0:T(8,128)(2,1)S(1)}, bf16[256,512]{1,0:T(8,128)(2,1)S(1)}, u32[]{:S(2)}, u32[]{:S(2)}) collective-permute-start(bf16[256,512]{1,0:T(8,128)(2,1)S(1)} %copy-done.4), channel_id=1, source_target_pairs={{0,1},{1,0},{2,3},{3,2},{4,5},{5,4},{6,7},{7,6},{8,9},{9,8},{10,11... | collective-permute-start | bytes 786440 | tf_op jit(solution)/shard_map/ppermute | solution.py:428
  57.4 3.0 %collective-permute-done.8 = bf16[4,64,384]{2,1,0:T(8,128)(2,1)S(1)} collective-permute-done((bf16[4,64,384]{2,1,0:T(8,128)(2,1)S(1)}, bf16[4,64,384]{2,1,0:T(8,128)(2,1)S(1)}, u32[]{:S(2)}, u32[]{:S(2)}) %collective-permute-start.8) | collective-permute-done | bytes 196640 | tf_op jit(solution)/shard_map/ppermute | solution.py:433
  60.6 1.8 %collective-permute-start.9 = (bf16[256,256]{1,0:T(8,128)(2,1)S(1)}, bf16[256,256]{1,0:T(8,128)(2,1)S(1)}, u32[]{:S(2)}, u32[]{:S(2)}) collective-permute-start(bf16[256,256]{1,0:T(8,128)(2,1)S(1)} %join_keys.1.own_ref), channel_id=1, source_target_pairs={{0,1},{1,0},{2,3},{3,2},{4,5},{5,4},{6,7},{7,6},{8,9},{9,8},{10,11... | collective-permute-start | bytes 393224 | tf_op jit(solution)/shard_map/ppermute | solution.py:428
  62.4 1.0 %collective-permute-done.9.other_ref = bf16[256,256]{1,0:T(8,128)(2,1)S(1)} collective-permute-done((bf16[256,256]{1,0:T(8,128)(2,1)S(1)}, bf16[256,256]{1,0:T(8,128)(2,1)S(1)}, u32[]{:S(2)}, u32[]{:S(2)}) %collective-permute-start.9) | collective-permute-done | bytes 131104 | tf_op jit(solution)/shard_map/ppermute | solution.py:428
  63.4 0.9 %out.1 = bf16[4,64,256]{2,1,0:T(8,128)(2,1)} custom-call(f32[256,512]{1,0:T(8,128)S(1)} %get-tuple-element.17.hid_ref, bf16[256,256]{1,0:T(8,128)(2,1)S(1)} %join_keys.1.own_ref, bf16[256,256]{1,0:T(8,128)(2,1)S(1)} %collective-permute-done.9.other_ref, bf16[256,512]{1,0:T(8,128)(2,1)S(1)} %copy-done.4, bf16[256,512]{1,0:T(8,128)(2,1)S(1)} %collective-permute-done.10.wp_ref), custom_call_target="tpu_custom_call" | custom-call | flops 67108864 | bytes 1048576 | tf_op jit(solution)/shard_map/out/pallas_call | solution.py:415
  (22 shorter events, 0.6 us)
Async XLA Ops:
  0.0 25.1 %copy-start = (bf16[4,128,512]{2,1,0:T(8,128)(2,1)S(1)}, bf16[4,128,512]{2,1,0:T(8,128)(2,1)}, u32[]{:S(2)}) copy-start(bf16[4,128,512]{2,1,0:T(8,128)(2,1)} %lat_ref.1) | copy-start | bytes 1572868
  0.0 15.9 %copy-start.2 = (bf16[256,512]{1,0:T(8,128)(2,1)S(1)}, bf16[256,512]{1,0:T(8,128)(2,1)}, u32[]{:S(2)}) copy-start(bf16[256,512]{1,0:T(8,128)(2,1)} %wo_ref.2) | copy-start | bytes 786436
  0.0 25.1 %copy-start.3 = (bf16[512,256]{1,0:T(8,128)(2,1)S(1)}, bf16[512,256]{1,0:T(8,128)(2,1)}, u32[]{:S(2)}) copy-start(bf16[512,256]{1,0:T(8,128)(2,1)} %wq_ref.1) | copy-start | bytes 786436
  0.0 47.7 %copy-start.8 = (s32[4,16]{1,0:T(4,128)S(1)}, s32[4,16]{1,0:T(4,128)}, u32[]{:S(2)}) copy-start(s32[4,16]{1,0:T(4,128)} %pattern_ref.1) | copy-start | bytes 772
  0.0 47.7 %copy-start.6 = (bf16[512,256]{1,0:T(8,128)(2,1)S(1)}, bf16[512,256]{1,0:T(8,128)(2,1)}, u32[]{:S(2)}) copy-start(bf16[512,256]{1,0:T(8,128)(2,1)} %wk_ref.1) | copy-start | bytes 786436
  0.0 47.7 %copy-start.7 = (bf16[512,256]{1,0:T(8,128)(2,1)S(1)}, bf16[512,256]{1,0:T(8,128)(2,1)}, u32[]{:S(2)}) copy-start(bf16[512,256]{1,0:T(8,128)(2,1)} %wv_ref.1) | copy-start | bytes 786436
  0.0 56.1 %copy-start.4 = (bf16[256,512]{1,0:T(8,128)(2,1)S(1)}, bf16[256,512]{1,0:T(8,128)(2,1)}, u32[]{:S(2)}) copy-start(bf16[256,512]{1,0:T(8,128)(2,1)} %wo_ref.3) | copy-start | bytes 786436
  10.7 10.1 %collective-permute-start = (bf16[4,64,384]{2,1,0:T(8,128)(2,1)}, bf16[4,64,384]{2,1,0:T(8,128)(2,1)S(1)}, u32[]{:S(2)}, u32[]{:S(2)}) collective-permute-start(bf16[4,64,384]{2,1,0:T(8,128)(2,1)} %get-tuple-element.16), channel_id=1, source_target_pairs={{0,2},{2,0},{1,3},{3,1},{4,6},{6,4},{5,7},{7,5},{8,10},{10,8},{9,1... | collective-permute-start | bytes 589832 | tf_op jit(solution)/shard_map/ppermute | solution.py:433
  15.9 8.2 %collective-permute-start.2 = (bf16[256,512]{1,0:T(8,128)(2,1)S(1)}, bf16[256,512]{1,0:T(8,128)(2,1)S(1)}, u32[]{:S(2)}, u32[]{:S(2)}) collective-permute-start(bf16[256,512]{1,0:T(8,128)(2,1)S(1)} %copy-done.2), channel_id=1, source_target_pairs={{0,1},{1,0},{2,3},{3,2},{4,5},{5,4},{6,7},{7,6},{8,9},{9,8},{10,11... | collective-permute-start | bytes 786440 | tf_op jit(solution)/shard_map/ppermute | solution.py:428
  20.8 1.0 %copy-start.1 = (f32[4,64,256]{2,1,0:T(8,128)S(1)}, f32[4,64,256]{2,1,0:T(8,128)}, u32[]{:S(2)}) copy-start(f32[4,64,256]{2,1,0:T(8,128)} %get-tuple-element.14) | copy-start | bytes 786436
  21.7 0.8 %copy-start.5 = (bf16[4,64,128]{2,1,0:T(8,128)(2,1)S(1)}, bf16[4,64,128]{2,1,0:T(8,128)(2,1)}, u32[]{:S(2)}) copy-start(bf16[4,64,128]{2,1,0:T(8,128)(2,1)} %get-tuple-element.15) | copy-start | bytes 196612
  22.8 2.3 %collective-permute-start.1 = (bf16[256,256]{1,0:T(8,128)(2,1)S(1)}, bf16[256,256]{1,0:T(8,128)(2,1)S(1)}, u32[]{:S(2)}, u32[]{:S(2)}) collective-permute-start(bf16[256,256]{1,0:T(8,128)(2,1)S(1)} %join_reads.1.own_ref), channel_id=1, source_target_pairs={{0,1},{1,0},{2,3},{3,2},{4,5},{5,4},{6,7},{7,6},{8,9},{9,8},{10,11... | collective-permute-start | bytes 393224 | tf_op jit(solution)/shard_map/ppermute | solution.py:428
  25.8 7.4 %collective-permute-start.4 = (bf16[256,512]{1,0:T(8,128)(2,1)S(1)}, bf16[256,512]{1,0:T(8,128)(2,1)S(1)}, u32[]{:S(2)}, u32[]{:S(2)}) collective-permute-start(bf16[256,512]{1,0:T(8,128)(2,1)S(1)} %get-tuple-element.19.rest_2_), channel_id=1, source_target_pairs={{0,4},{4,8},{5,1},{8,12},{9,5},{13,9},{2,6},{6,10},{7,3},{10,14},{... | collective-permute-start | bytes 786440 | tf_op jit(solution)/shard_map/ppermute | solution.py:444
  33.2 7.4 %collective-permute-start.6 = (bf16[256,512]{1,0:T(8,128)(2,1)S(1)}, bf16[256,512]{1,0:T(8,128)(2,1)S(1)}, u32[]{:S(2)}, u32[]{:S(2)}) collective-permute-start(bf16[256,512]{1,0:T(8,128)(2,1)S(1)} %collective-permute-done.4.rest_3_), channel_id=1, source_target_pairs={{0,4},{4,8},{5,1},{8,12},{9,5},{13,9},{2,6},{6,10},{7,3},{10,14},{... | collective-permute-start | bytes 786440 | tf_op jit(solution)/shard_map/ppermute | solution.py:444
  35.1 12.6 %collective-permute-start.5 = (bf16[256,512]{1,0:T(8,128)(2,1)S(1)}, bf16[256,512]{1,0:T(8,128)(2,1)S(1)}, u32[]{:S(2)}, u32[]{:S(2)}) collective-permute-start(bf16[256,512]{1,0:T(8,128)(2,1)S(1)} %collective-permute-done.4.rest_3_), channel_id=1, source_target_pairs={{0,1},{1,0},{2,3},{3,2},{4,5},{5,4},{6,7},{7,6},{8,9},{9,8},{10,11... | collective-permute-start | bytes 786440 | tf_op jit(solution)/shard_map/ppermute | solution.py:428
  40.6 7.1 %collective-permute-start.7 = (bf16[256,512]{1,0:T(8,128)(2,1)S(1)}, bf16[256,512]{1,0:T(8,128)(2,1)S(1)}, u32[]{:S(2)}, u32[]{:S(2)}) collective-permute-start(bf16[256,512]{1,0:T(8,128)(2,1)S(1)} %collective-permute-done.6.rest_5_), channel_id=1, source_target_pairs={{0,1},{1,0},{2,3},{3,2},{4,5},{5,4},{6,7},{7,6},{8,9},{9,8},{10,11... | collective-permute-start | bytes 786440 | tf_op jit(solution)/shard_map/ppermute | solution.py:428
  42.7 5.1 %collective-permute-start.3 = (bf16[256,256]{1,0:T(8,128)(2,1)S(1)}, bf16[256,256]{1,0:T(8,128)(2,1)S(1)}, u32[]{:S(2)}, u32[]{:S(2)}) collective-permute-start(bf16[256,256]{1,0:T(8,128)(2,1)S(1)} %get-tuple-element.18.rest_0_), channel_id=1, source_target_pairs={{0,2},{2,0},{1,3},{3,1},{4,6},{6,4},{5,7},{7,5},{8,10},{10,8},{9,1... | collective-permute-start | bytes 393224 | tf_op jit(solution)/shard_map/ppermute | solution.py:433
  54.6 5.7 %collective-permute-start.8 = (bf16[4,64,384]{2,1,0:T(8,128)(2,1)S(1)}, bf16[4,64,384]{2,1,0:T(8,128)(2,1)S(1)}, u32[]{:S(2)}, u32[]{:S(2)}) collective-permute-start(bf16[4,64,384]{2,1,0:T(8,128)(2,1)S(1)} %get-tuple-element.22), channel_id=1, source_target_pairs={{0,2},{2,0},{1,3},{3,1},{4,6},{6,4},{5,7},{7,5},{8,10},{10,8},{9,1... | collective-permute-start | bytes 589832 | tf_op jit(solution)/shard_map/ppermute | solution.py:433
  56.2 6.2 %collective-permute-start.10 = (bf16[256,512]{1,0:T(8,128)(2,1)S(1)}, bf16[256,512]{1,0:T(8,128)(2,1)S(1)}, u32[]{:S(2)}, u32[]{:S(2)}) collective-permute-start(bf16[256,512]{1,0:T(8,128)(2,1)S(1)} %copy-done.4), channel_id=1, source_target_pairs={{0,1},{1,0},{2,3},{3,2},{4,5},{5,4},{6,7},{7,6},{8,9},{9,8},{10,11... | collective-permute-start | bytes 786440 | tf_op jit(solution)/shard_map/ppermute | solution.py:428
  60.6 2.8 %collective-permute-start.9 = (bf16[256,256]{1,0:T(8,128)(2,1)S(1)}, bf16[256,256]{1,0:T(8,128)(2,1)S(1)}, u32[]{:S(2)}, u32[]{:S(2)}) collective-permute-start(bf16[256,256]{1,0:T(8,128)(2,1)S(1)} %join_keys.1.own_ref), channel_id=1, source_target_pairs={{0,1},{1,0},{2,3},{3,2},{4,5},{5,4},{6,7},{7,6},{8,9},{9,8},{10,11... | collective-permute-start | bytes 393224 | tf_op jit(solution)/shard_map/ppermute | solution.py:428

commit v4 on v3

--- a/solution.py
+++ b/solution.py
@@ -6,6 +6,7 @@
 from jax.experimental import pallas as pl
 from jax.experimental.pallas import tpu as pltpu
 from jax.sharding import PartitionSpec as P
+
 
 HD = 64
 EPSILON = 1e-06
@@ -31,11 +32,15 @@
 
 def spread_queries(query, heads, target):
     rows, width = query.shape
-    column_head = lax.broadcasted_iota(jnp.int32, (rows, width), 1) // HD
+    lane = lax.broadcasted_iota(jnp.int32, (rows, 128), 1)
     for head in range(heads):
-        target[head * rows : (head + 1) * rows, :] = jnp.where(
-            column_head == head, query.astype(F32), 0.0
-        ).astype(BF16)
+        inside = (lane >= HD) if head % 2 else (lane < HD)
+        for tile in range(width // 128):
+            cols = slice(tile * 128, (tile + 1) * 128)
+            kept = jnp.zeros((rows, 128), BF16)
+            if tile == head // 2:
+                kept = jnp.where(inside, query[:, cols].astype(F32), 0.0).astype(BF16)
+            target[head * rows : (head + 1) * rows, cols] = kept
 
 
 def tile_fold(values, combine):
@@ -45,39 +50,25 @@
     return folded
 
 
-def attend(chunks, chunk_scores, value_of, scratch):
-    score_buf, max_buf, total_buf, acc = scratch
-    max_buf[...] = jnp.full(max_buf.shape, NEG, F32)
-    total_buf[...] = jnp.zeros(total_buf.shape, F32)
-    acc[...] = jnp.zeros(acc.shape, F32)
-
-    def first(chunk, carry):
-        scores = chunk_scores(chunk)
-        score_buf[chunk] = scores
-        max_buf[...] = jnp.maximum(max_buf[...], tile_fold(scores, jnp.maximum))
-        return carry
-
-    lax.fori_loop(0, chunks, first, 0)
-    row_max = jnp.max(max_buf[...], axis=1, keepdims=True)
-
-    def second(chunk, carry):
-        weights = jnp.exp(score_buf[chunk] - row_max)
-        total_buf[...] += tile_fold(weights, jnp.add)
-        acc[...] += mm(weights.astype(BF16), value_of(chunk))
-        return carry
-
-    lax.fori_loop(0, chunks, second, 0)
-    return row_max, jnp.sum(total_buf[...], axis=1, keepdims=True)
-
-
 def emit(segment, row_max, row_total, acc, heads, full, stat_full, own_ref, own_stat_ref, sends):
     readers = len(sends) + 1
     rows, width = full.shape
     part = rows // readers
     lane = lax.broadcasted_iota(jnp.int32, (rows, 128), 1)
-    filled = row_total > 0
-    divisor = jnp.where(filled, row_total, 1.0)
-    level = jnp.where(filled, row_max + jnp.log(divisor), NEG)
+    group = STATS // heads
+
+    def compact(values):
+        packed = values[:rows]
+        for head in range(1, heads):
+            packed = jnp.where(lane < head * group, packed, values[head * rows : (head + 1) * rows])
+        return packed
+
+    divisor = jnp.where(row_total > 0, row_total, 1.0)
+    packed_total = compact(row_total)
+    level = jnp.where(
+        packed_total > 0, compact(row_max) + jnp.log(jnp.where(packed_total > 0, packed_total, 1.0)),
+        NEG,
+    )
     for tile in range(width // 128):
         low = slice(2 * tile * rows, (2 * tile + 1) * rows)
         high = slice((2 * tile + 1) * rows, (2 * tile + 2) * rows)
@@ -86,12 +77,10 @@
             lane < HD, divisor[low], divisor[high]
         )
     stats = jnp.zeros((rows, STATS), F32)
-    for head in range(heads):
-        left = level[head * rows : (head + 1) * rows]
-        for step in range(3):
-            piece = left.astype(BF16).astype(F32)
-            stats = jnp.where(lane == 3 * head + step, piece, stats)
-            left = left - piece
+    for step in range(3):
+        piece = level.astype(BF16).astype(F32)
+        stats = jnp.where(lax.rem(lane, group) == step, piece, stats)
+        level = level - piece
     stat_full[...] = stats
     reader = lax.axis_index("read")
     for step in range(readers):
@@ -185,10 +174,12 @@
     acc[...] = jnp.zeros(acc.shape, F32)
     for load in loads[3:]:
         load.wait()
+    normed = rms_rows(lat_ref[...].reshape(segs * lat_rows, width).astype(F32)).astype(BF16)
+    query = (mm(normed, wq_ref[...]) * (HD ** (-0.5))).astype(BF16)
     for segment in range(segs):
-        normed = rms_rows(lat_ref[segment].astype(F32)).astype(BF16)
-        query = (mm(normed, wq_ref[...]) * (HD ** (-0.5))).astype(BF16)
-        spread_queries(query, heads, spread.at[segment])
+        spread_queries(
+            query[segment * lat_rows : (segment + 1) * lat_rows], heads, spread.at[segment]
+        )
 
     def landed(segment):
         size = pl.multiple_of(low_of[segment, reads], ROWS)
@@ -277,26 +268,34 @@
     lax.fori_loop(0, segs, finish, 0)
 
 
-def combine_kernel(own_ref, stat_ref, *rest):
+def row_levels(stats, width):
+    group = STATS // (width // HD)
+    lane = lax.broadcasted_iota(jnp.int32, (STATS, width), 0)
+    head = lax.broadcasted_iota(jnp.int32, (STATS, width), 1) // HD
+    pick = ((lane // group == head) & (lax.rem(lane, group) < 3)).astype(F32).astype(BF16)
+    return mm(stats, pick)
+
+
+def own_kernel(own_ref, stat_ref, kept_ref, level_ref):
+    kept_ref[...] = own_ref[...]
+    level_ref[...] = row_levels(stat_ref[...], own_ref.shape[1])
+
+
+def combine_kernel(own_ref, level_ref, *rest):
     received, out_ref = rest[:-1], rest[-1]
     width = own_ref.shape[1]
-    lane = lax.broadcasted_iota(jnp.int32, (STATS, width), 0)
-    head = lax.broadcasted_iota(jnp.int32, (STATS, width), 1) // HD
-    pick = ((lane // 3) == head).astype(F32).astype(BF16)
-    parts = [(own_ref[...], stat_ref[...])]
-    for ref in received:
-        parts.append((ref[:, :width].astype(F32), ref[:, width:]))
-    levels = [mm(stat, pick) for _, stat in parts]
+    parts = [own_ref[...]] + [ref[:, :width].astype(F32) for ref in received]
+    levels = [level_ref[...]] + [row_levels(ref[:, width:], width) for ref in received]
     joint = functools.reduce(jnp.maximum, levels)
     factors = [jnp.exp(level - joint) for level in levels]
-    mixed = sum(part[0] * factor for part, factor in zip(parts, factors))
+    mixed = sum(part * factor for part, factor in zip(parts, factors))
     out_ref[...] = (mixed / sum(factors)).astype(BF16)
 
 
 def hidden_kernel(
     lat_ref, own_ref, other_ref, wo_ref, wp_ref, wq_ref, hid_ref, norm_ref, query_ref
 ):
-    segs, lat_rows, width = lat_ref.shape
+    segs, _, _ = lat_ref.shape
     part = own_ref.shape[0] // segs
     first = pl.multiple_of(lax.axis_index("read") * part, part)
     delta = mm(own_ref[...], wo_ref[...]) + mm(other_ref[...], wp_ref[...])
@@ -308,36 +307,54 @@
     query_ref[...] = (mm(normed, wq_ref[...]) * (HD ** (-0.5))).astype(BF16)
 
 
-def self_kernel(readers, steps, offsets, pattern_ref, wk_ref, wv_ref, *rest):
-    queries = rest[:readers]
-    count = 1 + 2 * len(steps)
-    blocks = rest[readers : readers + count]
-    rest = rest[readers + count :]
-    own_ref, own_stat_ref = rest[:2]
-    sends = rest[2 : 1 + readers]
-    (query_buf, spread, key_all, value_all, key_buf, value_buf, score_buf, max_buf, total_buf, acc,
-     full, stat_full) = rest[1 + readers :]
-    segs = own_ref.shape[0]
-    part = own_ref.shape[1]
-    local = wk_ref.shape[1]
-    heads = local // HD
-    seg_total = pattern_ref.shape[1]
-    reader = lax.axis_index("read")
-    core = lax.axis_index("head")
-    group = lax.axis_index("pos")
-    size = segs * part
-
-    key_buf[...] = jnp.zeros(key_buf.shape, BF16)
-    value_buf[...] = jnp.zeros(value_buf.shape, BF16)
-    for index, block in enumerate(blocks):
-        if index == 0:
-            slot = 0
-        else:
-            pair = (index - 1) // 2
-            slot = 1 + 2 * pair + (core if index % 2 == 1 else 1 - core)
+def project_blocks(blocks, slots, wk_ref, wv_ref, key_all, value_all):
+    for block, slot in zip(blocks, slots):
+        size = block.shape[0]
         place = pl.ds(pl.multiple_of(slot * size, size), size)
         key_all[place, :] = mm(block[...], wk_ref[...]).astype(BF16)
         value_all[place, :] = mm(block[...], wv_ref[...]).astype(BF16)
+
+
+def collect(segment, segs, part, slot_of, offsets, pattern_ref, sources, targets):
+    seg_total = pattern_ref.shape[1]
+    home = lax.axis_index("pos") * segs + segment
+    live = jnp.int32(0)
+    for offset in offsets:
+        block_step, inner = divmod(segment + offset, segs)
+        if block_step not in slot_of:
+            continue
+        inside = (home + offset >= 0) & (home + offset < seg_total)
+        flag = pattern_ref[segment, jnp.clip(home + offset, 0, seg_total - 1)]
+        chosen = inside & (flag > 0)
+        source = (slot_of[block_step] * segs + inner) * part
+
+        @pl.when(chosen)
+        def _(live=live, source=source):
+            place = pl.ds(pl.multiple_of(live * part, part), part)
+            for whole, packed in zip(sources, targets):
+                packed[place, :] = whole[source : source + part, :]
+
+        live = live + chosen.astype(jnp.int32)
+    return live
+
+
+def near_kernel(readers, offsets, pattern_ref, wk_ref, wv_ref, *rest):
+    queries = rest[:readers]
+    own, ahead, behind = rest[readers : readers + 3]
+    spread, max_out, total_out, acc = rest[readers + 3 : readers + 7]
+    query_buf, key_all, value_all, key_buf, value_buf, score_buf = rest[readers + 7 :]
+    segs, spread_rows, local = spread.shape
+    lat_rows = query_buf.shape[1]
+    part = lat_rows // readers
+    heads = local // HD
+    reader = lax.axis_index("read")
+    core = lax.axis_index("head")
+
+    key_buf[...] = jnp.zeros(key_buf.shape, BF16)
+    value_buf[...] = jnp.zeros(value_buf.shape, BF16)
+    project_blocks(
+        (own, ahead, behind), (0, 1 + core, 2 - core), wk_ref, wv_ref, key_all, value_all
+    )
     for step in range(readers):
         first = pl.multiple_of(lax.rem(reader + readers - step, readers) * part, part)
         for segment in range(segs):
@@ -346,46 +363,87 @@
             ]
 
     for segment in range(segs):
-        spread_queries(query_buf[segment], heads, spread)
-        live = jnp.int32(0)
-        for offset in offsets:
-            block_step = (segment + offset) // segs
-            inner = (segment + offset) % segs
-            if block_step == 0:
-                slot = 0
-            else:
-                slot = 1 + 2 * steps.index(abs(block_step)) + (1 if block_step > 0 else 0)
-            target = group * segs + segment + offset
-            inside = (target >= 0) & (target < seg_total)
-            flag = pattern_ref[segment, jnp.clip(target, 0, seg_total - 1)]
-            chosen = inside & (flag > 0)
-            source = (slot * segs + inner) * part
-
-            @pl.when(chosen)
-            def _(live=live, source=source):
-                place = pl.ds(pl.multiple_of(live * part, part), part)
-                key_buf[place, :] = key_all[source : source + part, :]
-                value_buf[place, :] = value_all[source : source + part, :]
-
-            live = live + chosen.astype(jnp.int32)
-
-        def chunk_scores(chunk, live=live):
+        spread_queries(query_buf[segment], heads, spread.at[segment])
+        live = collect(
+            segment, segs, part, {0: 0, -1: 1, 1: 2}, offsets, pattern_ref,
+            (key_all, value_all), (key_buf, value_buf),
+        )
+        max_out[segment] = jnp.full(max_out.shape[1:], NEG, F32)
+        total_out[segment] = jnp.zeros(total_out.shape[1:], F32)
+        acc[segment] = jnp.zeros(acc.shape[1:], F32)
+
+        def first_pass(chunk, carry, segment=segment, live=live):
             base = pl.multiple_of(chunk * CHUNK, CHUNK)
-            keys = key_buf[pl.ds(base, CHUNK), :]
             place = base + lax.broadcasted_iota(jnp.int32, (1, CHUNK), 1)
-            return jnp.where(place < live * part, nt_dot(spread[...], keys), NEG)
-
-        def value_of(chunk):
-            return value_buf[pl.ds(pl.multiple_of(chunk * CHUNK, CHUNK), CHUNK), :]
+            scores = nt_dot(spread[segment], key_buf[pl.ds(base, CHUNK), :])
+            scores = jnp.where(place < live * part, scores, NEG)
+            score_buf[chunk] = scores
+            max_out[segment] = jnp.maximum(max_out[segment], tile_fold(scores, jnp.maximum))
+            return carry
 
         chunks = (live * part + CHUNK - 1) // CHUNK
-        row_max, row_total = attend(
-            chunks, chunk_scores, value_of, (score_buf, max_buf, total_buf, acc)
-        )
-        wide = (heads * full.shape[0], 128)
-        row_max, row_total = jnp.broadcast_to(row_max, wide), jnp.broadcast_to(row_total, wide)
+        lax.fori_loop(0, chunks, first_pass, 0)
+        row_max = jnp.max(max_out[segment], axis=1, keepdims=True)
+        max_out[segment] = jnp.broadcast_to(row_max, max_out.shape[1:])
+
+        def second_pass(chunk, carry, segment=segment):
+            value = value_buf[pl.ds(pl.multiple_of(chunk * CHUNK, CHUNK), CHUNK), :]
+            for block in range(2):
+                rows = slice(block * spread_rows // 2, (block + 1) * spread_rows // 2)
+                weights = jnp.exp(
+                    score_buf[chunk, rows] - jnp.tile(max_out[segment, rows], (1, CHUNK // 128))
+                )
+                total_out[segment, rows] += tile_fold(weights, jnp.add)
+                acc[segment, rows] += mm(weights.astype(BF16), value)
+            return carry
+
+        lax.fori_loop(0, chunks, second_pass, 0)
+
+
+def far_kernel(readers, steps, offsets, pattern_ref, wk_ref, wv_ref, *rest):
+    spread, max_in, total_in, acc_in = rest[:4]
+    blocks = rest[4 : 4 + 2 * len(steps)]
+    rest = rest[4 + 2 * len(steps) :]
+    own_ref, own_stat_ref = rest[:2]
+    sends = rest[2 : 1 + readers]
+    key_all, value_all, key_buf, value_buf, max_buf, total_buf, acc, full, stat_full = rest[
+        1 + readers :
+    ]
+    segs, _, local = spread.shape
+    heads = local // HD
+    part = own_ref.shape[1]
+    core = lax.axis_index("head")
+    many = key_buf.shape[0]
+
+    key_buf[...] = jnp.zeros(key_buf.shape, BF16)
+    value_buf[...] = jnp.zeros(value_buf.shape, BF16)
+    slots, slot_of = [], {}
+    for index, step in enumerate(steps):
+        slots += [2 * index + core, 2 * index + 1 - core]
+        slot_of[-step], slot_of[step] = 2 * index, 2 * index + 1
+    project_blocks(blocks, slots, wk_ref, wv_ref, key_all, value_all)
+
+    for segment in range(segs):
+        live = collect(
+            segment, segs, part, slot_of, offsets, pattern_ref,
+            (key_all, value_all), (key_buf, value_buf),
+        )
+        place = lax.broadcasted_iota(jnp.int32, (1, many), 1)
+        scores = nt_dot(spread[segment], key_buf[...])
+        scores = jnp.where(place < live * part, scores, NEG)
+        before = max_in[segment]
+        top = jnp.max(tile_fold(scores, jnp.maximum), axis=1, keepdims=True)
+        max_buf[...] = jnp.maximum(before, jnp.broadcast_to(top, before.shape))
+        factor = jnp.exp(before - max_buf[...])
+        weights = jnp.exp(scores - jnp.tile(max_buf[...], (1, many // 128)))
+        total_buf[...] = total_in[segment] * factor + tile_fold(weights, jnp.add)
+        acc[...] = acc_in[segment] * jnp.tile(factor, (1, local // 128)) + mm(
+            weights.astype(BF16), value_buf[...]
+        )
+        row_total = jnp.sum(total_buf[...], axis=1, keepdims=True)
         emit(
-            segment, row_max, row_total, acc, heads, full, stat_full, own_ref, own_stat_ref, sends
+            segment, max_buf[...], jnp.broadcast_to(row_total, total_buf.shape), acc, heads, full,
+            stat_full, own_ref, own_stat_ref, sends,
         )
 
 
@@ -411,7 +469,7 @@
     return pl.BlockSpec(memory_space=pltpu.SMEM)
 
 
-def call(kernel, inputs, outputs, specs=None, scratch=(), estimate=None, limit=8 << 20, name=None):
+def call(kernel, inputs, outputs, specs=None, scratch=(), estimate=None, limit=8 << 20):
     return pl.pallas_call(
         kernel,
         out_shape=[jax.ShapeDtypeStruct(shape, kind) for shape, kind in outputs],
@@ -420,7 +478,6 @@
         scratch_shapes=list(scratch),
         cost_estimate=estimate,
         compiler_params=pltpu.CompilerParams(vmem_limit_bytes=limit),
-        name=name,
     )(*inputs)
 
 
@@ -444,7 +501,7 @@
     return lax.ppermute(value, ("pos", "head"), moves)
 
 
-def per_device(
+def layer(
     latents, read_tokens, band_start, coverage, present, pattern, cross_query, cross_key,
     cross_value, cross_out, self_query, self_key, self_value, self_out,
 ):
@@ -474,13 +531,7 @@
     part_outputs = [((segs, part, local), F32), ((segs, part, STATS), BF16)] + [
         ((segs, part, local + STATS), BF16)
     ] * (readers - 1)
-    work = [
-        pltpu.VMEM((spread_rows, 128), F32),
-        pltpu.VMEM((spread_rows, 128), F32),
-        pltpu.VMEM((spread_rows, local), F32),
-        pltpu.VMEM((lat_rows, local), F32),
-        pltpu.VMEM((lat_rows, STATS), F32),
-    ]
+    work = [pltpu.VMEM((lat_rows, local), F32), pltpu.VMEM((lat_rows, STATS), F32)]
     most = reads * length
     tiles = -(-most // CHUNK)
     spare = (segs * tiles + 1) // 2 * 2 + 2
@@ -509,7 +560,7 @@
             pltpu.VMEM((segs + 1, spread_rows, 128), F32),
             pltpu.VMEM((segs + 1, spread_rows, local), F32),
         ]
-        + work[3:]
+        + work
         + [pltpu.SemaphoreType.DMA((7,)), pltpu.SemaphoreType.DMA((segs,))],
         estimate=cost(
             2 * segs * most * local * (2 * width + 2 * spread_rows),
@@ -517,65 +568,100 @@
             segs * most * spread_rows,
         ),
         limit=60 * 1024 * 1024,
-        name="cross",
-    )
-
-    def combine(parts, name):
+    )
+
+    def combine(parts):
         own, own_stat, sends = parts[0], parts[1], parts[2:]
         received = [to_reader(value, step + 1) for step, value in enumerate(sends)]
-        inputs = [own.reshape(size, local), own_stat.reshape(size, STATS)] + [
-            value.reshape(size, local + STATS) for value in received
-        ]
+        kept, level = call(
+            own_kernel,
+            (own.reshape(size, local), own_stat.reshape(size, STATS)),
+            [((size, local), F32), ((size, local), F32)],
+            estimate=cost(2 * size * STATS * local, 12 * size * local),
+        )
         return call(
-            combine_kernel, inputs, [((size, local), BF16)], name=name,
+            combine_kernel,
+            [kept, level] + [value.reshape(size, local + STATS) for value in received],
+            [((size, local), BF16)],
             estimate=cost(8 * size * STATS * local, 8 * size * local),
         )[0]
 
-    attended = combine(produced, "join_reads")
+    attended = combine(produced)
     attended_other = swap_cores(attended)
     hidden, normed, query = call(
         hidden_kernel,
         (latents, attended, attended_other, cross_out, cross_out_other, self_query),
         [((size, width), F32), ((size, width), BF16), ((size, local), BF16)],
-        name="hidden",
         estimate=cost(2 * size * width * (width + local), 8 * size * width),
     )
     queries = [query] + [to_reader(query, step) for step in range(1, readers)]
-    blocks = [normed]
-    direct = {0: normed}
+    direct, pair = {}, {}
     for step in steps:
         half = step // 2
-        source = direct[half] if half and half * 2 == step and half in direct else normed
-        direct[step] = both_ways(source, step - half if half in direct and half else step)
-    for step in steps:
-        blocks += [direct[step], swap_cores(direct[step])]
-    keys_most = -(-len(offsets) * part // CHUNK) * CHUNK
-    produced = call(
-        functools.partial(self_kernel, readers, tuple(steps), tuple(offsets)),
-        (pattern, self_key, self_value, *queries, *blocks),
-        part_outputs,
-        specs=[smem()] + [vmem()] * (2 + len(queries) + len(blocks)),
+        if half in direct and 2 * half == step:
+            direct[step] = both_ways(direct[half], half)
+        else:
+            direct[step] = both_ways(normed, step)
+        pair[step] = (direct[step], swap_cores(direct[step]))
+    state = [
+        ((segs, spread_rows, local), BF16),
+        ((segs, spread_rows, 128), F32),
+        ((segs, spread_rows, 128), F32),
+        ((segs, spread_rows, local), F32),
+    ]
+
+    def reach(test):
+        return max(
+            sum(test(abs((segment + offset) // segs)) for offset in offsets)
+            for segment in range(segs)
+        )
+
+    near_keys = -(-reach(lambda step: step <= 1) * part // CHUNK) * CHUNK
+    far_keys = -(-reach(lambda step: step > 1) * part // 128) * 128
+    carried = call(
+        functools.partial(near_kernel, readers, tuple(offsets)),
+        (pattern, self_key, self_value, *queries, normed, *pair[1]),
+        state,
+        specs=[smem()] + [vmem()] * (5 + len(queries)),
         scratch=[
             pltpu.VMEM((segs, lat_rows, local), BF16),
-            pltpu.VMEM((spread_rows, local), BF16),
-            pltpu.VMEM((len(blocks) * size, local), BF16),
-            pltpu.VMEM((len(blocks) * size, local), BF16),
-            pltpu.VMEM((keys_most, local), BF16),
-            pltpu.VMEM((keys_most, local), BF16),
-            pltpu.VMEM((keys_most // CHUNK, spread_rows, CHUNK), F32),
+            pltpu.VMEM((3 * size, local), BF16),
+            pltpu.VMEM((3 * size, local), BF16),
+            pltpu.VMEM((near_keys, local), BF16),
+            pltpu.VMEM((near_keys, local), BF16),
+            pltpu.VMEM((near_keys // CHUNK, spread_rows, CHUNK), F32),
+        ],
+        estimate=cost(4 * segs * near_keys * local * spread_rows, 8 * segs * spread_rows * local),
+        limit=16 << 20,
+    )
+    far = [step for step in steps if step > 1]
+    far_blocks = [block for step in far for block in pair[step]]
+    produced = call(
+        functools.partial(far_kernel, readers, tuple(far), tuple(offsets)),
+        (pattern, self_key, self_value, *carried, *far_blocks),
+        part_outputs,
+        specs=[smem()] + [vmem()] * (6 + len(far_blocks)),
+        scratch=[
+            pltpu.VMEM((len(far_blocks) * size, local), BF16),
+            pltpu.VMEM((len(far_blocks) * size, local), BF16),
+            pltpu.VMEM((far_keys, local), BF16),
+            pltpu.VMEM((far_keys, local), BF16),
+            pltpu.VMEM((spread_rows, 128), F32),
+            pltpu.VMEM((spread_rows, 128), F32),
+            pltpu.VMEM((spread_rows, local), F32),
         ]
         + work,
-        estimate=cost(4 * segs * keys_most * local * spread_rows, 4 * len(blocks) * size * width),
+        estimate=cost(
+            4 * segs * far_keys * local * spread_rows, 8 * segs * spread_rows * local
+        ),
         limit=16 << 20,
-        name="within",
-    )
-    mixed = combine(produced, "join_keys")
+    )
+    mixed = combine(produced)
     mixed_other = swap_cores(mixed)
     return call(
         out_kernel,
         (hidden, mixed, mixed_other, self_out, self_out_other),
         [((segs, part, share), BF16)],
-        name="out",
         estimate=cost(2 * size * width * share, 8 * size * width),
     )[0]
 
@@ -598,7 +684,7 @@
         P("head", None),
     )
     return jax.shard_map(
-        per_device,
+        layer,
         mesh=mesh,
         in_specs=placed,
         out_specs=P(("grp", "pos"), "read", "head"),

time: 64.8 us -> 64.5 us (level)
  waiting for transfers between devices: 21.9 us -> 19.8 us
  Pallas kernels: 19.6 us -> 21 us
    ppermute x3, waiting for transfers between devices: 10.4 us -> 8.34 us  [to_reader(): lax.ppermute(value, 'read', [(i, (i + step) % readers) for i in range(rea...]
    pallas_call x6 -> x9, Pallas kernels: 19.6 us -> 21 us  [call(): pl.pallas_call(kernel, out_shape=[jax.ShapeDtypeStruct(shape, kind) for s...]
  transfers between devices with their start and end apart: 11 -> 11, of which waited for: 7 -> 7; matrix products, arithmetic and copies ran while one was open for 0% -> 0% of each run, Pallas kernels for 1% -> 9%
where the time goes in v4:
time: 64.5 us; the launch traced here: 63.5 us
  Pallas kernels  21 us (33%)
  starting transfers between devices  20.8 us (32%)
  waiting for transfers between devices  19.8 us (31%)
  local copies, waits for them, and re-layouts  1.82 us (3%)
    pallas_call x9, Pallas kernels, call(): pl.pallas_call(kernel, out_shape=[jax.ShapeDtypeStruct(shape, kind) for s...  21 us
    ppermute x2, waiting for transfers between devices, both_ways(): return lax.ppermute(value, ('pos', 'head'), moves)  9.51 us
    ppermute x6, starting transfers between devices, swap_cores(): return lax.ppermute(value, 'head', [(0, 1), (1, 0)])  8.49 us
    ppermute x3, waiting for transfers between devices, to_reader(): lax.ppermute(value, 'read', [(i, (i + step) % readers) for i in range(rea...  8.34 us
    ppermute x3, starting transfers between devices, to_reader(): lax.ppermute(value, 'read', [(i, (i + step) % readers) for i in range(rea...  8.26 us
    ppermute x2, starting transfers between devices, both_ways(): return lax.ppermute(value, ('pos', 'head'), moves)  4 us
    ppermute x6, waiting for transfers between devices, swap_cores(): return lax.ppermute(value, 'head', [(0, 1), (1, 0)])  1.98 us
    unnamed x18, local copies, waits for them, and re-layouts  1.82 us
  transfers between devices with their start and end apart: 11, of which 7 were waited for; matrix products, arithmetic and copies ran while one was open for 0% of the time, Pallas kernels for 9%

profile of v4, /device:TPU:9, one launch (start us, length us, event | category | flops | bytes accessed | tf_op | source)
XLA Modules:
  0.0 63.5 jit_solution(2860652384402503357)
XLA Ops:
  0.0 10.4 %shard_map.136 = (f32[4,64,256]{2,1,0:T(8,128)}, bf16[4,64,128]{2,1,0:T(8,128)(2,1)}, bf16[4,64,384]{2,1,0:T(8,128)(2,1)}) custom-call(s32[4,4]{1,0:T(4,128)} %start_hbm.1, s32[4,4]{1,0:T(4,128)} %cov_hbm.1, s32[4,4]{1,0:T(4,128)} %present_hbm.1, bf16[4,128,512]{2,1,0:T(8,128)(2,1)} %lat_ref.1, bf16[4,4,512,512]{3,2,1,0:T(8,128)(2,1)} %tok_ref.1, ...), custom_call_target="tpu_custom_call" | custom-call | flops 8589934592 | bytes 8388608 | tf_op jit(solution)/shard_map/pallas_call | solution.py:473
  10.5 5.3 %collective-permute-start = (bf16[4,64,384]{2,1,0:T(8,128)(2,1)}, bf16[4,64,384]{2,1,0:T(8,128)(2,1)S(1)}, u32[]{:S(2)}, u32[]{:S(2)}) collective-permute-start(bf16[4,64,384]{2,1,0:T(8,128)(2,1)} %get-tuple-element.26), channel_id=1, source_target_pairs={{0,2},{2,0},{1,3},{3,1},{4,6},{6,4},{5,7},{7,5},{8,10},{10,8},{9,1... | collective-permute-start | bytes 589832 | tf_op jit(solution)/shard_map/ppermute | solution.py:490
  15.7 0.9 %collective-permute-start.2 = (bf16[256,512]{1,0:T(8,128)(2,1)S(1)}, bf16[256,512]{1,0:T(8,128)(2,1)S(1)}, u32[]{:S(2)}, u32[]{:S(2)}) collective-permute-start(bf16[256,512]{1,0:T(8,128)(2,1)S(1)} %copy-done.4), channel_id=1, source_target_pairs={{0,1},{1,0},{2,3},{3,2},{4,5},{5,4},{6,7},{7,6},{8,9},{9,8},{10,11... | collective-permute-start | bytes 786440 | tf_op jit(solution)/shard_map/ppermute | solution.py:485
  16.7 0.9 %copy-done.3 = f32[4,64,256]{2,1,0:T(8,128)S(1)} copy-done((f32[4,64,256]{2,1,0:T(8,128)S(1)}, f32[4,64,256]{2,1,0:T(8,128)}, u32[]{:S(2)}) %copy-start.3) | copy-done | bytes 262168
  17.6 0.8 %copy-done.7 = bf16[4,64,128]{2,1,0:T(8,128)(2,1)S(1)} copy-done((bf16[4,64,128]{2,1,0:T(8,128)(2,1)S(1)}, bf16[4,64,128]{2,1,0:T(8,128)(2,1)}, u32[]{:S(2)}) %copy-start.7) | copy-done | bytes 65560
  18.7 1.9 %collective-permute-done = bf16[4,64,384]{2,1,0:T(8,128)(2,1)S(1)} collective-permute-done((bf16[4,64,384]{2,1,0:T(8,128)(2,1)}, bf16[4,64,384]{2,1,0:T(8,128)(2,1)S(1)}, u32[]{:S(2)}, u32[]{:S(2)}) %collective-permute-start) | collective-permute-done | bytes 196640 | tf_op jit(solution)/shard_map/ppermute | solution.py:490
  20.8 1.3 %collective-permute-start.1 = (bf16[256,256]{1,0:T(8,128)(2,1)S(1)}, bf16[256,256]{1,0:T(8,128)(2,1)S(1)}, u32[]{:S(2)}, u32[]{:S(2)}) collective-permute-start(bf16[256,256]{1,0:T(8,128)(2,1)S(1)} %shard_map.138.own_ref), channel_id=1, source_target_pairs={{0,1},{1,0},{2,3},{3,2},{4,5},{5,4},{6,7},{7,6},{8,9},{9,8},{10,11... | collective-permute-start | bytes 393224 | tf_op jit(solution)/shard_map/ppermute | solution.py:485
  22.2 1.0 %collective-permute-done.1.other_ref = bf16[256,256]{1,0:T(8,128)(2,1)S(1)} collective-permute-done((bf16[256,256]{1,0:T(8,128)(2,1)S(1)}, bf16[256,256]{1,0:T(8,128)(2,1)S(1)}, u32[]{:S(2)}, u32[]{:S(2)}) %collective-permute-start.1) | collective-permute-done | bytes 131104 | tf_op jit(solution)/shard_map/ppermute | solution.py:485
  23.8 2.1 %collective-permute-start.4 = (bf16[256,512]{1,0:T(8,128)(2,1)S(1)}, bf16[256,512]{1,0:T(8,128)(2,1)S(1)}, u32[]{:S(2)}, u32[]{:S(2)}) collective-permute-start(bf16[256,512]{1,0:T(8,128)(2,1)S(1)} %get-tuple-element.29.rest_2_), channel_id=1, source_target_pairs={{0,4},{4,8},{5,1},{8,12},{9,5},{13,9},{2,6},{6,10},{7,3},{10,14},{... | collective-permute-start | bytes 786440 | tf_op jit(solution)/shard_map/ppermute | solution.py:501
  25.9 5.3 %collective-permute-done.4.rest_3_ = bf16[256,512]{1,0:T(8,128)(2,1)S(1)} collective-permute-done((bf16[256,512]{1,0:T(8,128)(2,1)S(1)}, bf16[256,512]{1,0:T(8,128)(2,1)S(1)}, u32[]{:S(2)}, u32[]{:S(2)}) %collective-permute-start.4) | collective-permute-done | bytes 262176 | tf_op jit(solution)/shard_map/ppermute | solution.py:501
  31.2 1.9 %collective-permute-start.6 = (bf16[256,512]{1,0:T(8,128)(2,1)S(1)}, bf16[256,512]{1,0:T(8,128)(2,1)S(1)}, u32[]{:S(2)}, u32[]{:S(2)}) collective-permute-start(bf16[256,512]{1,0:T(8,128)(2,1)S(1)} %collective-permute-done.4.rest_3_), channel_id=1, source_target_pairs={{0,4},{4,8},{5,1},{8,12},{9,5},{13,9},{2,6},{6,10},{7,3},{10,14},{... | collective-permute-start | bytes 786440 | tf_op jit(solution)/shard_map/ppermute | solution.py:501
  33.1 1.3 %collective-permute-start.5 = (bf16[256,512]{1,0:T(8,128)(2,1)S(1)}, bf16[256,512]{1,0:T(8,128)(2,1)S(1)}, u32[]{:S(2)}, u32[]{:S(2)}) collective-permute-start(bf16[256,512]{1,0:T(8,128)(2,1)S(1)} %collective-permute-done.4.rest_3_), channel_id=1, source_target_pairs={{0,1},{1,0},{2,3},{3,2},{4,5},{5,4},{6,7},{7,6},{8,9},{9,8},{10,11... | collective-permute-start | bytes 786440 | tf_op jit(solution)/shard_map/ppermute | solution.py:485
  34.4 4.2 %collective-permute-done.6.rest_4_ = bf16[256,512]{1,0:T(8,128)(2,1)S(1)} collective-permute-done((bf16[256,512]{1,0:T(8,128)(2,1)S(1)}, bf16[256,512]{1,0:T(8,128)(2,1)S(1)}, u32[]{:S(2)}, u32[]{:S(2)}) %collective-permute-start.6) | collective-permute-done | bytes 262176 | tf_op jit(solution)/shard_map/ppermute | solution.py:501
  38.6 2.1 %collective-permute-start.7 = (bf16[256,512]{1,0:T(8,128)(2,1)S(1)}, bf16[256,512]{1,0:T(8,128)(2,1)S(1)}, u32[]{:S(2)}, u32[]{:S(2)}) collective-permute-start(bf16[256,512]{1,0:T(8,128)(2,1)S(1)} %collective-permute-done.6.rest_4_), channel_id=1, source_target_pairs={{0,1},{1,0},{2,3},{3,2},{4,5},{5,4},{6,7},{7,6},{8,9},{9,8},{10,11... | collective-permute-start | bytes 786440 | tf_op jit(solution)/shard_map/ppermute | solution.py:485
  40.7 1.5 %collective-permute-start.3 = (bf16[256,256]{1,0:T(8,128)(2,1)S(1)}, bf16[256,256]{1,0:T(8,128)(2,1)S(1)}, u32[]{:S(2)}, u32[]{:S(2)}) collective-permute-start(bf16[256,256]{1,0:T(8,128)(2,1)S(1)} %get-tuple-element.28.rest_0_), channel_id=1, source_target_pairs={{0,2},{2,0},{1,3},{3,1},{4,6},{6,4},{5,7},{7,5},{8,10},{10,8},{9,1... | collective-permute-start | bytes 393224 | tf_op jit(solution)/shard_map/ppermute | solution.py:490
  42.1 3.6 %collective-permute-done.3.rest_1_ = bf16[256,256]{1,0:T(8,128)(2,1)S(1)} collective-permute-done((bf16[256,256]{1,0:T(8,128)(2,1)S(1)}, bf16[256,256]{1,0:T(8,128)(2,1)S(1)}, u32[]{:S(2)}, u32[]{:S(2)}) %collective-permute-start.3) | collective-permute-done | bytes 131104 | tf_op jit(solution)/shard_map/ppermute | solution.py:490
  45.8 5.0 %shard_map.140 = (bf16[4,512,256]{2,1,0:T(8,128)(2,1)S(1)}, f32[4,512,128]{2,1,0:T(8,128)S(1)}, f32[4,512,128]{2,1,0:T(8,128)S(1)}, f32[4,512,256]{2,1,0:T(8,128)S(1)}) custom-call(s32[4,16]{1,0:T(4,128)S(1)} %copy-done.8, bf16[512,256]{1,0:T(8,128)(2,1)S(1)} %copy-done.1, bf16[512,256]{1,0:T(8,128)(2,1)S(1)} %copy-done.2, ...), custom_call_target="tpu_custom_call" | custom-call | flops 1073741824 | bytes 4194304 | tf_op jit(solution)/shard_map/pallas_call | solution.py:473
  50.8 3.1 %shard_map.141 = (f32[4,64,256]{2,1,0:T(8,128)S(1)}, bf16[4,64,128]{2,1,0:T(8,128)(2,1)S(1)}, bf16[4,64,384]{2,1,0:T(8,128)(2,1)S(1)}) custom-call(s32[4,16]{1,0:T(4,128)S(1)} %copy-done.8, bf16[512,256]{1,0:T(8,128)(2,1)S(1)} %copy-done.1, bf16[512,256]{1,0:T(8,128)(2,1)S(1)} %copy-done.2, bf16[4,512,256]{2,1,0:T(8,128)(2,1)S(1)} %get-tuple-element.30.rest_0_, ...), custom_call_target="tpu_custom_call" | custom-call | flops 268435456 | bytes 4194304 | tf_op jit(solution)/shard_map/pallas_call | solution.py:473
  53.9 1.5 %collective-permute-start.8 = (bf16[4,64,384]{2,1,0:T(8,128)(2,1)S(1)}, bf16[4,64,384]{2,1,0:T(8,128)(2,1)S(1)}, u32[]{:S(2)}, u32[]{:S(2)}) collective-permute-start(bf16[4,64,384]{2,1,0:T(8,128)(2,1)S(1)} %get-tuple-element.38), channel_id=1, source_target_pairs={{0,2},{2,0},{1,3},{3,1},{4,6},{6,4},{5,7},{7,5},{8,10},{10,8},{9,1... | collective-permute-start | bytes 589832 | tf_op jit(solution)/shard_map/ppermute | solution.py:490
  55.4 1.1 %collective-permute-start.10 = (bf16[256,512]{1,0:T(8,128)(2,1)S(1)}, bf16[256,512]{1,0:T(8,128)(2,1)S(1)}, u32[]{:S(2)}, u32[]{:S(2)}) collective-permute-start(bf16[256,512]{1,0:T(8,128)(2,1)S(1)} %copy-done.6), channel_id=1, source_target_pairs={{0,1},{1,0},{2,3},{3,2},{4,5},{5,4},{6,7},{7,6},{8,9},{9,8},{10,11... | collective-permute-start | bytes 786440 | tf_op jit(solution)/shard_map/ppermute | solution.py:485
  56.8 2.9 %collective-permute-done.8 = bf16[4,64,384]{2,1,0:T(8,128)(2,1)S(1)} collective-permute-done((bf16[4,64,384]{2,1,0:T(8,128)(2,1)S(1)}, bf16[4,64,384]{2,1,0:T(8,128)(2,1)S(1)}, u32[]{:S(2)}, u32[]{:S(2)}) %collective-permute-start.8) | collective-permute-done | bytes 196640 | tf_op jit(solution)/shard_map/ppermute | solution.py:490
  59.9 1.8 %collective-permute-start.9 = (bf16[256,256]{1,0:T(8,128)(2,1)S(1)}, bf16[256,256]{1,0:T(8,128)(2,1)S(1)}, u32[]{:S(2)}, u32[]{:S(2)}) collective-permute-start(bf16[256,256]{1,0:T(8,128)(2,1)S(1)} %shard_map.143.own_ref), channel_id=1, source_target_pairs={{0,1},{1,0},{2,3},{3,2},{4,5},{5,4},{6,7},{7,6},{8,9},{9,8},{10,11... | collective-permute-start | bytes 393224 | tf_op jit(solution)/shard_map/ppermute | solution.py:485
  61.6 1.0 %collective-permute-done.9.other_ref = bf16[256,256]{1,0:T(8,128)(2,1)S(1)} collective-permute-done((bf16[256,256]{1,0:T(8,128)(2,1)S(1)}, bf16[256,256]{1,0:T(8,128)(2,1)S(1)}, u32[]{:S(2)}, u32[]{:S(2)}) %collective-permute-start.9) | collective-permute-done | bytes 131104 | tf_op jit(solution)/shard_map/ppermute | solution.py:485
  62.6 0.9 %shard_map.144 = bf16[4,64,256]{2,1,0:T(8,128)(2,1)} custom-call(f32[256,512]{1,0:T(8,128)S(1)} %get-tuple-element.27.hid_ref, bf16[256,256]{1,0:T(8,128)(2,1)S(1)} %shard_map.143.own_ref, bf16[256,256]{1,0:T(8,128)(2,1)S(1)} %collective-permute-done.9.other_ref, bf16[256,512]{1,0:T(8,128)(2,1)S(1)} %copy-done.6, ...), custom_call_target="tpu_custom_call" | custom-call | flops 67108864 | bytes 1048576 | tf_op jit(solution)/shard_map/pallas_call | solution.py:473
  (25 shorter events, 1.6 us)
Async XLA Ops:
  0.0 23.1 %copy-start = (bf16[4,128,512]{2,1,0:T(8,128)(2,1)S(1)}, bf16[4,128,512]{2,1,0:T(8,128)(2,1)}, u32[]{:S(2)}) copy-start(bf16[4,128,512]{2,1,0:T(8,128)(2,1)} %lat_ref.1) | copy-start | bytes 1572868
  0.0 15.7 %copy-start.4 = (bf16[256,512]{1,0:T(8,128)(2,1)S(1)}, bf16[256,512]{1,0:T(8,128)(2,1)}, u32[]{:S(2)}) copy-start(bf16[256,512]{1,0:T(8,128)(2,1)} %wo_ref.2) | copy-start | bytes 786436
  0.0 23.1 %copy-start.5 = (bf16[512,256]{1,0:T(8,128)(2,1)S(1)}, bf16[512,256]{1,0:T(8,128)(2,1)}, u32[]{:S(2)}) copy-start(bf16[512,256]{1,0:T(8,128)(2,1)} %wq_ref.1) | copy-start | bytes 786436
  0.0 45.7 %copy-start.8 = (s32[4,16]{1,0:T(4,128)S(1)}, s32[4,16]{1,0:T(4,128)}, u32[]{:S(2)}) copy-start(s32[4,16]{1,0:T(4,128)} %pattern_ref.3) | copy-start | bytes 772
  0.0 45.7 %copy-start.1 = (bf16[512,256]{1,0:T(8,128)(2,1)S(1)}, bf16[512,256]{1,0:T(8,128)(2,1)}, u32[]{:S(2)}) copy-start(bf16[512,256]{1,0:T(8,128)(2,1)} %wk_ref.3) | copy-start | bytes 786436
  0.0 45.7 %copy-start.2 = (bf16[512,256]{1,0:T(8,128)(2,1)S(1)}, bf16[512,256]{1,0:T(8,128)(2,1)}, u32[]{:S(2)}) copy-start(bf16[512,256]{1,0:T(8,128)(2,1)} %wv_ref.3) | copy-start | bytes 786436
  0.0 55.4 %copy-start.6 = (bf16[256,512]{1,0:T(8,128)(2,1)S(1)}, bf16[256,512]{1,0:T(8,128)(2,1)}, u32[]{:S(2)}) copy-start(bf16[256,512]{1,0:T(8,128)(2,1)} %wo_ref.3) | copy-start | bytes 786436
  10.5 10.1 %collective-permute-start = (bf16[4,64,384]{2,1,0:T(8,128)(2,1)}, bf16[4,64,384]{2,1,0:T(8,128)(2,1)S(1)}, u32[]{:S(2)}, u32[]{:S(2)}) collective-permute-start(bf16[4,64,384]{2,1,0:T(8,128)(2,1)} %get-tuple-element.26), channel_id=1, source_target_pairs={{0,2},{2,0},{1,3},{3,1},{4,6},{6,4},{5,7},{7,5},{8,10},{10,8},{9,1... | collective-permute-start | bytes 589832 | tf_op jit(solution)/shard_map/ppermute | solution.py:490
  15.7 6.4 %collective-permute-start.2 = (bf16[256,512]{1,0:T(8,128)(2,1)S(1)}, bf16[256,512]{1,0:T(8,128)(2,1)S(1)}, u32[]{:S(2)}, u32[]{:S(2)}) collective-permute-start(bf16[256,512]{1,0:T(8,128)(2,1)S(1)} %copy-done.4), channel_id=1, source_target_pairs={{0,1},{1,0},{2,3},{3,2},{4,5},{5,4},{6,7},{7,6},{8,9},{9,8},{10,11... | collective-permute-start | bytes 786440 | tf_op jit(solution)/shard_map/ppermute | solution.py:485
  16.7 0.9 %copy-start.3 = (f32[4,64,256]{2,1,0:T(8,128)S(1)}, f32[4,64,256]{2,1,0:T(8,128)}, u32[]{:S(2)}) copy-start(f32[4,64,256]{2,1,0:T(8,128)} %get-tuple-element.22) | copy-start | bytes 786436
  17.6 0.8 %copy-start.7 = (bf16[4,64,128]{2,1,0:T(8,128)(2,1)S(1)}, bf16[4,64,128]{2,1,0:T(8,128)(2,1)}, u32[]{:S(2)}) copy-start(bf16[4,64,128]{2,1,0:T(8,128)(2,1)} %get-tuple-element.23) | copy-start | bytes 196612
  20.8 2.3 %collective-permute-start.1 = (bf16[256,256]{1,0:T(8,128)(2,1)S(1)}, bf16[256,256]{1,0:T(8,128)(2,1)S(1)}, u32[]{:S(2)}, u32[]{:S(2)}) collective-permute-start(bf16[256,256]{1,0:T(8,128)(2,1)S(1)} %shard_map.138.own_ref), channel_id=1, source_target_pairs={{0,1},{1,0},{2,3},{3,2},{4,5},{5,4},{6,7},{7,6},{8,9},{9,8},{10,11... | collective-permute-start | bytes 393224 | tf_op jit(solution)/shard_map/ppermute | solution.py:485
  23.8 7.4 %collective-permute-start.4 = (bf16[256,512]{1,0:T(8,128)(2,1)S(1)}, bf16[256,512]{1,0:T(8,128)(2,1)S(1)}, u32[]{:S(2)}, u32[]{:S(2)}) collective-permute-start(bf16[256,512]{1,0:T(8,128)(2,1)S(1)} %get-tuple-element.29.rest_2_), channel_id=1, source_target_pairs={{0,4},{4,8},{5,1},{8,12},{9,5},{13,9},{2,6},{6,10},{7,3},{10,14},{... | collective-permute-start | bytes 786440 | tf_op jit(solution)/shard_map/ppermute | solution.py:501
  31.2 7.4 %collective-permute-start.6 = (bf16[256,512]{1,0:T(8,128)(2,1)S(1)}, bf16[256,512]{1,0:T(8,128)(2,1)S(1)}, u32[]{:S(2)}, u32[]{:S(2)}) collective-permute-start(bf16[256,512]{1,0:T(8,128)(2,1)S(1)} %collective-permute-done.4.rest_3_), channel_id=1, source_target_pairs={{0,4},{4,8},{5,1},{8,12},{9,5},{13,9},{2,6},{6,10},{7,3},{10,14},{... | collective-permute-start | bytes 786440 | tf_op jit(solution)/shard_map/ppermute | solution.py:501
  33.1 12.6 %collective-permute-start.5 = (bf16[256,512]{1,0:T(8,128)(2,1)S(1)}, bf16[256,512]{1,0:T(8,128)(2,1)S(1)}, u32[]{:S(2)}, u32[]{:S(2)}) collective-permute-start(bf16[256,512]{1,0:T(8,128)(2,1)S(1)} %collective-permute-done.4.rest_3_), channel_id=1, source_target_pairs={{0,1},{1,0},{2,3},{3,2},{4,5},{5,4},{6,7},{7,6},{8,9},{9,8},{10,11... | collective-permute-start | bytes 786440 | tf_op jit(solution)/shard_map/ppermute | solution.py:485
  38.6 12.2 %collective-permute-start.7 = (bf16[256,512]{1,0:T(8,128)(2,1)S(1)}, bf16[256,512]{1,0:T(8,128)(2,1)S(1)}, u32[]{:S(2)}, u32[]{:S(2)}) collective-permute-start(bf16[256,512]{1,0:T(8,128)(2,1)S(1)} %collective-permute-done.6.rest_4_), channel_id=1, source_target_pairs={{0,1},{1,0},{2,3},{3,2},{4,5},{5,4},{6,7},{7,6},{8,9},{9,8},{10,11... | collective-permute-start | bytes 786440 | tf_op jit(solution)/shard_map/ppermute | solution.py:485
  40.7 5.1 %collective-permute-start.3 = (bf16[256,256]{1,0:T(8,128)(2,1)S(1)}, bf16[256,256]{1,0:T(8,128)(2,1)S(1)}, u32[]{:S(2)}, u32[]{:S(2)}) collective-permute-start(bf16[256,256]{1,0:T(8,128)(2,1)S(1)} %get-tuple-element.28.rest_0_), channel_id=1, source_target_pairs={{0,2},{2,0},{1,3},{3,1},{4,6},{6,4},{5,7},{7,5},{8,10},{10,8},{9,1... | collective-permute-start | bytes 393224 | tf_op jit(solution)/shard_map/ppermute | solution.py:490
  53.9 5.7 %collective-permute-start.8 = (bf16[4,64,384]{2,1,0:T(8,128)(2,1)S(1)}, bf16[4,64,384]{2,1,0:T(8,128)(2,1)S(1)}, u32[]{:S(2)}, u32[]{:S(2)}) collective-permute-start(bf16[4,64,384]{2,1,0:T(8,128)(2,1)S(1)} %get-tuple-element.38), channel_id=1, source_target_pairs={{0,2},{2,0},{1,3},{3,1},{4,6},{6,4},{5,7},{7,5},{8,10},{10,8},{9,1... | collective-permute-start | bytes 589832 | tf_op jit(solution)/shard_map/ppermute | solution.py:490
  55.4 6.2 %collective-permute-start.10 = (bf16[256,512]{1,0:T(8,128)(2,1)S(1)}, bf16[256,512]{1,0:T(8,128)(2,1)S(1)}, u32[]{:S(2)}, u32[]{:S(2)}) collective-permute-start(bf16[256,512]{1,0:T(8,128)(2,1)S(1)} %copy-done.6), channel_id=1, source_target_pairs={{0,1},{1,0},{2,3},{3,2},{4,5},{5,4},{6,7},{7,6},{8,9},{9,8},{10,11... | collective-permute-start | bytes 786440 | tf_op jit(solution)/shard_map/ppermute | solution.py:485
  59.9 2.7 %collective-permute-start.9 = (bf16[256,256]{1,0:T(8,128)(2,1)S(1)}, bf16[256,256]{1,0:T(8,128)(2,1)S(1)}, u32[]{:S(2)}, u32[]{:S(2)}) collective-permute-start(bf16[256,256]{1,0:T(8,128)(2,1)S(1)} %shard_map.143.own_ref), channel_id=1, source_target_pairs={{0,1},{1,0},{2,3},{3,2},{4,5},{5,4},{6,7},{7,6},{8,9},{9,8},{10,11... | collective-permute-start | bytes 393224 | tf_op jit(solution)/shard_map/ppermute | solution.py:485

commit v5 on v4

--- a/solution.py
+++ b/solution.py
@@ -492,12 +492,9 @@
 
 def both_ways(value, step):
     count = lax.axis_size("pos")
-    moves = []
-    for place in range(count):
-        if place + step < count:
-            moves.append((2 * place, 2 * (place + step)))
-        if place - step >= 0:
-            moves.append((2 * place + 1, 2 * (place - step) + 1))
+    ring = [2 * place for place in range(count)]
+    ring += [2 * place + 1 for place in reversed(range(count))]
+    moves = [(ring[i], ring[(i + step) % len(ring)]) for i in range(len(ring))]
     return lax.ppermute(value, ("pos", "head"), moves)
 
 

time: 64.5 us -> 60.8 us (0.943)
  starting transfers between devices: 20.8 us -> 16.9 us
    ppermute x2, starting transfers between devices: 4 us -> 0.2 us  [both_ways(): return lax.ppermute(value, ('pos', 'head'), moves)]
  transfers between devices with their start and end apart: 11 -> 11, of which waited for: 7 -> 7; matrix products, arithmetic and copies ran while one was open for 0% -> 0% of each run, Pallas kernels for 9% -> 10%
where the time goes in v5:
time: 60.8 us; the launch traced here: 59.8 us
  Pallas kernels  21 us (35%)
  waiting for transfers between devices  19.9 us (33%)
  starting transfers between devices  16.9 us (28%)
  local copies, waits for them, and re-layouts  1.82 us (3%)
    pallas_call x9, Pallas kernels, call(): pl.pallas_call(kernel, out_shape=[jax.ShapeDtypeStruct(shape, kind) for s...  21 us
    ppermute x2, waiting for transfers between devices, both_ways(): return lax.ppermute(value, ('pos', 'head'), moves)  9.63 us
    ppermute x6, starting transfers between devices, swap_cores(): return lax.ppermute(value, 'head', [(0, 1), (1, 0)])  8.48 us
    ppermute x3, waiting for transfers between devices, to_reader(): lax.ppermute(value, 'read', [(i, (i + step) % readers) for i in range(rea...  8.29 us
    ppermute x3, starting transfers between devices, to_reader(): lax.ppermute(value, 'read', [(i, (i + step) % readers) for i in range(rea...  8.26 us
    ppermute x6, waiting for transfers between devices, swap_cores(): return lax.ppermute(value, 'head', [(0, 1), (1, 0)])  1.98 us
    unnamed x18, local copies, waits for them, and re-layouts  1.82 us
  transfers between devices with their start and end apart: 11, of which 7 were waited for; matrix products, arithmetic and copies ran while one was open for 0% of the time, Pallas kernels for 10%

profile of v5, /device:TPU:9, one launch (start us, length us, event | category | flops | bytes accessed | tf_op | source)
XLA Modules:
  0.0 59.8 jit_solution(15296386536008491514)
XLA Ops:
  0.0 10.4 %shard_map.136 = (f32[4,64,256]{2,1,0:T(8,128)}, bf16[4,64,128]{2,1,0:T(8,128)(2,1)}, bf16[4,64,384]{2,1,0:T(8,128)(2,1)}) custom-call(s32[4,4]{1,0:T(4,128)} %start_hbm.1, s32[4,4]{1,0:T(4,128)} %cov_hbm.1, s32[4,4]{1,0:T(4,128)} %present_hbm.1, bf16[4,128,512]{2,1,0:T(8,128)(2,1)} %lat_ref.1, bf16[4,4,512,512]{3,2,1,0:T(8,128)(2,1)} %tok_ref.1, ...), custom_call_target="tpu_custom_call" | custom-call | flops 8589934592 | bytes 8388608 | tf_op jit(solution)/shard_map/pallas_call | solution.py:473
  10.5 5.3 %collective-permute-start = (bf16[4,64,384]{2,1,0:T(8,128)(2,1)}, bf16[4,64,384]{2,1,0:T(8,128)(2,1)S(1)}, u32[]{:S(2)}, u32[]{:S(2)}) collective-permute-start(bf16[4,64,384]{2,1,0:T(8,128)(2,1)} %get-tuple-element.26), channel_id=1, source_target_pairs={{0,2},{2,0},{1,3},{3,1},{4,6},{6,4},{5,7},{7,5},{8,10},{10,8},{9,1... | collective-permute-start | bytes 589832 | tf_op jit(solution)/shard_map/ppermute | solution.py:490
  15.7 0.9 %collective-permute-start.2 = (bf16[256,512]{1,0:T(8,128)(2,1)S(1)}, bf16[256,512]{1,0:T(8,128)(2,1)S(1)}, u32[]{:S(2)}, u32[]{:S(2)}) collective-permute-start(bf16[256,512]{1,0:T(8,128)(2,1)S(1)} %copy-done.4), channel_id=1, source_target_pairs={{0,1},{1,0},{2,3},{3,2},{4,5},{5,4},{6,7},{7,6},{8,9},{9,8},{10,11... | collective-permute-start | bytes 786440 | tf_op jit(solution)/shard_map/ppermute | solution.py:485
  16.7 0.9 %copy-done.3 = f32[4,64,256]{2,1,0:T(8,128)S(1)} copy-done((f32[4,64,256]{2,1,0:T(8,128)S(1)}, f32[4,64,256]{2,1,0:T(8,128)}, u32[]{:S(2)}) %copy-start.3) | copy-done | bytes 262168
  17.6 0.8 %copy-done.7 = bf16[4,64,128]{2,1,0:T(8,128)(2,1)S(1)} copy-done((bf16[4,64,128]{2,1,0:T(8,128)(2,1)S(1)}, bf16[4,64,128]{2,1,0:T(8,128)(2,1)}, u32[]{:S(2)}) %copy-start.7) | copy-done | bytes 65560
  18.7 1.9 %collective-permute-done = bf16[4,64,384]{2,1,0:T(8,128)(2,1)S(1)} collective-permute-done((bf16[4,64,384]{2,1,0:T(8,128)(2,1)}, bf16[4,64,384]{2,1,0:T(8,128)(2,1)S(1)}, u32[]{:S(2)}, u32[]{:S(2)}) %collective-permute-start) | collective-permute-done | bytes 196640 | tf_op jit(solution)/shard_map/ppermute | solution.py:490
  20.6 0.3 shard_map.138.own_ref
  20.8 1.3 %collective-permute-start.1 = (bf16[256,256]{1,0:T(8,128)(2,1)S(1)}, bf16[256,256]{1,0:T(8,128)(2,1)S(1)}, u32[]{:S(2)}, u32[]{:S(2)}) collective-permute-start(bf16[256,256]{1,0:T(8,128)(2,1)S(1)} %shard_map.138.own_ref), channel_id=1, source_target_pairs={{0,1},{1,0},{2,3},{3,2},{4,5},{5,4},{6,7},{7,6},{8,9},{9,8},{10,11... | collective-permute-start | bytes 393224 | tf_op jit(solution)/shard_map/ppermute | solution.py:485
  22.2 1.0 %collective-permute-done.1.other_ref = bf16[256,256]{1,0:T(8,128)(2,1)S(1)} collective-permute-done((bf16[256,256]{1,0:T(8,128)(2,1)S(1)}, bf16[256,256]{1,0:T(8,128)(2,1)S(1)}, u32[]{:S(2)}, u32[]{:S(2)}) %collective-permute-start.1) | collective-permute-done | bytes 131104 | tf_op jit(solution)/shard_map/ppermute | solution.py:485
  23.1 0.6 %shard_map.139 = (f32[256,512]{1,0:T(8,128)S(1)}, bf16[256,512]{1,0:T(8,128)(2,1)S(1)}, bf16[256,256]{1,0:T(8,128)(2,1)S(1)}) custom-call(bf16[4,128,512]{2,1,0:T(8,128)(2,1)S(1)} %copy-done, bf16[256,256]{1,0:T(8,128)(2,1)S(1)} %shard_map.138.own_ref, bf16[256,256]{1,0:T(8,128)(2,1)S(1)} %collective-permute-done.1.other_ref, ...), custom_call_target="tpu_custom_call" | custom-call | flops 201326592 | bytes 1048576 | tf_op jit(solution)/shard_map/pallas_call | solution.py:473
  24.0 5.3 %collective-permute-done.4.rest_3_ = bf16[256,512]{1,0:T(8,128)(2,1)S(1)} collective-permute-done((bf16[256,512]{1,0:T(8,128)(2,1)S(1)}, bf16[256,512]{1,0:T(8,128)(2,1)S(1)}, u32[]{:S(2)}, u32[]{:S(2)}) %collective-permute-start.4) | collective-permute-done | bytes 262176 | tf_op jit(solution)/shard_map/ppermute | solution.py:498
  29.3 1.2 %collective-permute-start.5 = (bf16[256,512]{1,0:T(8,128)(2,1)S(1)}, bf16[256,512]{1,0:T(8,128)(2,1)S(1)}, u32[]{:S(2)}, u32[]{:S(2)}) collective-permute-start(bf16[256,512]{1,0:T(8,128)(2,1)S(1)} %collective-permute-done.4.rest_3_), channel_id=1, source_target_pairs={{0,1},{1,0},{2,3},{3,2},{4,5},{5,4},{6,7},{7,6},{8,9},{9,8},{10,11... | collective-permute-start | bytes 786440 | tf_op jit(solution)/shard_map/ppermute | solution.py:485
  30.6 4.3 %collective-permute-done.6.rest_4_ = bf16[256,512]{1,0:T(8,128)(2,1)S(1)} collective-permute-done((bf16[256,512]{1,0:T(8,128)(2,1)S(1)}, bf16[256,512]{1,0:T(8,128)(2,1)S(1)}, u32[]{:S(2)}, u32[]{:S(2)}) %collective-permute-start.6) | collective-permute-done | bytes 262176 | tf_op jit(solution)/shard_map/ppermute | solution.py:498
  34.8 2.1 %collective-permute-start.7 = (bf16[256,512]{1,0:T(8,128)(2,1)S(1)}, bf16[256,512]{1,0:T(8,128)(2,1)S(1)}, u32[]{:S(2)}, u32[]{:S(2)}) collective-permute-start(bf16[256,512]{1,0:T(8,128)(2,1)S(1)} %collective-permute-done.6.rest_4_), channel_id=1, source_target_pairs={{0,1},{1,0},{2,3},{3,2},{4,5},{5,4},{6,7},{7,6},{8,9},{9,8},{10,11... | collective-permute-start | bytes 786440 | tf_op jit(solution)/shard_map/ppermute | solution.py:485
  36.9 1.5 %collective-permute-start.3 = (bf16[256,256]{1,0:T(8,128)(2,1)S(1)}, bf16[256,256]{1,0:T(8,128)(2,1)S(1)}, u32[]{:S(2)}, u32[]{:S(2)}) collective-permute-start(bf16[256,256]{1,0:T(8,128)(2,1)S(1)} %get-tuple-element.28.rest_0_), channel_id=1, source_target_pairs={{0,2},{2,0},{1,3},{3,1},{4,6},{6,4},{5,7},{7,5},{8,10},{10,8},{9,1... | collective-permute-start | bytes 393224 | tf_op jit(solution)/shard_map/ppermute | solution.py:490
  38.4 3.6 %collective-permute-done.3.rest_1_ = bf16[256,256]{1,0:T(8,128)(2,1)S(1)} collective-permute-done((bf16[256,256]{1,0:T(8,128)(2,1)S(1)}, bf16[256,256]{1,0:T(8,128)(2,1)S(1)}, u32[]{:S(2)}, u32[]{:S(2)}) %collective-permute-start.3) | collective-permute-done | bytes 131104 | tf_op jit(solution)/shard_map/ppermute | solution.py:490
  42.0 5.0 %shard_map.140 = (bf16[4,512,256]{2,1,0:T(8,128)(2,1)S(1)}, f32[4,512,128]{2,1,0:T(8,128)S(1)}, f32[4,512,128]{2,1,0:T(8,128)S(1)}, f32[4,512,256]{2,1,0:T(8,128)S(1)}) custom-call(s32[4,16]{1,0:T(4,128)S(1)} %copy-done.8, bf16[512,256]{1,0:T(8,128)(2,1)S(1)} %copy-done.1, bf16[512,256]{1,0:T(8,128)(2,1)S(1)} %copy-done.2, ...), custom_call_target="tpu_custom_call" | custom-call | flops 1073741824 | bytes 4194304 | tf_op jit(solution)/shard_map/pallas_call | solution.py:473
  47.0 3.1 %shard_map.141 = (f32[4,64,256]{2,1,0:T(8,128)S(1)}, bf16[4,64,128]{2,1,0:T(8,128)(2,1)S(1)}, bf16[4,64,384]{2,1,0:T(8,128)(2,1)S(1)}) custom-call(s32[4,16]{1,0:T(4,128)S(1)} %copy-done.8, bf16[512,256]{1,0:T(8,128)(2,1)S(1)} %copy-done.1, bf16[512,256]{1,0:T(8,128)(2,1)S(1)} %copy-done.2, bf16[4,512,256]{2,1,0:T(8,128)(2,1)S(1)} %get-tuple-element.30.rest_0_, ...), custom_call_target="tpu_custom_call" | custom-call | flops 268435456 | bytes 4194304 | tf_op jit(solution)/shard_map/pallas_call | solution.py:473
  50.1 1.5 %collective-permute-start.8 = (bf16[4,64,384]{2,1,0:T(8,128)(2,1)S(1)}, bf16[4,64,384]{2,1,0:T(8,128)(2,1)S(1)}, u32[]{:S(2)}, u32[]{:S(2)}) collective-permute-start(bf16[4,64,384]{2,1,0:T(8,128)(2,1)S(1)} %get-tuple-element.38), channel_id=1, source_target_pairs={{0,2},{2,0},{1,3},{3,1},{4,6},{6,4},{5,7},{7,5},{8,10},{10,8},{9,1... | collective-permute-start | bytes 589832 | tf_op jit(solution)/shard_map/ppermute | solution.py:490
  51.7 1.1 %collective-permute-start.10 = (bf16[256,512]{1,0:T(8,128)(2,1)S(1)}, bf16[256,512]{1,0:T(8,128)(2,1)S(1)}, u32[]{:S(2)}, u32[]{:S(2)}) collective-permute-start(bf16[256,512]{1,0:T(8,128)(2,1)S(1)} %copy-done.6), channel_id=1, source_target_pairs={{0,1},{1,0},{2,3},{3,2},{4,5},{5,4},{6,7},{7,6},{8,9},{9,8},{10,11... | collective-permute-start | bytes 786440 | tf_op jit(solution)/shard_map/ppermute | solution.py:485
  53.0 2.8 %collective-permute-done.8 = bf16[4,64,384]{2,1,0:T(8,128)(2,1)S(1)} collective-permute-done((bf16[4,64,384]{2,1,0:T(8,128)(2,1)S(1)}, bf16[4,64,384]{2,1,0:T(8,128)(2,1)S(1)}, u32[]{:S(2)}, u32[]{:S(2)}) %collective-permute-start.8) | collective-permute-done | bytes 196640 | tf_op jit(solution)/shard_map/ppermute | solution.py:490
  56.1 1.8 %collective-permute-start.9 = (bf16[256,256]{1,0:T(8,128)(2,1)S(1)}, bf16[256,256]{1,0:T(8,128)(2,1)S(1)}, u32[]{:S(2)}, u32[]{:S(2)}) collective-permute-start(bf16[256,256]{1,0:T(8,128)(2,1)S(1)} %shard_map.143.own_ref), channel_id=1, source_target_pairs={{0,1},{1,0},{2,3},{3,2},{4,5},{5,4},{6,7},{7,6},{8,9},{9,8},{10,11... | collective-permute-start | bytes 393224 | tf_op jit(solution)/shard_map/ppermute | solution.py:485
  57.9 1.0 %collective-permute-done.9.other_ref = bf16[256,256]{1,0:T(8,128)(2,1)S(1)} collective-permute-done((bf16[256,256]{1,0:T(8,128)(2,1)S(1)}, bf16[256,256]{1,0:T(8,128)(2,1)S(1)}, u32[]{:S(2)}, u32[]{:S(2)}) %collective-permute-start.9) | collective-permute-done | bytes 131104 | tf_op jit(solution)/shard_map/ppermute | solution.py:485
  58.9 0.9 %shard_map.144 = bf16[4,64,256]{2,1,0:T(8,128)(2,1)} custom-call(f32[256,512]{1,0:T(8,128)S(1)} %get-tuple-element.27.hid_ref, bf16[256,256]{1,0:T(8,128)(2,1)S(1)} %shard_map.143.own_ref, bf16[256,256]{1,0:T(8,128)(2,1)S(1)} %collective-permute-done.9.other_ref, bf16[256,512]{1,0:T(8,128)(2,1)S(1)} %copy-done.6, ...), custom_call_target="tpu_custom_call" | custom-call | flops 67108864 | bytes 1048576 | tf_op jit(solution)/shard_map/pallas_call | solution.py:473
  (25 shorter events, 0.9 us)
Async XLA Ops:
  0.0 23.1 %copy-start = (bf16[4,128,512]{2,1,0:T(8,128)(2,1)S(1)}, bf16[4,128,512]{2,1,0:T(8,128)(2,1)}, u32[]{:S(2)}) copy-start(bf16[4,128,512]{2,1,0:T(8,128)(2,1)} %lat_ref.1) | copy-start | bytes 1572868
  0.0 15.7 %copy-start.4 = (bf16[256,512]{1,0:T(8,128)(2,1)S(1)}, bf16[256,512]{1,0:T(8,128)(2,1)}, u32[]{:S(2)}) copy-start(bf16[256,512]{1,0:T(8,128)(2,1)} %wo_ref.2) | copy-start | bytes 786436
  0.0 23.1 %copy-start.5 = (bf16[512,256]{1,0:T(8,128)(2,1)S(1)}, bf16[512,256]{1,0:T(8,128)(2,1)}, u32[]{:S(2)}) copy-start(bf16[512,256]{1,0:T(8,128)(2,1)} %wq_ref.1) | copy-start | bytes 786436
  0.0 42.0 %copy-start.8 = (s32[4,16]{1,0:T(4,128)S(1)}, s32[4,16]{1,0:T(4,128)}, u32[]{:S(2)}) copy-start(s32[4,16]{1,0:T(4,128)} %pattern_ref.3) | copy-start | bytes 772
  0.0 42.0 %copy-start.1 = (bf16[512,256]{1,0:T(8,128)(2,1)S(1)}, bf16[512,256]{1,0:T(8,128)(2,1)}, u32[]{:S(2)}) copy-start(bf16[512,256]{1,0:T(8,128)(2,1)} %wk_ref.3) | copy-start | bytes 786436
  0.0 42.0 %copy-start.2 = (bf16[512,256]{1,0:T(8,128)(2,1)S(1)}, bf16[512,256]{1,0:T(8,128)(2,1)}, u32[]{:S(2)}) copy-start(bf16[512,256]{1,0:T(8,128)(2,1)} %wv_ref.3) | copy-start | bytes 786436
  0.0 51.6 %copy-start.6 = (bf16[256,512]{1,0:T(8,128)(2,1)S(1)}, bf16[256,512]{1,0:T(8,128)(2,1)}, u32[]{:S(2)}) copy-start(bf16[256,512]{1,0:T(8,128)(2,1)} %wo_ref.3) | copy-start | bytes 786436
  10.5 10.1 %collective-permute-start = (bf16[4,64,384]{2,1,0:T(8,128)(2,1)}, bf16[4,64,384]{2,1,0:T(8,128)(2,1)S(1)}, u32[]{:S(2)}, u32[]{:S(2)}) collective-permute-start(bf16[4,64,384]{2,1,0:T(8,128)(2,1)} %get-tuple-element.26), channel_id=1, source_target_pairs={{0,2},{2,0},{1,3},{3,1},{4,6},{6,4},{5,7},{7,5},{8,10},{10,8},{9,1... | collective-permute-start | bytes 589832 | tf_op jit(solution)/shard_map/ppermute | solution.py:490
  15.7 6.4 %collective-permute-start.2 = (bf16[256,512]{1,0:T(8,128)(2,1)S(1)}, bf16[256,512]{1,0:T(8,128)(2,1)S(1)}, u32[]{:S(2)}, u32[]{:S(2)}) collective-permute-start(bf16[256,512]{1,0:T(8,128)(2,1)S(1)} %copy-done.4), channel_id=1, source_target_pairs={{0,1},{1,0},{2,3},{3,2},{4,5},{5,4},{6,7},{7,6},{8,9},{9,8},{10,11... | collective-permute-start | bytes 786440 | tf_op jit(solution)/shard_map/ppermute | solution.py:485
  16.7 0.9 %copy-start.3 = (f32[4,64,256]{2,1,0:T(8,128)S(1)}, f32[4,64,256]{2,1,0:T(8,128)}, u32[]{:S(2)}) copy-start(f32[4,64,256]{2,1,0:T(8,128)} %get-tuple-element.22) | copy-start | bytes 786436
  17.6 0.8 %copy-start.7 = (bf16[4,64,128]{2,1,0:T(8,128)(2,1)S(1)}, bf16[4,64,128]{2,1,0:T(8,128)(2,1)}, u32[]{:S(2)}) copy-start(bf16[4,64,128]{2,1,0:T(8,128)(2,1)} %get-tuple-element.23) | copy-start | bytes 196612
  20.8 2.3 %collective-permute-start.1 = (bf16[256,256]{1,0:T(8,128)(2,1)S(1)}, bf16[256,256]{1,0:T(8,128)(2,1)S(1)}, u32[]{:S(2)}, u32[]{:S(2)}) collective-permute-start(bf16[256,256]{1,0:T(8,128)(2,1)S(1)} %shard_map.138.own_ref), channel_id=1, source_target_pairs={{0,1},{1,0},{2,3},{3,2},{4,5},{5,4},{6,7},{7,6},{8,9},{9,8},{10,11... | collective-permute-start | bytes 393224 | tf_op jit(solution)/shard_map/ppermute | solution.py:485
  23.8 5.5 %collective-permute-start.4 = (bf16[256,512]{1,0:T(8,128)(2,1)S(1)}, bf16[256,512]{1,0:T(8,128)(2,1)S(1)}, u32[]{:S(2)}, u32[]{:S(2)}) collective-permute-start(bf16[256,512]{1,0:T(8,128)(2,1)S(1)} %get-tuple-element.29.rest_2_), channel_id=1, source_target_pairs={{0,4},{4,8},{8,12},{12,13},{13,9},{9,5},{5,1},{1,0},{2,6},{6,10},{... | collective-permute-start | bytes 786440 | tf_op jit(solution)/shard_map/ppermute | solution.py:498
  29.3 5.5 %collective-permute-start.6 = (bf16[256,512]{1,0:T(8,128)(2,1)S(1)}, bf16[256,512]{1,0:T(8,128)(2,1)S(1)}, u32[]{:S(2)}, u32[]{:S(2)}) collective-permute-start(bf16[256,512]{1,0:T(8,128)(2,1)S(1)} %collective-permute-done.4.rest_3_), channel_id=1, source_target_pairs={{0,4},{4,8},{8,12},{12,13},{13,9},{9,5},{5,1},{1,0},{2,6},{6,10},{... | collective-permute-start | bytes 786440 | tf_op jit(solution)/shard_map/ppermute | solution.py:498
  29.3 12.6 %collective-permute-start.5 = (bf16[256,512]{1,0:T(8,128)(2,1)S(1)}, bf16[256,512]{1,0:T(8,128)(2,1)S(1)}, u32[]{:S(2)}, u32[]{:S(2)}) collective-permute-start(bf16[256,512]{1,0:T(8,128)(2,1)S(1)} %collective-permute-done.4.rest_3_), channel_id=1, source_target_pairs={{0,1},{1,0},{2,3},{3,2},{4,5},{5,4},{6,7},{7,6},{8,9},{9,8},{10,11... | collective-permute-start | bytes 786440 | tf_op jit(solution)/shard_map/ppermute | solution.py:485
  34.8 12.1 %collective-permute-start.7 = (bf16[256,512]{1,0:T(8,128)(2,1)S(1)}, bf16[256,512]{1,0:T(8,128)(2,1)S(1)}, u32[]{:S(2)}, u32[]{:S(2)}) collective-permute-start(bf16[256,512]{1,0:T(8,128)(2,1)S(1)} %collective-permute-done.6.rest_4_), channel_id=1, source_target_pairs={{0,1},{1,0},{2,3},{3,2},{4,5},{5,4},{6,7},{7,6},{8,9},{9,8},{10,11... | collective-permute-start | bytes 786440 | tf_op jit(solution)/shard_map/ppermute | solution.py:485
  36.9 5.1 %collective-permute-start.3 = (bf16[256,256]{1,0:T(8,128)(2,1)S(1)}, bf16[256,256]{1,0:T(8,128)(2,1)S(1)}, u32[]{:S(2)}, u32[]{:S(2)}) collective-permute-start(bf16[256,256]{1,0:T(8,128)(2,1)S(1)} %get-tuple-element.28.rest_0_), channel_id=1, source_target_pairs={{0,2},{2,0},{1,3},{3,1},{4,6},{6,4},{5,7},{7,5},{8,10},{10,8},{9,1... | collective-permute-start | bytes 393224 | tf_op jit(solution)/shard_map/ppermute | solution.py:490
  50.1 5.7 %collective-permute-start.8 = (bf16[4,64,384]{2,1,0:T(8,128)(2,1)S(1)}, bf16[4,64,384]{2,1,0:T(8,128)(2,1)S(1)}, u32[]{:S(2)}, u32[]{:S(2)}) collective-permute-start(bf16[4,64,384]{2,1,0:T(8,128)(2,1)S(1)} %get-tuple-element.38), channel_id=1, source_target_pairs={{0,2},{2,0},{1,3},{3,1},{4,6},{6,4},{5,7},{7,5},{8,10},{10,8},{9,1... | collective-permute-start | bytes 589832 | tf_op jit(solution)/shard_map/ppermute | solution.py:490
  51.7 6.2 %collective-permute-start.10 = (bf16[256,512]{1,0:T(8,128)(2,1)S(1)}, bf16[256,512]{1,0:T(8,128)(2,1)S(1)}, u32[]{:S(2)}, u32[]{:S(2)}) collective-permute-start(bf16[256,512]{1,0:T(8,128)(2,1)S(1)} %copy-done.6), channel_id=1, source_target_pairs={{0,1},{1,0},{2,3},{3,2},{4,5},{5,4},{6,7},{7,6},{8,9},{9,8},{10,11... | collective-permute-start | bytes 786440 | tf_op jit(solution)/shard_map/ppermute | solution.py:485
  56.1 2.8 %collective-permute-start.9 = (bf16[256,256]{1,0:T(8,128)(2,1)S(1)}, bf16[256,256]{1,0:T(8,128)(2,1)S(1)}, u32[]{:S(2)}, u32[]{:S(2)}) collective-permute-start(bf16[256,256]{1,0:T(8,128)(2,1)S(1)} %shard_map.143.own_ref), channel_id=1, source_target_pairs={{0,1},{1,0},{2,3},{3,2},{4,5},{5,4},{6,7},{7,6},{8,9},{9,8},{10,11... | collective-permute-start | bytes 393224 | tf_op jit(solution)/shard_map/ppermute | solution.py:485

commit v6 on v5

--- a/solution.py
+++ b/solution.py
@@ -13,6 +13,7 @@
 NEG = -1e30
 CHUNK = 256
 STATS = 128
+STAT_ROWS = 16
 ROWS = 16
 F32 = jnp.float32
 BF16 = jnp.bfloat16
@@ -55,12 +56,12 @@
     rows, width = full.shape
     part = rows // readers
     lane = lax.broadcasted_iota(jnp.int32, (rows, 128), 1)
-    group = STATS // heads
+    lane_head = lax.rem(lane, heads)
 
     def compact(values):
         packed = values[:rows]
         for head in range(1, heads):
-            packed = jnp.where(lane < head * group, packed, values[head * rows : (head + 1) * rows])
+            packed = jnp.where(lane_head == head, values[head * rows : (head + 1) * rows], packed)
         return packed
 
     divisor = jnp.where(row_total > 0, row_total, 1.0)
@@ -79,9 +80,10 @@
     stats = jnp.zeros((rows, STATS), F32)
     for step in range(3):
         piece = level.astype(BF16).astype(F32)
-        stats = jnp.where(lax.rem(lane, group) == step, piece, stats)
+        stats = jnp.where(lane // heads == step, piece, stats)
         level = level - piece
     stat_full[...] = stats
+    flipped = stats.T[:STAT_ROWS]
     reader = lax.axis_index("read")
     for step in range(readers):
         first = pl.multiple_of(lax.rem(reader + step, readers) * part, part)
@@ -89,8 +91,11 @@
             own_ref[segment] = full[pl.ds(first, part), :]
             own_stat_ref[segment] = stat_full[pl.ds(first, part), :].astype(BF16)
         else:
-            sends[step - 1][segment, :, :width] = full[pl.ds(first, part), :].astype(BF16)
-            sends[step - 1][segment, :, width:] = stat_full[pl.ds(first, part), :].astype(BF16)
+            sends[step - 1][segment, :part, :] = full[pl.ds(first, part), :].astype(BF16)
+            turned = pltpu.roll(flipped, lax.rem(rows - first, rows), 1)
+            sends[step - 1][segment, part:, :] = jnp.concatenate(
+                [turned, jnp.zeros((STAT_ROWS, width - rows), F32)], axis=1
+            ).astype(BF16)
 
 
 def cross_kernel(
@@ -131,9 +136,9 @@
             start = start_ref[segment, read]
             length = cov_ref[segment, read]
             live = present_ref[segment, read] > 0
-            first = (start // ROWS) * ROWS
-            last = ((start + length + ROWS - 1) // ROWS) * ROWS
-            rows = jnp.where(live, last - first, 0)
+            first = start & -ROWS
+            last = (start + length + ROWS - 1) & -ROWS
+            rows = pl.multiple_of(jnp.where(live, last - first, 0), ROWS)
             low_of[segment, read] = offset + start - first
             high_of[segment, read] = offset + jnp.where(live, start - first + length, 0)
 
@@ -169,9 +174,9 @@
         low_of[segs, read] = 0
         high_of[segs, read] = 0
 
-    max_buf[...] = jnp.full(max_buf.shape, NEG, F32)
-    total_buf[...] = jnp.zeros(total_buf.shape, F32)
-    acc[...] = jnp.zeros(acc.shape, F32)
+    max_buf[:segs] = jnp.full((segs,) + max_buf.shape[1:], NEG, F32)
+    total_buf[:segs] = jnp.zeros((segs,) + total_buf.shape[1:], F32)
+    acc[:segs] = jnp.zeros((segs,) + acc.shape[1:], F32)
     for load in loads[3:]:
         load.wait()
     normed = rms_rows(lat_ref[...].reshape(segs * lat_rows, width).astype(F32)).astype(BF16)
@@ -268,28 +273,39 @@
     lax.fori_loop(0, segs, finish, 0)
 
 
-def row_levels(stats, width):
-    group = STATS // (width // HD)
-    lane = lax.broadcasted_iota(jnp.int32, (STATS, width), 0)
-    head = lax.broadcasted_iota(jnp.int32, (STATS, width), 1) // HD
-    pick = ((lane // group == head) & (lax.rem(lane, group) < 3)).astype(F32).astype(BF16)
-    return mm(stats, pick)
+def pick_heads(rows, width):
+    heads = width // HD
+    place = lax.broadcasted_iota(jnp.int32, (rows, width), 0)
+    head = lax.broadcasted_iota(jnp.int32, (rows, width), 1) // HD
+    return ((lax.rem(place, heads) == head) & (place < 3 * heads)).astype(F32).astype(BF16)
 
 
 def own_kernel(own_ref, stat_ref, kept_ref, level_ref):
     kept_ref[...] = own_ref[...]
-    level_ref[...] = row_levels(stat_ref[...], own_ref.shape[1])
+    level_ref[...] = mm(stat_ref[...], pick_heads(STATS, own_ref.shape[1]))
 
 
 def combine_kernel(own_ref, level_ref, *rest):
     received, out_ref = rest[:-1], rest[-1]
     width = own_ref.shape[1]
-    parts = [own_ref[...]] + [ref[:, :width].astype(F32) for ref in received]
-    levels = [level_ref[...]] + [row_levels(ref[:, width:], width) for ref in received]
-    joint = functools.reduce(jnp.maximum, levels)
-    factors = [jnp.exp(level - joint) for level in levels]
-    mixed = sum(part * factor for part, factor in zip(parts, factors))
-    out_ref[...] = (mixed / sum(factors)).astype(BF16)
+    segs = received[0].shape[0]
+    part = own_ref.shape[0] // segs
+    pick = pick_heads(STAT_ROWS, width)
+    for segment in range(segs):
+        rows = slice(segment * part, (segment + 1) * part)
+        parts, levels = [own_ref[rows, :]], [level_ref[rows, :]]
+        for ref in received:
+            parts.append(ref[segment, :part, :].astype(F32))
+            stats = ref[segment, part:, :STATS]
+            levels.append(
+                lax.dot_general(
+                    stats, pick, (((0,), (0,)), ((), ())), preferred_element_type=F32
+                )[:part]
+            )
+        joint = functools.reduce(jnp.maximum, levels)
+        factors = [jnp.exp(level - joint) for level in levels]
+        mixed = sum(value * factor for value, factor in zip(parts, factors))
+        out_ref[rows, :] = (mixed / sum(factors)).astype(BF16)
 
 
 def hidden_kernel(
@@ -328,12 +344,9 @@
         chosen = inside & (flag > 0)
         source = (slot_of[block_step] * segs + inner) * part
 
-        @pl.when(chosen)
-        def _(live=live, source=source):
-            place = pl.ds(pl.multiple_of(live * part, part), part)
-            for whole, packed in zip(sources, targets):
-                packed[place, :] = whole[source : source + part, :]
-
+        place = pl.ds(pl.multiple_of(live * part, part), part)
+        for whole, packed in zip(sources, targets):
+            packed[place, :] = whole[source : source + part, :]
         live = live + chosen.astype(jnp.int32)
     return live
 
@@ -413,7 +426,7 @@
     heads = local // HD
     part = own_ref.shape[1]
     core = lax.axis_index("head")
-    many = key_buf.shape[0]
+    many = key_buf.shape[1]
 
     key_buf[...] = jnp.zeros(key_buf.shape, BF16)
     value_buf[...] = jnp.zeros(value_buf.shape, BF16)
@@ -422,28 +435,35 @@
         slots += [2 * index + core, 2 * index + 1 - core]
         slot_of[-step], slot_of[step] = 2 * index, 2 * index + 1
     project_blocks(blocks, slots, wk_ref, wv_ref, key_all, value_all)
-
-    for segment in range(segs):
-        live = collect(
+    counts = [
+        collect(
             segment, segs, part, slot_of, offsets, pattern_ref,
-            (key_all, value_all), (key_buf, value_buf),
-        )
+            (key_all, value_all), (key_buf.at[segment], value_buf.at[segment]),
+        )
+        for segment in range(segs)
+    ]
+
+    for segment in range(segs):
         place = lax.broadcasted_iota(jnp.int32, (1, many), 1)
-        scores = nt_dot(spread[segment], key_buf[...])
-        scores = jnp.where(place < live * part, scores, NEG)
+        scores = nt_dot(spread[segment], key_buf[segment])
+        scores = jnp.where(place < counts[segment] * part, scores, NEG)
         before = max_in[segment]
         top = jnp.max(tile_fold(scores, jnp.maximum), axis=1, keepdims=True)
-        max_buf[...] = jnp.maximum(before, jnp.broadcast_to(top, before.shape))
-        factor = jnp.exp(before - max_buf[...])
-        weights = jnp.exp(scores - jnp.tile(max_buf[...], (1, many // 128)))
-        total_buf[...] = total_in[segment] * factor + tile_fold(weights, jnp.add)
-        acc[...] = acc_in[segment] * jnp.tile(factor, (1, local // 128)) + mm(
-            weights.astype(BF16), value_buf[...]
-        )
-        row_total = jnp.sum(total_buf[...], axis=1, keepdims=True)
+        peak = jnp.maximum(before, jnp.broadcast_to(top, before.shape))
+        max_buf[segment] = peak
+        factor = jnp.exp(before - peak)
+        weights = jnp.exp(scores - jnp.tile(peak, (1, many // 128)))
+        row_total = jnp.sum(
+            total_in[segment] * factor + tile_fold(weights, jnp.add), axis=1, keepdims=True
+        )
+        total_buf[segment] = jnp.broadcast_to(row_total, before.shape)
+        acc[segment] = acc_in[segment] * jnp.tile(factor, (1, local // 128)) + mm(
+            weights.astype(BF16), value_buf[segment]
+        )
+    for segment in range(segs):
         emit(
-            segment, max_buf[...], jnp.broadcast_to(row_total, total_buf.shape), acc, heads, full,
-            stat_full, own_ref, own_stat_ref, sends,
+            segment, max_buf[segment], total_buf[segment], acc.at[segment], heads,
+            full.at[segment], stat_full.at[segment], own_ref, own_stat_ref, sends,
         )
 
 
@@ -526,7 +546,7 @@
     self_out_other = swap_cores(self_out)
 
     part_outputs = [((segs, part, local), F32), ((segs, part, STATS), BF16)] + [
-        ((segs, part, local + STATS), BF16)
+        ((segs, part + STAT_ROWS, local), BF16)
     ] * (readers - 1)
     work = [pltpu.VMEM((lat_rows, local), F32), pltpu.VMEM((lat_rows, STATS), F32)]
     most = reads * length
@@ -578,7 +598,7 @@
         )
         return call(
             combine_kernel,
-            [kept, level] + [value.reshape(size, local + STATS) for value in received],
+            [kept, level] + received,
             [((size, local), BF16)],
             estimate=cost(8 * size * STATS * local, 8 * size * local),
         )[0]
@@ -641,13 +661,14 @@
         scratch=[
             pltpu.VMEM((len(far_blocks) * size, local), BF16),
             pltpu.VMEM((len(far_blocks) * size, local), BF16),
-            pltpu.VMEM((far_keys, local), BF16),
-            pltpu.VMEM((far_keys, local), BF16),
-            pltpu.VMEM((spread_rows, 128), F32),
-            pltpu.VMEM((spread_rows, 128), F32),
-            pltpu.VMEM((spread_rows, local), F32),
-        ]
-        + work,
+            pltpu.VMEM((segs, far_keys, local), BF16),
+            pltpu.VMEM((segs, far_keys, local), BF16),
+            pltpu.VMEM((segs, spread_rows, 128), F32),
+            pltpu.VMEM((segs, spread_rows, 128), F32),
+            pltpu.VMEM((segs, spread_rows, local), F32),
+            pltpu.VMEM((segs, lat_rows, local), F32),
+            pltpu.VMEM((segs, lat_rows, STATS), F32),
+        ],
         estimate=cost(
             4 * segs * far_keys * local * spread_rows, 8 * segs * spread_rows * local
         ),

time: 60.8 us -> 58.4 us (0.961)
  waiting for transfers between devices: 19.9 us -> 18.5 us
  Pallas kernels: 21 us -> 20.1 us
    ppermute x3, waiting for transfers between devices: 8.29 us -> 6.89 us  [to_reader(): lax.ppermute(value, 'read', [(i, (i + step) % readers) for i in range(rea...]
    pallas_call x9, Pallas kernels: 21 us -> 20.1 us  [call(): pl.pallas_call(kernel, out_shape=[jax.ShapeDtypeStruct(shape, kind) for s...]
where the time goes in v6:
time: 58.4 us; the launch traced here: 57.3 us
  Pallas kernels  20.1 us (34%)
  waiting for transfers between devices  18.5 us (32%)
  starting transfers between devices  16.9 us (29%)
  local copies, waits for them, and re-layouts  1.82 us (3%)
    pallas_call x9, Pallas kernels, call(): pl.pallas_call(kernel, out_shape=[jax.ShapeDtypeStruct(shape, kind) for s...  20.1 us
    ppermute x2, waiting for transfers between devices, both_ways(): return lax.ppermute(value, ('pos', 'head'), moves)  9.58 us
    ppermute x6, starting transfers between devices, swap_cores(): return lax.ppermute(value, 'head', [(0, 1), (1, 0)])  8.5 us
    ppermute x3, starting transfers between devices, to_reader(): lax.ppermute(value, 'read', [(i, (i + step) % readers) for i in range(rea...  8.12 us
    ppermute x3, waiting for transfers between devices, to_reader(): lax.ppermute(value, 'read', [(i, (i + step) % readers) for i in range(rea...  6.89 us
    ppermute x6, waiting for transfers between devices, swap_cores(): return lax.ppermute(value, 'head', [(0, 1), (1, 0)])  1.98 us
    unnamed x18, local copies, waits for them, and re-layouts  1.82 us
  transfers between devices with their start and end apart: 11, of which 7 were waited for; matrix products, arithmetic and copies ran while one was open for 0% of the time, Pallas kernels for 10%

profile of v6, /device:TPU:9, one launch (start us, length us, event | category | flops | bytes accessed | tf_op | source)
XLA Modules:
  0.0 57.3 jit_solution(423343161435388599)
XLA Ops:
  0.0 10.6 %shard_map.136 = (f32[4,64,256]{2,1,0:T(8,128)}, bf16[4,64,128]{2,1,0:T(8,128)(2,1)}, bf16[4,80,256]{2,1,0:T(8,128)(2,1)}) custom-call(s32[4,4]{1,0:T(4,128)} %start_hbm.1, s32[4,4]{1,0:T(4,128)} %cov_hbm.1, s32[4,4]{1,0:T(4,128)} %present_hbm.1, bf16[4,128,512]{2,1,0:T(8,128)(2,1)} %lat_ref.1, bf16[4,4,512,512]{3,2,1,0:T(8,128)(2,1)} %tok_ref.1, ...), custom_call_target="tpu_custom_call" | custom-call | flops 8589934592 | bytes 8388608 | tf_op jit(solution)/shard_map/pallas_call | solution.py:493
  10.7 5.2 %collective-permute-start = (bf16[4,80,256]{2,1,0:T(8,128)(2,1)}, bf16[4,80,256]{2,1,0:T(8,128)(2,1)S(1)}, u32[]{:S(2)}, u32[]{:S(2)}) collective-permute-start(bf16[4,80,256]{2,1,0:T(8,128)(2,1)} %get-tuple-element.26), channel_id=1, source_target_pairs={{0,2},{2,0},{1,3},{3,1},{4,6},{6,4},{5,7},{7,5},{8,10},{10,8},{9,1... | collective-permute-start | bytes 491528 | tf_op jit(solution)/shard_map/ppermute | solution.py:510
  15.9 1.0 %collective-permute-start.2 = (bf16[256,512]{1,0:T(8,128)(2,1)S(1)}, bf16[256,512]{1,0:T(8,128)(2,1)S(1)}, u32[]{:S(2)}, u32[]{:S(2)}) collective-permute-start(bf16[256,512]{1,0:T(8,128)(2,1)S(1)} %copy-done.4), channel_id=1, source_target_pairs={{0,1},{1,0},{2,3},{3,2},{4,5},{5,4},{6,7},{7,6},{8,9},{9,8},{10,11... | collective-permute-start | bytes 786440 | tf_op jit(solution)/shard_map/ppermute | solution.py:505
  16.8 0.9 %copy-done.3 = f32[4,64,256]{2,1,0:T(8,128)S(1)} copy-done((f32[4,64,256]{2,1,0:T(8,128)S(1)}, f32[4,64,256]{2,1,0:T(8,128)}, u32[]{:S(2)}) %copy-start.3) | copy-done | bytes 262168
  17.8 0.8 %copy-done.7 = bf16[4,64,128]{2,1,0:T(8,128)(2,1)S(1)} copy-done((bf16[4,64,128]{2,1,0:T(8,128)(2,1)S(1)}, bf16[4,64,128]{2,1,0:T(8,128)(2,1)}, u32[]{:S(2)}) %copy-start.7) | copy-done | bytes 65560
  18.8 1.2 %collective-permute-done.rest_0_ = bf16[4,80,256]{2,1,0:T(8,128)(2,1)S(1)} collective-permute-done((bf16[4,80,256]{2,1,0:T(8,128)(2,1)}, bf16[4,80,256]{2,1,0:T(8,128)(2,1)S(1)}, u32[]{:S(2)}, u32[]{:S(2)}) %collective-permute-start) | collective-permute-done | bytes 163872 | tf_op jit(solution)/shard_map/ppermute | solution.py:510
  20.3 1.3 %collective-permute-start.1 = (bf16[256,256]{1,0:T(8,128)(2,1)S(1)}, bf16[256,256]{1,0:T(8,128)(2,1)S(1)}, u32[]{:S(2)}, u32[]{:S(2)}) collective-permute-start(bf16[256,256]{1,0:T(8,128)(2,1)S(1)} %shard_map.138.own_ref), channel_id=1, source_target_pairs={{0,1},{1,0},{2,3},{3,2},{4,5},{5,4},{6,7},{7,6},{8,9},{9,8},{10,11... | collective-permute-start | bytes 393224 | tf_op jit(solution)/shard_map/ppermute | solution.py:505
  21.6 1.0 %collective-permute-done.1.other_ref = bf16[256,256]{1,0:T(8,128)(2,1)S(1)} collective-permute-done((bf16[256,256]{1,0:T(8,128)(2,1)S(1)}, bf16[256,256]{1,0:T(8,128)(2,1)S(1)}, u32[]{:S(2)}, u32[]{:S(2)}) %collective-permute-start.1) | collective-permute-done | bytes 131104 | tf_op jit(solution)/shard_map/ppermute | solution.py:505
  22.6 0.6 %shard_map.139 = (f32[256,512]{1,0:T(8,128)S(1)}, bf16[256,512]{1,0:T(8,128)(2,1)S(1)}, bf16[256,256]{1,0:T(8,128)(2,1)S(1)}) custom-call(bf16[4,128,512]{2,1,0:T(8,128)(2,1)S(1)} %copy-done, bf16[256,256]{1,0:T(8,128)(2,1)S(1)} %shard_map.138.own_ref, bf16[256,256]{1,0:T(8,128)(2,1)S(1)} %collective-permute-done.1.other_ref, ...), custom_call_target="tpu_custom_call" | custom-call | flops 201326592 | bytes 1048576 | tf_op jit(solution)/shard_map/pallas_call | solution.py:493
  23.5 5.3 %collective-permute-done.4.rest_3_ = bf16[256,512]{1,0:T(8,128)(2,1)S(1)} collective-permute-done((bf16[256,512]{1,0:T(8,128)(2,1)S(1)}, bf16[256,512]{1,0:T(8,128)(2,1)S(1)}, u32[]{:S(2)}, u32[]{:S(2)}) %collective-permute-start.4) | collective-permute-done | bytes 262176 | tf_op jit(solution)/shard_map/ppermute | solution.py:518
  28.8 1.2 %collective-permute-start.5 = (bf16[256,512]{1,0:T(8,128)(2,1)S(1)}, bf16[256,512]{1,0:T(8,128)(2,1)S(1)}, u32[]{:S(2)}, u32[]{:S(2)}) collective-permute-start(bf16[256,512]{1,0:T(8,128)(2,1)S(1)} %collective-permute-done.4.rest_3_), channel_id=1, source_target_pairs={{0,1},{1,0},{2,3},{3,2},{4,5},{5,4},{6,7},{7,6},{8,9},{9,8},{10,11... | collective-permute-start | bytes 786440 | tf_op jit(solution)/shard_map/ppermute | solution.py:505
  30.0 4.3 %collective-permute-done.6.rest_4_ = bf16[256,512]{1,0:T(8,128)(2,1)S(1)} collective-permute-done((bf16[256,512]{1,0:T(8,128)(2,1)S(1)}, bf16[256,512]{1,0:T(8,128)(2,1)S(1)}, u32[]{:S(2)}, u32[]{:S(2)}) %collective-permute-start.6) | collective-permute-done | bytes 262176 | tf_op jit(solution)/shard_map/ppermute | solution.py:518
  34.3 2.1 %collective-permute-start.7 = (bf16[256,512]{1,0:T(8,128)(2,1)S(1)}, bf16[256,512]{1,0:T(8,128)(2,1)S(1)}, u32[]{:S(2)}, u32[]{:S(2)}) collective-permute-start(bf16[256,512]{1,0:T(8,128)(2,1)S(1)} %collective-permute-done.6.rest_4_), channel_id=1, source_target_pairs={{0,1},{1,0},{2,3},{3,2},{4,5},{5,4},{6,7},{7,6},{8,9},{9,8},{10,11... | collective-permute-start | bytes 786440 | tf_op jit(solution)/shard_map/ppermute | solution.py:505
  36.4 1.5 %collective-permute-start.3 = (bf16[256,256]{1,0:T(8,128)(2,1)S(1)}, bf16[256,256]{1,0:T(8,128)(2,1)S(1)}, u32[]{:S(2)}, u32[]{:S(2)}) collective-permute-start(bf16[256,256]{1,0:T(8,128)(2,1)S(1)} %get-tuple-element.28.rest_0_), channel_id=1, source_target_pairs={{0,2},{2,0},{1,3},{3,1},{4,6},{6,4},{5,7},{7,5},{8,10},{10,8},{9,1... | collective-permute-start | bytes 393224 | tf_op jit(solution)/shard_map/ppermute | solution.py:510
  37.8 3.6 %collective-permute-done.3.rest_1_ = bf16[256,256]{1,0:T(8,128)(2,1)S(1)} collective-permute-done((bf16[256,256]{1,0:T(8,128)(2,1)S(1)}, bf16[256,256]{1,0:T(8,128)(2,1)S(1)}, u32[]{:S(2)}, u32[]{:S(2)}) %collective-permute-start.3) | collective-permute-done | bytes 131104 | tf_op jit(solution)/shard_map/ppermute | solution.py:510
  41.4 4.7 %shard_map.140 = (bf16[4,512,256]{2,1,0:T(8,128)(2,1)S(1)}, f32[4,512,128]{2,1,0:T(8,128)S(1)}, f32[4,512,128]{2,1,0:T(8,128)S(1)}, f32[4,512,256]{2,1,0:T(8,128)S(1)}) custom-call(s32[4,16]{1,0:T(4,128)S(1)} %copy-done.8, bf16[512,256]{1,0:T(8,128)(2,1)S(1)} %copy-done.1, bf16[512,256]{1,0:T(8,128)(2,1)S(1)} %copy-done.2, ...), custom_call_target="tpu_custom_call" | custom-call | flops 1073741824 | bytes 4194304 | tf_op jit(solution)/shard_map/pallas_call | solution.py:493
  46.2 2.3 %shard_map.141 = (f32[4,64,256]{2,1,0:T(8,128)S(1)}, bf16[4,64,128]{2,1,0:T(8,128)(2,1)S(1)}, bf16[4,80,256]{2,1,0:T(8,128)(2,1)S(1)}) custom-call(s32[4,16]{1,0:T(4,128)S(1)} %copy-done.8, bf16[512,256]{1,0:T(8,128)(2,1)S(1)} %copy-done.1, bf16[512,256]{1,0:T(8,128)(2,1)S(1)} %copy-done.2, bf16[4,512,256]{2,1,0:T(8,128)(2,1)S(1)} %get-tuple-element.30.rest_0_, ...), custom_call_target="tpu_custom_call" | custom-call | flops 268435456 | bytes 4194304 | tf_op jit(solution)/shard_map/pallas_call | solution.py:493
  48.5 1.5 %collective-permute-start.8 = (bf16[4,80,256]{2,1,0:T(8,128)(2,1)S(1)}, bf16[4,80,256]{2,1,0:T(8,128)(2,1)S(1)}, u32[]{:S(2)}, u32[]{:S(2)}) collective-permute-start(bf16[4,80,256]{2,1,0:T(8,128)(2,1)S(1)} %get-tuple-element.38), channel_id=1, source_target_pairs={{0,2},{2,0},{1,3},{3,1},{4,6},{6,4},{5,7},{7,5},{8,10},{10,8},{9,1... | collective-permute-start | bytes 491528 | tf_op jit(solution)/shard_map/ppermute | solution.py:510
  49.9 1.1 %collective-permute-start.10 = (bf16[256,512]{1,0:T(8,128)(2,1)S(1)}, bf16[256,512]{1,0:T(8,128)(2,1)S(1)}, u32[]{:S(2)}, u32[]{:S(2)}) collective-permute-start(bf16[256,512]{1,0:T(8,128)(2,1)S(1)} %copy-done.6), channel_id=1, source_target_pairs={{0,1},{1,0},{2,3},{3,2},{4,5},{5,4},{6,7},{7,6},{8,9},{9,8},{10,11... | collective-permute-start | bytes 786440 | tf_op jit(solution)/shard_map/ppermute | solution.py:505
  51.3 2.1 %collective-permute-done.8.rest_0_ = bf16[4,80,256]{2,1,0:T(8,128)(2,1)S(1)} collective-permute-done((bf16[4,80,256]{2,1,0:T(8,128)(2,1)S(1)}, bf16[4,80,256]{2,1,0:T(8,128)(2,1)S(1)}, u32[]{:S(2)}, u32[]{:S(2)}) %collective-permute-start.8) | collective-permute-done | bytes 163872 | tf_op jit(solution)/shard_map/ppermute | solution.py:510
  53.4 0.3 shard_map.143.own_ref
  53.7 1.8 %collective-permute-start.9 = (bf16[256,256]{1,0:T(8,128)(2,1)S(1)}, bf16[256,256]{1,0:T(8,128)(2,1)S(1)}, u32[]{:S(2)}, u32[]{:S(2)}) collective-permute-start(bf16[256,256]{1,0:T(8,128)(2,1)S(1)} %shard_map.143.own_ref), channel_id=1, source_target_pairs={{0,1},{1,0},{2,3},{3,2},{4,5},{5,4},{6,7},{7,6},{8,9},{9,8},{10,11... | collective-permute-start | bytes 393224 | tf_op jit(solution)/shard_map/ppermute | solution.py:505
  55.5 1.0 %collective-permute-done.9.other_ref = bf16[256,256]{1,0:T(8,128)(2,1)S(1)} collective-permute-done((bf16[256,256]{1,0:T(8,128)(2,1)S(1)}, bf16[256,256]{1,0:T(8,128)(2,1)S(1)}, u32[]{:S(2)}, u32[]{:S(2)}) %collective-permute-start.9) | collective-permute-done | bytes 131104 | tf_op jit(solution)/shard_map/ppermute | solution.py:505
  56.5 0.9 %shard_map.144 = bf16[4,64,256]{2,1,0:T(8,128)(2,1)} custom-call(f32[256,512]{1,0:T(8,128)S(1)} %get-tuple-element.27.hid_ref, bf16[256,256]{1,0:T(8,128)(2,1)S(1)} %shard_map.143.own_ref, bf16[256,256]{1,0:T(8,128)(2,1)S(1)} %collective-permute-done.9.other_ref, bf16[256,512]{1,0:T(8,128)(2,1)S(1)} %copy-done.6, ...), custom_call_target="tpu_custom_call" | custom-call | flops 67108864 | bytes 1048576 | tf_op jit(solution)/shard_map/pallas_call | solution.py:493
  (25 shorter events, 0.9 us)
Async XLA Ops:
  0.0 22.6 %copy-start = (bf16[4,128,512]{2,1,0:T(8,128)(2,1)S(1)}, bf16[4,128,512]{2,1,0:T(8,128)(2,1)}, u32[]{:S(2)}) copy-start(bf16[4,128,512]{2,1,0:T(8,128)(2,1)} %lat_ref.1) | copy-start | bytes 1572868
  0.0 15.9 %copy-start.4 = (bf16[256,512]{1,0:T(8,128)(2,1)S(1)}, bf16[256,512]{1,0:T(8,128)(2,1)}, u32[]{:S(2)}) copy-start(bf16[256,512]{1,0:T(8,128)(2,1)} %wo_ref.2) | copy-start | bytes 786436
  0.0 22.6 %copy-start.5 = (bf16[512,256]{1,0:T(8,128)(2,1)S(1)}, bf16[512,256]{1,0:T(8,128)(2,1)}, u32[]{:S(2)}) copy-start(bf16[512,256]{1,0:T(8,128)(2,1)} %wq_ref.1) | copy-start | bytes 786436
  0.0 41.4 %copy-start.8 = (s32[4,16]{1,0:T(4,128)S(1)}, s32[4,16]{1,0:T(4,128)}, u32[]{:S(2)}) copy-start(s32[4,16]{1,0:T(4,128)} %pattern_ref.3) | copy-start | bytes 772
  0.0 41.4 %copy-start.1 = (bf16[512,256]{1,0:T(8,128)(2,1)S(1)}, bf16[512,256]{1,0:T(8,128)(2,1)}, u32[]{:S(2)}) copy-start(bf16[512,256]{1,0:T(8,128)(2,1)} %wk_ref.3) | copy-start | bytes 786436
  0.0 41.4 %copy-start.2 = (bf16[512,256]{1,0:T(8,128)(2,1)S(1)}, bf16[512,256]{1,0:T(8,128)(2,1)}, u32[]{:S(2)}) copy-start(bf16[512,256]{1,0:T(8,128)(2,1)} %wv_ref.3) | copy-start | bytes 786436
  0.0 49.9 %copy-start.6 = (bf16[256,512]{1,0:T(8,128)(2,1)S(1)}, bf16[256,512]{1,0:T(8,128)(2,1)}, u32[]{:S(2)}) copy-start(bf16[256,512]{1,0:T(8,128)(2,1)} %wo_ref.3) | copy-start | bytes 786436
  10.7 9.3 %collective-permute-start = (bf16[4,80,256]{2,1,0:T(8,128)(2,1)}, bf16[4,80,256]{2,1,0:T(8,128)(2,1)S(1)}, u32[]{:S(2)}, u32[]{:S(2)}) collective-permute-start(bf16[4,80,256]{2,1,0:T(8,128)(2,1)} %get-tuple-element.26), channel_id=1, source_target_pairs={{0,2},{2,0},{1,3},{3,1},{4,6},{6,4},{5,7},{7,5},{8,10},{10,8},{9,1... | collective-permute-start | bytes 491528 | tf_op jit(solution)/shard_map/ppermute | solution.py:510
  15.9 5.7 %collective-permute-start.2 = (bf16[256,512]{1,0:T(8,128)(2,1)S(1)}, bf16[256,512]{1,0:T(8,128)(2,1)S(1)}, u32[]{:S(2)}, u32[]{:S(2)}) collective-permute-start(bf16[256,512]{1,0:T(8,128)(2,1)S(1)} %copy-done.4), channel_id=1, source_target_pairs={{0,1},{1,0},{2,3},{3,2},{4,5},{5,4},{6,7},{7,6},{8,9},{9,8},{10,11... | collective-permute-start | bytes 786440 | tf_op jit(solution)/shard_map/ppermute | solution.py:505
  16.8 0.9 %copy-start.3 = (f32[4,64,256]{2,1,0:T(8,128)S(1)}, f32[4,64,256]{2,1,0:T(8,128)}, u32[]{:S(2)}) copy-start(f32[4,64,256]{2,1,0:T(8,128)} %get-tuple-element.22) | copy-start | bytes 786436
  17.8 0.8 %copy-start.7 = (bf16[4,64,128]{2,1,0:T(8,128)(2,1)S(1)}, bf16[4,64,128]{2,1,0:T(8,128)(2,1)}, u32[]{:S(2)}) copy-start(bf16[4,64,128]{2,1,0:T(8,128)(2,1)} %get-tuple-element.23) | copy-start | bytes 196612
  20.3 2.3 %collective-permute-start.1 = (bf16[256,256]{1,0:T(8,128)(2,1)S(1)}, bf16[256,256]{1,0:T(8,128)(2,1)S(1)}, u32[]{:S(2)}, u32[]{:S(2)}) collective-permute-start(bf16[256,256]{1,0:T(8,128)(2,1)S(1)} %shard_map.138.own_ref), channel_id=1, source_target_pairs={{0,1},{1,0},{2,3},{3,2},{4,5},{5,4},{6,7},{7,6},{8,9},{9,8},{10,11... | collective-permute-start | bytes 393224 | tf_op jit(solution)/shard_map/ppermute | solution.py:505
  23.2 5.5 %collective-permute-start.4 = (bf16[256,512]{1,0:T(8,128)(2,1)S(1)}, bf16[256,512]{1,0:T(8,128)(2,1)S(1)}, u32[]{:S(2)}, u32[]{:S(2)}) collective-permute-start(bf16[256,512]{1,0:T(8,128)(2,1)S(1)} %get-tuple-element.29.rest_2_), channel_id=1, source_target_pairs={{0,4},{4,8},{8,12},{12,13},{13,9},{9,5},{5,1},{1,0},{2,6},{6,10},{... | collective-permute-start | bytes 786440 | tf_op jit(solution)/shard_map/ppermute | solution.py:518
  28.8 5.5 %collective-permute-start.6 = (bf16[256,512]{1,0:T(8,128)(2,1)S(1)}, bf16[256,512]{1,0:T(8,128)(2,1)S(1)}, u32[]{:S(2)}, u32[]{:S(2)}) collective-permute-start(bf16[256,512]{1,0:T(8,128)(2,1)S(1)} %collective-permute-done.4.rest_3_), channel_id=1, source_target_pairs={{0,4},{4,8},{8,12},{12,13},{13,9},{9,5},{5,1},{1,0},{2,6},{6,10},{... | collective-permute-start | bytes 786440 | tf_op jit(solution)/shard_map/ppermute | solution.py:518
  28.8 12.6 %collective-permute-start.5 = (bf16[256,512]{1,0:T(8,128)(2,1)S(1)}, bf16[256,512]{1,0:T(8,128)(2,1)S(1)}, u32[]{:S(2)}, u32[]{:S(2)}) collective-permute-start(bf16[256,512]{1,0:T(8,128)(2,1)S(1)} %collective-permute-done.4.rest_3_), channel_id=1, source_target_pairs={{0,1},{1,0},{2,3},{3,2},{4,5},{5,4},{6,7},{7,6},{8,9},{9,8},{10,11... | collective-permute-start | bytes 786440 | tf_op jit(solution)/shard_map/ppermute | solution.py:505
  34.3 11.9 %collective-permute-start.7 = (bf16[256,512]{1,0:T(8,128)(2,1)S(1)}, bf16[256,512]{1,0:T(8,128)(2,1)S(1)}, u32[]{:S(2)}, u32[]{:S(2)}) collective-permute-start(bf16[256,512]{1,0:T(8,128)(2,1)S(1)} %collective-permute-done.6.rest_4_), channel_id=1, source_target_pairs={{0,1},{1,0},{2,3},{3,2},{4,5},{5,4},{6,7},{7,6},{8,9},{9,8},{10,11... | collective-permute-start | bytes 786440 | tf_op jit(solution)/shard_map/ppermute | solution.py:505
  36.4 5.1 %collective-permute-start.3 = (bf16[256,256]{1,0:T(8,128)(2,1)S(1)}, bf16[256,256]{1,0:T(8,128)(2,1)S(1)}, u32[]{:S(2)}, u32[]{:S(2)}) collective-permute-start(bf16[256,256]{1,0:T(8,128)(2,1)S(1)} %get-tuple-element.28.rest_0_), channel_id=1, source_target_pairs={{0,2},{2,0},{1,3},{3,1},{4,6},{6,4},{5,7},{7,5},{8,10},{10,8},{9,1... | collective-permute-start | bytes 393224 | tf_op jit(solution)/shard_map/ppermute | solution.py:510
  48.5 4.9 %collective-permute-start.8 = (bf16[4,80,256]{2,1,0:T(8,128)(2,1)S(1)}, bf16[4,80,256]{2,1,0:T(8,128)(2,1)S(1)}, u32[]{:S(2)}, u32[]{:S(2)}) collective-permute-start(bf16[4,80,256]{2,1,0:T(8,128)(2,1)S(1)} %get-tuple-element.38), channel_id=1, source_target_pairs={{0,2},{2,0},{1,3},{3,1},{4,6},{6,4},{5,7},{7,5},{8,10},{10,8},{9,1... | collective-permute-start | bytes 491528 | tf_op jit(solution)/shard_map/ppermute | solution.py:510
  49.9 5.5 %collective-permute-start.10 = (bf16[256,512]{1,0:T(8,128)(2,1)S(1)}, bf16[256,512]{1,0:T(8,128)(2,1)S(1)}, u32[]{:S(2)}, u32[]{:S(2)}) collective-permute-start(bf16[256,512]{1,0:T(8,128)(2,1)S(1)} %copy-done.6), channel_id=1, source_target_pairs={{0,1},{1,0},{2,3},{3,2},{4,5},{5,4},{6,7},{7,6},{8,9},{9,8},{10,11... | collective-permute-start | bytes 786440 | tf_op jit(solution)/shard_map/ppermute | solution.py:505
  53.7 2.8 %collective-permute-start.9 = (bf16[256,256]{1,0:T(8,128)(2,1)S(1)}, bf16[256,256]{1,0:T(8,128)(2,1)S(1)}, u32[]{:S(2)}, u32[]{:S(2)}) collective-permute-start(bf16[256,256]{1,0:T(8,128)(2,1)S(1)} %shard_map.143.own_ref), channel_id=1, source_target_pairs={{0,1},{1,0},{2,3},{3,2},{4,5},{5,4},{6,7},{7,6},{8,9},{9,8},{10,11... | collective-permute-start | bytes 393224 | tf_op jit(solution)/shard_map/ppermute | solution.py:505

commit v7 on v6

--- a/solution.py
+++ b/solution.py
@@ -261,16 +261,13 @@
 
     lax.fori_loop(0, pairs, second_pass, 0)
 
-    def finish(segment, carry):
+    for segment in range(segs):
         row_total = jnp.sum(total_buf[segment], axis=1, keepdims=True)
-        row_total = jnp.broadcast_to(row_total, total_buf.shape[1:])
         emit(
-            segment, max_buf[segment], row_total, acc.at[segment], heads, full, stat_full,
-            own_ref, own_stat_ref, sends,
-        )
-        return carry
-
-    lax.fori_loop(0, segs, finish, 0)
+            segment, max_buf[segment], jnp.broadcast_to(row_total, total_buf.shape[1:]),
+            acc.at[segment], heads, full.at[segment], stat_full.at[segment], own_ref,
+            own_stat_ref, sends,
+        )
 
 
 def pick_heads(rows, width):
@@ -355,8 +352,8 @@
     queries = rest[:readers]
     own, ahead, behind = rest[readers : readers + 3]
     spread, max_out, total_out, acc = rest[readers + 3 : readers + 7]
-    query_buf, key_all, value_all, key_buf, value_buf, score_buf = rest[readers + 7 :]
-    segs, spread_rows, local = spread.shape
+    query_buf, key_all, value_all, key_buf, value_buf = rest[readers + 7 :]
+    segs, _, local = spread.shape
     lat_rows = query_buf.shape[1]
     part = lat_rows // readers
     heads = local // HD
@@ -377,40 +374,40 @@
 
     for segment in range(segs):
         spread_queries(query_buf[segment], heads, spread.at[segment])
-        live = collect(
+    counts = [
+        collect(
             segment, segs, part, {0: 0, -1: 1, 1: 2}, offsets, pattern_ref,
-            (key_all, value_all), (key_buf, value_buf),
-        )
-        max_out[segment] = jnp.full(max_out.shape[1:], NEG, F32)
-        total_out[segment] = jnp.zeros(total_out.shape[1:], F32)
-        acc[segment] = jnp.zeros(acc.shape[1:], F32)
-
-        def first_pass(chunk, carry, segment=segment, live=live):
-            base = pl.multiple_of(chunk * CHUNK, CHUNK)
-            place = base + lax.broadcasted_iota(jnp.int32, (1, CHUNK), 1)
-            scores = nt_dot(spread[segment], key_buf[pl.ds(base, CHUNK), :])
-            scores = jnp.where(place < live * part, scores, NEG)
-            score_buf[chunk] = scores
-            max_out[segment] = jnp.maximum(max_out[segment], tile_fold(scores, jnp.maximum))
-            return carry
-
-        chunks = (live * part + CHUNK - 1) // CHUNK
-        lax.fori_loop(0, chunks, first_pass, 0)
-        row_max = jnp.max(max_out[segment], axis=1, keepdims=True)
-        max_out[segment] = jnp.broadcast_to(row_max, max_out.shape[1:])
-
-        def second_pass(chunk, carry, segment=segment):
-            value = value_buf[pl.ds(pl.multiple_of(chunk * CHUNK, CHUNK), CHUNK), :]
-            for block in range(2):
-                rows = slice(block * spread_rows // 2, (block + 1) * spread_rows // 2)
-                weights = jnp.exp(
-                    score_buf[chunk, rows] - jnp.tile(max_out[segment, rows], (1, CHUNK // 128))
-                )
-                total_out[segment, rows] += tile_fold(weights, jnp.add)
-                acc[segment, rows] += mm(weights.astype(BF16), value)
-            return carry
-
-        lax.fori_loop(0, chunks, second_pass, 0)
+            (key_all, value_all), (key_buf.at[segment], value_buf.at[segment]),
+        )
+        for segment in range(segs)
+    ]
+
+    def weigh(segment, base, before):
+        keys = slice(base, base + CHUNK)
+        place = base + lax.broadcasted_iota(jnp.int32, (1, CHUNK), 1)
+        scores = nt_dot(spread[segment], key_buf[segment, keys])
+        scores = jnp.where(place < counts[segment] * part, scores, NEG)
+        top = jnp.max(tile_fold(scores, jnp.maximum), axis=1, keepdims=True)
+        peak = jnp.broadcast_to(top, max_out.shape[1:])
+        if before is not None:
+            peak = jnp.maximum(peak, before)
+        weights = jnp.exp(scores - jnp.tile(peak, (1, CHUNK // 128)))
+        update = mm(weights.astype(BF16), value_buf[segment, keys])
+        return peak, tile_fold(weights, jnp.add), update
+
+    for segment in range(segs):
+        max_out[segment], total_out[segment], acc[segment] = weigh(segment, 0, None)
+    for segment in range(segs):
+        for base in range(CHUNK, key_buf.shape[1], CHUNK):
+
+            @pl.when(counts[segment] * part > base)
+            def _(segment=segment, base=base):
+                before = max_out[segment]
+                peak, totals, update = weigh(segment, base, before)
+                factor = jnp.exp(before - peak)
+                max_out[segment] = peak
+                total_out[segment] = total_out[segment] * factor + totals
+                acc[segment] = acc[segment] * jnp.tile(factor, (1, local // 128)) + update
 
 
 def far_kernel(readers, steps, offsets, pattern_ref, wk_ref, wv_ref, *rest):
@@ -548,7 +545,7 @@
     part_outputs = [((segs, part, local), F32), ((segs, part, STATS), BF16)] + [
         ((segs, part + STAT_ROWS, local), BF16)
     ] * (readers - 1)
-    work = [pltpu.VMEM((lat_rows, local), F32), pltpu.VMEM((lat_rows, STATS), F32)]
+    work = [pltpu.VMEM((segs, lat_rows, local), F32), pltpu.VMEM((segs, lat_rows, STATS), F32)]
     most = reads * length
     tiles = -(-most // CHUNK)
     spare = (segs * tiles + 1) // 2 * 2 + 2
@@ -644,9 +641,8 @@
             pltpu.VMEM((segs, lat_rows, local), BF16),
             pltpu.VMEM((3 * size, local), BF16),
             pltpu.VMEM((3 * size, local), BF16),
-            pltpu.VMEM((near_keys, local), BF16),
-            pltpu.VMEM((near_keys, local), BF16),
-            pltpu.VMEM((near_keys // CHUNK, spread_rows, CHUNK), F32),
+            pltpu.VMEM((segs, near_keys, local), BF16),
+            pltpu.VMEM((segs, near_keys, local), BF16),
         ],
         estimate=cost(4 * segs * near_keys * local * spread_rows, 8 * segs * spread_rows * local),
         limit=16 << 20,
@@ -666,9 +662,8 @@
             pltpu.VMEM((segs, spread_rows, 128), F32),
             pltpu.VMEM((segs, spread_rows, 128), F32),
             pltpu.VMEM((segs, spread_rows, local), F32),
-            pltpu.VMEM((segs, lat_rows, local), F32),
-            pltpu.VMEM((segs, lat_rows, STATS), F32),
-        ],
+        ]
+        + work,
         estimate=cost(
             4 * segs * far_keys * local * spread_rows, 8 * segs * spread_rows * local
         ),

time: 58.4 us -> 56.4 us (0.966)
  Pallas kernels: 20.1 us -> 18.1 us
    pallas_call x9, Pallas kernels: 20.1 us -> 18.1 us  [call(): pl.pallas_call(kernel, out_shape=[jax.ShapeDtypeStruct(shape, kind) for s...]
  transfers between devices with their start and end apart: 11 -> 11, of which waited for: 7 -> 7; matrix products, arithmetic and copies ran while one was open for 0% -> 0% of each run, Pallas kernels for 10% -> 7%
where the time goes in v7:
time: 56.4 us; the launch traced here: 55.3 us
  waiting for transfers between devices  18.4 us (33%)
  Pallas kernels  18.1 us (32%)
  starting transfers between devices  16.9 us (30%)
  local copies, waits for them, and re-layouts  1.82 us (3%)
    pallas_call x9, Pallas kernels, call(): pl.pallas_call(kernel, out_shape=[jax.ShapeDtypeStruct(shape, kind) for s...  18.1 us
    ppermute x2, waiting for transfers between devices, both_ways(): return lax.ppermute(value, ('pos', 'head'), moves)  9.58 us
    ppermute x6, starting transfers between devices, swap_cores(): return lax.ppermute(value, 'head', [(0, 1), (1, 0)])  8.51 us
    ppermute x3, starting transfers between devices, to_reader(): lax.ppermute(value, 'read', [(i, (i + step) % readers) for i in range(rea...  8.1 us
    ppermute x3, waiting for transfers between devices, to_reader(): lax.ppermute(value, 'read', [(i, (i + step) % readers) for i in range(rea...  6.89 us
    ppermute x6, waiting for transfers between devices, swap_cores(): return lax.ppermute(value, 'head', [(0, 1), (1, 0)])  1.98 us
    unnamed x18, local copies, waits for them, and re-layouts  1.82 us
  transfers between devices with their start and end apart: 11, of which 7 were waited for; matrix products, arithmetic and copies ran while one was open for 0% of the time, Pallas kernels for 7%

profile of v7, /device:TPU:9, one launch (start us, length us, event | category | flops | bytes accessed | tf_op | source)
XLA Modules:
  0.0 55.3 jit_solution(14059556840304796940)
XLA Ops:
  0.0 10.4 %shard_map.136 = (f32[4,64,256]{2,1,0:T(8,128)}, bf16[4,64,128]{2,1,0:T(8,128)(2,1)}, bf16[4,80,256]{2,1,0:T(8,128)(2,1)}) custom-call(s32[4,4]{1,0:T(4,128)} %start_hbm.1, s32[4,4]{1,0:T(4,128)} %cov_hbm.1, s32[4,4]{1,0:T(4,128)} %present_hbm.1, bf16[4,128,512]{2,1,0:T(8,128)(2,1)} %lat_ref.1, bf16[4,4,512,512]{3,2,1,0:T(8,128)(2,1)} %tok_ref.1, ...), custom_call_target="tpu_custom_call" | custom-call | flops 8589934592 | bytes 8388608 | tf_op jit(solution)/shard_map/pallas_call | solution.py:490
  10.5 5.2 %collective-permute-start = (bf16[4,80,256]{2,1,0:T(8,128)(2,1)}, bf16[4,80,256]{2,1,0:T(8,128)(2,1)S(1)}, u32[]{:S(2)}, u32[]{:S(2)}) collective-permute-start(bf16[4,80,256]{2,1,0:T(8,128)(2,1)} %get-tuple-element.26), channel_id=1, source_target_pairs={{0,2},{2,0},{1,3},{3,1},{4,6},{6,4},{5,7},{7,5},{8,10},{10,8},{9,1... | collective-permute-start | bytes 491528 | tf_op jit(solution)/shard_map/ppermute | solution.py:507
  15.7 1.0 %collective-permute-start.2 = (bf16[256,512]{1,0:T(8,128)(2,1)S(1)}, bf16[256,512]{1,0:T(8,128)(2,1)S(1)}, u32[]{:S(2)}, u32[]{:S(2)}) collective-permute-start(bf16[256,512]{1,0:T(8,128)(2,1)S(1)} %copy-done.4), channel_id=1, source_target_pairs={{0,1},{1,0},{2,3},{3,2},{4,5},{5,4},{6,7},{7,6},{8,9},{9,8},{10,11... | collective-permute-start | bytes 786440 | tf_op jit(solution)/shard_map/ppermute | solution.py:502
  16.6 0.9 %copy-done.3 = f32[4,64,256]{2,1,0:T(8,128)S(1)} copy-done((f32[4,64,256]{2,1,0:T(8,128)S(1)}, f32[4,64,256]{2,1,0:T(8,128)}, u32[]{:S(2)}) %copy-start.3) | copy-done | bytes 262168
  17.6 0.8 %copy-done.7 = bf16[4,64,128]{2,1,0:T(8,128)(2,1)S(1)} copy-done((bf16[4,64,128]{2,1,0:T(8,128)(2,1)S(1)}, bf16[4,64,128]{2,1,0:T(8,128)(2,1)}, u32[]{:S(2)}) %copy-start.7) | copy-done | bytes 65560
  18.6 1.2 %collective-permute-done.rest_0_ = bf16[4,80,256]{2,1,0:T(8,128)(2,1)S(1)} collective-permute-done((bf16[4,80,256]{2,1,0:T(8,128)(2,1)}, bf16[4,80,256]{2,1,0:T(8,128)(2,1)S(1)}, u32[]{:S(2)}, u32[]{:S(2)}) %collective-permute-start) | collective-permute-done | bytes 163872 | tf_op jit(solution)/shard_map/ppermute | solution.py:507
  19.8 0.3 shard_map.138.own_ref
  20.1 1.3 %collective-permute-start.1 = (bf16[256,256]{1,0:T(8,128)(2,1)S(1)}, bf16[256,256]{1,0:T(8,128)(2,1)S(1)}, u32[]{:S(2)}, u32[]{:S(2)}) collective-permute-start(bf16[256,256]{1,0:T(8,128)(2,1)S(1)} %shard_map.138.own_ref), channel_id=1, source_target_pairs={{0,1},{1,0},{2,3},{3,2},{4,5},{5,4},{6,7},{7,6},{8,9},{9,8},{10,11... | collective-permute-start | bytes 393224 | tf_op jit(solution)/shard_map/ppermute | solution.py:502
  21.4 1.0 %collective-permute-done.1.other_ref = bf16[256,256]{1,0:T(8,128)(2,1)S(1)} collective-permute-done((bf16[256,256]{1,0:T(8,128)(2,1)S(1)}, bf16[256,256]{1,0:T(8,128)(2,1)S(1)}, u32[]{:S(2)}, u32[]{:S(2)}) %collective-permute-start.1) | collective-permute-done | bytes 131104 | tf_op jit(solution)/shard_map/ppermute | solution.py:502
  22.4 0.6 %shard_map.139 = (f32[256,512]{1,0:T(8,128)S(1)}, bf16[256,512]{1,0:T(8,128)(2,1)S(1)}, bf16[256,256]{1,0:T(8,128)(2,1)S(1)}) custom-call(bf16[4,128,512]{2,1,0:T(8,128)(2,1)S(1)} %copy-done, bf16[256,256]{1,0:T(8,128)(2,1)S(1)} %shard_map.138.own_ref, bf16[256,256]{1,0:T(8,128)(2,1)S(1)} %collective-permute-done.1.other_ref, ...), custom_call_target="tpu_custom_call" | custom-call | flops 201326592 | bytes 1048576 | tf_op jit(solution)/shard_map/pallas_call | solution.py:490
  23.3 5.3 %collective-permute-done.4.rest_3_ = bf16[256,512]{1,0:T(8,128)(2,1)S(1)} collective-permute-done((bf16[256,512]{1,0:T(8,128)(2,1)S(1)}, bf16[256,512]{1,0:T(8,128)(2,1)S(1)}, u32[]{:S(2)}, u32[]{:S(2)}) %collective-permute-start.4) | collective-permute-done | bytes 262176 | tf_op jit(solution)/shard_map/ppermute | solution.py:515
  28.6 1.2 %collective-permute-start.5 = (bf16[256,512]{1,0:T(8,128)(2,1)S(1)}, bf16[256,512]{1,0:T(8,128)(2,1)S(1)}, u32[]{:S(2)}, u32[]{:S(2)}) collective-permute-start(bf16[256,512]{1,0:T(8,128)(2,1)S(1)} %collective-permute-done.4.rest_3_), channel_id=1, source_target_pairs={{0,1},{1,0},{2,3},{3,2},{4,5},{5,4},{6,7},{7,6},{8,9},{9,8},{10,11... | collective-permute-start | bytes 786440 | tf_op jit(solution)/shard_map/ppermute | solution.py:502
  29.8 4.3 %collective-permute-done.6.rest_4_ = bf16[256,512]{1,0:T(8,128)(2,1)S(1)} collective-permute-done((bf16[256,512]{1,0:T(8,128)(2,1)S(1)}, bf16[256,512]{1,0:T(8,128)(2,1)S(1)}, u32[]{:S(2)}, u32[]{:S(2)}) %collective-permute-start.6) | collective-permute-done | bytes 262176 | tf_op jit(solution)/shard_map/ppermute | solution.py:515
  34.1 2.1 %collective-permute-start.7 = (bf16[256,512]{1,0:T(8,128)(2,1)S(1)}, bf16[256,512]{1,0:T(8,128)(2,1)S(1)}, u32[]{:S(2)}, u32[]{:S(2)}) collective-permute-start(bf16[256,512]{1,0:T(8,128)(2,1)S(1)} %collective-permute-done.6.rest_4_), channel_id=1, source_target_pairs={{0,1},{1,0},{2,3},{3,2},{4,5},{5,4},{6,7},{7,6},{8,9},{9,8},{10,11... | collective-permute-start | bytes 786440 | tf_op jit(solution)/shard_map/ppermute | solution.py:502
  36.2 1.5 %collective-permute-start.3 = (bf16[256,256]{1,0:T(8,128)(2,1)S(1)}, bf16[256,256]{1,0:T(8,128)(2,1)S(1)}, u32[]{:S(2)}, u32[]{:S(2)}) collective-permute-start(bf16[256,256]{1,0:T(8,128)(2,1)S(1)} %get-tuple-element.28.rest_0_), channel_id=1, source_target_pairs={{0,2},{2,0},{1,3},{3,1},{4,6},{6,4},{5,7},{7,5},{8,10},{10,8},{9,1... | collective-permute-start | bytes 393224 | tf_op jit(solution)/shard_map/ppermute | solution.py:507
  37.6 3.6 %collective-permute-done.3.rest_1_ = bf16[256,256]{1,0:T(8,128)(2,1)S(1)} collective-permute-done((bf16[256,256]{1,0:T(8,128)(2,1)S(1)}, bf16[256,256]{1,0:T(8,128)(2,1)S(1)}, u32[]{:S(2)}, u32[]{:S(2)}) %collective-permute-start.3) | collective-permute-done | bytes 131104 | tf_op jit(solution)/shard_map/ppermute | solution.py:507
  41.3 2.9 %shard_map.140 = (bf16[4,512,256]{2,1,0:T(8,128)(2,1)S(1)}, f32[4,512,128]{2,1,0:T(8,128)S(1)}, f32[4,512,128]{2,1,0:T(8,128)S(1)}, f32[4,512,256]{2,1,0:T(8,128)S(1)}) custom-call(s32[4,16]{1,0:T(4,128)S(1)} %copy-done.8, bf16[512,256]{1,0:T(8,128)(2,1)S(1)} %copy-done.1, bf16[512,256]{1,0:T(8,128)(2,1)S(1)} %copy-done.2, ...), custom_call_target="tpu_custom_call" | custom-call | flops 1073741824 | bytes 4194304 | tf_op jit(solution)/shard_map/pallas_call | solution.py:490
  44.2 2.3 %shard_map.141 = (f32[4,64,256]{2,1,0:T(8,128)S(1)}, bf16[4,64,128]{2,1,0:T(8,128)(2,1)S(1)}, bf16[4,80,256]{2,1,0:T(8,128)(2,1)S(1)}) custom-call(s32[4,16]{1,0:T(4,128)S(1)} %copy-done.8, bf16[512,256]{1,0:T(8,128)(2,1)S(1)} %copy-done.1, bf16[512,256]{1,0:T(8,128)(2,1)S(1)} %copy-done.2, bf16[4,512,256]{2,1,0:T(8,128)(2,1)S(1)} %get-tuple-element.30.rest_0_, ...), custom_call_target="tpu_custom_call" | custom-call | flops 268435456 | bytes 4194304 | tf_op jit(solution)/shard_map/pallas_call | solution.py:490
  46.4 1.5 %collective-permute-start.8 = (bf16[4,80,256]{2,1,0:T(8,128)(2,1)S(1)}, bf16[4,80,256]{2,1,0:T(8,128)(2,1)S(1)}, u32[]{:S(2)}, u32[]{:S(2)}) collective-permute-start(bf16[4,80,256]{2,1,0:T(8,128)(2,1)S(1)} %get-tuple-element.38), channel_id=1, source_target_pairs={{0,2},{2,0},{1,3},{3,1},{4,6},{6,4},{5,7},{7,5},{8,10},{10,8},{9,1... | collective-permute-start | bytes 491528 | tf_op jit(solution)/shard_map/ppermute | solution.py:507
  47.9 1.2 %collective-permute-start.10 = (bf16[256,512]{1,0:T(8,128)(2,1)S(1)}, bf16[256,512]{1,0:T(8,128)(2,1)S(1)}, u32[]{:S(2)}, u32[]{:S(2)}) collective-permute-start(bf16[256,512]{1,0:T(8,128)(2,1)S(1)} %copy-done.6), channel_id=1, source_target_pairs={{0,1},{1,0},{2,3},{3,2},{4,5},{5,4},{6,7},{7,6},{8,9},{9,8},{10,11... | collective-permute-start | bytes 786440 | tf_op jit(solution)/shard_map/ppermute | solution.py:502
  49.2 2.1 %collective-permute-done.8.rest_0_ = bf16[4,80,256]{2,1,0:T(8,128)(2,1)S(1)} collective-permute-done((bf16[4,80,256]{2,1,0:T(8,128)(2,1)S(1)}, bf16[4,80,256]{2,1,0:T(8,128)(2,1)S(1)}, u32[]{:S(2)}, u32[]{:S(2)}) %collective-permute-start.8) | collective-permute-done | bytes 163872 | tf_op jit(solution)/shard_map/ppermute | solution.py:507
  51.7 1.8 %collective-permute-start.9 = (bf16[256,256]{1,0:T(8,128)(2,1)S(1)}, bf16[256,256]{1,0:T(8,128)(2,1)S(1)}, u32[]{:S(2)}, u32[]{:S(2)}) collective-permute-start(bf16[256,256]{1,0:T(8,128)(2,1)S(1)} %shard_map.143.own_ref), channel_id=1, source_target_pairs={{0,1},{1,0},{2,3},{3,2},{4,5},{5,4},{6,7},{7,6},{8,9},{9,8},{10,11... | collective-permute-start | bytes 393224 | tf_op jit(solution)/shard_map/ppermute | solution.py:502
  53.5 1.0 %collective-permute-done.9.other_ref = bf16[256,256]{1,0:T(8,128)(2,1)S(1)} collective-permute-done((bf16[256,256]{1,0:T(8,128)(2,1)S(1)}, bf16[256,256]{1,0:T(8,128)(2,1)S(1)}, u32[]{:S(2)}, u32[]{:S(2)}) %collective-permute-start.9) | collective-permute-done | bytes 131104 | tf_op jit(solution)/shard_map/ppermute | solution.py:502
  54.4 0.9 %shard_map.144 = bf16[4,64,256]{2,1,0:T(8,128)(2,1)} custom-call(f32[256,512]{1,0:T(8,128)S(1)} %get-tuple-element.27.hid_ref, bf16[256,256]{1,0:T(8,128)(2,1)S(1)} %shard_map.143.own_ref, bf16[256,256]{1,0:T(8,128)(2,1)S(1)} %collective-permute-done.9.other_ref, bf16[256,512]{1,0:T(8,128)(2,1)S(1)} %copy-done.6, ...), custom_call_target="tpu_custom_call" | custom-call | flops 67108864 | bytes 1048576 | tf_op jit(solution)/shard_map/pallas_call | solution.py:490
  (25 shorter events, 0.9 us)
Async XLA Ops:
  0.0 22.4 %copy-start = (bf16[4,128,512]{2,1,0:T(8,128)(2,1)S(1)}, bf16[4,128,512]{2,1,0:T(8,128)(2,1)}, u32[]{:S(2)}) copy-start(bf16[4,128,512]{2,1,0:T(8,128)(2,1)} %lat_ref.1) | copy-start | bytes 1572868
  0.0 15.7 %copy-start.4 = (bf16[256,512]{1,0:T(8,128)(2,1)S(1)}, bf16[256,512]{1,0:T(8,128)(2,1)}, u32[]{:S(2)}) copy-start(bf16[256,512]{1,0:T(8,128)(2,1)} %wo_ref.2) | copy-start | bytes 786436
  0.0 22.4 %copy-start.5 = (bf16[512,256]{1,0:T(8,128)(2,1)S(1)}, bf16[512,256]{1,0:T(8,128)(2,1)}, u32[]{:S(2)}) copy-start(bf16[512,256]{1,0:T(8,128)(2,1)} %wq_ref.1) | copy-start | bytes 786436
  0.0 41.2 %copy-start.8 = (s32[4,16]{1,0:T(4,128)S(1)}, s32[4,16]{1,0:T(4,128)}, u32[]{:S(2)}) copy-start(s32[4,16]{1,0:T(4,128)} %pattern_ref.3) | copy-start | bytes 772
  0.0 41.2 %copy-start.1 = (bf16[512,256]{1,0:T(8,128)(2,1)S(1)}, bf16[512,256]{1,0:T(8,128)(2,1)}, u32[]{:S(2)}) copy-start(bf16[512,256]{1,0:T(8,128)(2,1)} %wk_ref.3) | copy-start | bytes 786436
  0.0 41.2 %copy-start.2 = (bf16[512,256]{1,0:T(8,128)(2,1)S(1)}, bf16[512,256]{1,0:T(8,128)(2,1)}, u32[]{:S(2)}) copy-start(bf16[512,256]{1,0:T(8,128)(2,1)} %wv_ref.3) | copy-start | bytes 786436
  0.0 47.9 %copy-start.6 = (bf16[256,512]{1,0:T(8,128)(2,1)S(1)}, bf16[256,512]{1,0:T(8,128)(2,1)}, u32[]{:S(2)}) copy-start(bf16[256,512]{1,0:T(8,128)(2,1)} %wo_ref.3) | copy-start | bytes 786436
  10.5 9.3 %collective-permute-start = (bf16[4,80,256]{2,1,0:T(8,128)(2,1)}, bf16[4,80,256]{2,1,0:T(8,128)(2,1)S(1)}, u32[]{:S(2)}, u32[]{:S(2)}) collective-permute-start(bf16[4,80,256]{2,1,0:T(8,128)(2,1)} %get-tuple-element.26), channel_id=1, source_target_pairs={{0,2},{2,0},{1,3},{3,1},{4,6},{6,4},{5,7},{7,5},{8,10},{10,8},{9,1... | collective-permute-start | bytes 491528 | tf_op jit(solution)/shard_map/ppermute | solution.py:507
  15.7 5.7 %collective-permute-start.2 = (bf16[256,512]{1,0:T(8,128)(2,1)S(1)}, bf16[256,512]{1,0:T(8,128)(2,1)S(1)}, u32[]{:S(2)}, u32[]{:S(2)}) collective-permute-start(bf16[256,512]{1,0:T(8,128)(2,1)S(1)} %copy-done.4), channel_id=1, source_target_pairs={{0,1},{1,0},{2,3},{3,2},{4,5},{5,4},{6,7},{7,6},{8,9},{9,8},{10,11... | collective-permute-start | bytes 786440 | tf_op jit(solution)/shard_map/ppermute | solution.py:502
  16.6 0.9 %copy-start.3 = (f32[4,64,256]{2,1,0:T(8,128)S(1)}, f32[4,64,256]{2,1,0:T(8,128)}, u32[]{:S(2)}) copy-start(f32[4,64,256]{2,1,0:T(8,128)} %get-tuple-element.22) | copy-start | bytes 786436
  17.6 0.8 %copy-start.7 = (bf16[4,64,128]{2,1,0:T(8,128)(2,1)S(1)}, bf16[4,64,128]{2,1,0:T(8,128)(2,1)}, u32[]{:S(2)}) copy-start(bf16[4,64,128]{2,1,0:T(8,128)(2,1)} %get-tuple-element.23) | copy-start | bytes 196612
  20.1 2.3 %collective-permute-start.1 = (bf16[256,256]{1,0:T(8,128)(2,1)S(1)}, bf16[256,256]{1,0:T(8,128)(2,1)S(1)}, u32[]{:S(2)}, u32[]{:S(2)}) collective-permute-start(bf16[256,256]{1,0:T(8,128)(2,1)S(1)} %shard_map.138.own_ref), channel_id=1, source_target_pairs={{0,1},{1,0},{2,3},{3,2},{4,5},{5,4},{6,7},{7,6},{8,9},{9,8},{10,11... | collective-permute-start | bytes 393224 | tf_op jit(solution)/shard_map/ppermute | solution.py:502
  23.1 5.5 %collective-permute-start.4 = (bf16[256,512]{1,0:T(8,128)(2,1)S(1)}, bf16[256,512]{1,0:T(8,128)(2,1)S(1)}, u32[]{:S(2)}, u32[]{:S(2)}) collective-permute-start(bf16[256,512]{1,0:T(8,128)(2,1)S(1)} %get-tuple-element.29.rest_2_), channel_id=1, source_target_pairs={{0,4},{4,8},{8,12},{12,13},{13,9},{9,5},{5,1},{1,0},{2,6},{6,10},{... | collective-permute-start | bytes 786440 | tf_op jit(solution)/shard_map/ppermute | solution.py:515
  28.6 5.5 %collective-permute-start.6 = (bf16[256,512]{1,0:T(8,128)(2,1)S(1)}, bf16[256,512]{1,0:T(8,128)(2,1)S(1)}, u32[]{:S(2)}, u32[]{:S(2)}) collective-permute-start(bf16[256,512]{1,0:T(8,128)(2,1)S(1)} %collective-permute-done.4.rest_3_), channel_id=1, source_target_pairs={{0,4},{4,8},{8,12},{12,13},{13,9},{9,5},{5,1},{1,0},{2,6},{6,10},{... | collective-permute-start | bytes 786440 | tf_op jit(solution)/shard_map/ppermute | solution.py:515
  28.6 12.6 %collective-permute-start.5 = (bf16[256,512]{1,0:T(8,128)(2,1)S(1)}, bf16[256,512]{1,0:T(8,128)(2,1)S(1)}, u32[]{:S(2)}, u32[]{:S(2)}) collective-permute-start(bf16[256,512]{1,0:T(8,128)(2,1)S(1)} %collective-permute-done.4.rest_3_), channel_id=1, source_target_pairs={{0,1},{1,0},{2,3},{3,2},{4,5},{5,4},{6,7},{7,6},{8,9},{9,8},{10,11... | collective-permute-start | bytes 786440 | tf_op jit(solution)/shard_map/ppermute | solution.py:502
  34.1 10.0 %collective-permute-start.7 = (bf16[256,512]{1,0:T(8,128)(2,1)S(1)}, bf16[256,512]{1,0:T(8,128)(2,1)S(1)}, u32[]{:S(2)}, u32[]{:S(2)}) collective-permute-start(bf16[256,512]{1,0:T(8,128)(2,1)S(1)} %collective-permute-done.6.rest_4_), channel_id=1, source_target_pairs={{0,1},{1,0},{2,3},{3,2},{4,5},{5,4},{6,7},{7,6},{8,9},{9,8},{10,11... | collective-permute-start | bytes 786440 | tf_op jit(solution)/shard_map/ppermute | solution.py:502
  36.2 5.1 %collective-permute-start.3 = (bf16[256,256]{1,0:T(8,128)(2,1)S(1)}, bf16[256,256]{1,0:T(8,128)(2,1)S(1)}, u32[]{:S(2)}, u32[]{:S(2)}) collective-permute-start(bf16[256,256]{1,0:T(8,128)(2,1)S(1)} %get-tuple-element.28.rest_0_), channel_id=1, source_target_pairs={{0,2},{2,0},{1,3},{3,1},{4,6},{6,4},{5,7},{7,5},{8,10},{10,8},{9,1... | collective-permute-start | bytes 393224 | tf_op jit(solution)/shard_map/ppermute | solution.py:507
  46.4 4.9 %collective-permute-start.8 = (bf16[4,80,256]{2,1,0:T(8,128)(2,1)S(1)}, bf16[4,80,256]{2,1,0:T(8,128)(2,1)S(1)}, u32[]{:S(2)}, u32[]{:S(2)}) collective-permute-start(bf16[4,80,256]{2,1,0:T(8,128)(2,1)S(1)} %get-tuple-element.38), channel_id=1, source_target_pairs={{0,2},{2,0},{1,3},{3,1},{4,6},{6,4},{5,7},{7,5},{8,10},{10,8},{9,1... | collective-permute-start | bytes 491528 | tf_op jit(solution)/shard_map/ppermute | solution.py:507
  47.9 5.5 %collective-permute-start.10 = (bf16[256,512]{1,0:T(8,128)(2,1)S(1)}, bf16[256,512]{1,0:T(8,128)(2,1)S(1)}, u32[]{:S(2)}, u32[]{:S(2)}) collective-permute-start(bf16[256,512]{1,0:T(8,128)(2,1)S(1)} %copy-done.6), channel_id=1, source_target_pairs={{0,1},{1,0},{2,3},{3,2},{4,5},{5,4},{6,7},{7,6},{8,9},{9,8},{10,11... | collective-permute-start | bytes 786440 | tf_op jit(solution)/shard_map/ppermute | solution.py:502
  51.7 2.8 %collective-permute-start.9 = (bf16[256,256]{1,0:T(8,128)(2,1)S(1)}, bf16[256,256]{1,0:T(8,128)(2,1)S(1)}, u32[]{:S(2)}, u32[]{:S(2)}) collective-permute-start(bf16[256,256]{1,0:T(8,128)(2,1)S(1)} %shard_map.143.own_ref), channel_id=1, source_target_pairs={{0,1},{1,0},{2,3},{3,2},{4,5},{5,4},{6,7},{7,6},{8,9},{9,8},{10,11... | collective-permute-start | bytes 393224 | tf_op jit(solution)/shard_map/ppermute | solution.py:502

commit v8 on v7

--- a/solution.py
+++ b/solution.py
@@ -282,27 +282,32 @@
     level_ref[...] = mm(stat_ref[...], pick_heads(STATS, own_ref.shape[1]))
 
 
-def combine_kernel(own_ref, level_ref, *rest):
-    received, out_ref = rest[:-1], rest[-1]
-    width = own_ref.shape[1]
-    segs = received[0].shape[0]
-    part = own_ref.shape[0] // segs
+def combine_kernel(each, *refs):
+    out_ref = refs[-1]
+    width = out_ref.shape[1]
     pick = pick_heads(STAT_ROWS, width)
-    for segment in range(segs):
-        rows = slice(segment * part, (segment + 1) * part)
-        parts, levels = [own_ref[rows, :]], [level_ref[rows, :]]
-        for ref in received:
-            parts.append(ref[segment, :part, :].astype(F32))
-            stats = ref[segment, part:, :STATS]
-            levels.append(
-                lax.dot_general(
-                    stats, pick, (((0,), (0,)), ((), ())), preferred_element_type=F32
-                )[:part]
-            )
-        joint = functools.reduce(jnp.maximum, levels)
-        factors = [jnp.exp(level - joint) for level in levels]
-        mixed = sum(value * factor for value, factor in zip(parts, factors))
-        out_ref[rows, :] = (mixed / sum(factors)).astype(BF16)
+    done = 0
+    for group in range(0, len(refs) - 1, each):
+        own_ref, level_ref = refs[group : group + 2]
+        received = refs[group + 2 : group + each]
+        segs = received[0].shape[0]
+        part = own_ref.shape[0] // segs
+        for segment in range(segs):
+            rows = slice(segment * part, (segment + 1) * part)
+            parts, levels = [own_ref[rows, :]], [level_ref[rows, :]]
+            for ref in received:
+                parts.append(ref[segment, :part, :].astype(F32))
+                stats = ref[segment, part:, :STATS]
+                levels.append(
+                    lax.dot_general(
+                        stats, pick, (((0,), (0,)), ((), ())), preferred_element_type=F32
+                    )[:part]
+                )
+            joint = functools.reduce(jnp.maximum, levels)
+            factors = [jnp.exp(level - joint) for level in levels]
+            mixed = sum(value * factor for value, factor in zip(parts, factors))
+            out_ref[done : done + part, :] = (mixed / sum(factors)).astype(BF16)
+            done += part
 
 
 def hidden_kernel(
@@ -410,15 +415,24 @@
                 acc[segment] = acc[segment] * jnp.tile(factor, (1, local // 128)) + update
 
 
-def far_kernel(readers, steps, offsets, pattern_ref, wk_ref, wv_ref, *rest):
+def far_kernel(readers, steps, offsets, base, pattern_ref, *rest):
     spread, max_in, total_in, acc_in = rest[:4]
-    blocks = rest[4 : 4 + 2 * len(steps)]
-    rest = rest[4 + 2 * len(steps) :]
+    rest = rest[4:]
+    projects = base == 0
+    if projects:
+        wk_ref, wv_ref = rest[:2]
+        blocks = rest[2 : 2 + 2 * len(steps)]
+        rest = rest[2 + 2 * len(steps) :]
+    else:
+        key_all, value_all = rest[:2]
+        rest = rest[2:]
     own_ref, own_stat_ref = rest[:2]
     sends = rest[2 : 1 + readers]
-    key_all, value_all, key_buf, value_buf, max_buf, total_buf, acc, full, stat_full = rest[
-        1 + readers :
-    ]
+    rest = rest[1 + readers :]
+    if projects:
+        key_all, value_all = rest[:2]
+        rest = rest[2:]
+    key_buf, value_buf, max_buf, total_buf, acc, full, stat_full = rest
     segs, _, local = spread.shape
     heads = local // HD
     part = own_ref.shape[1]
@@ -431,33 +445,35 @@
     for index, step in enumerate(steps):
         slots += [2 * index + core, 2 * index + 1 - core]
         slot_of[-step], slot_of[step] = 2 * index, 2 * index + 1
-    project_blocks(blocks, slots, wk_ref, wv_ref, key_all, value_all)
+    if projects:
+        project_blocks(blocks, slots, wk_ref, wv_ref, key_all, value_all)
+    held = own_ref.shape[0]
     counts = [
         collect(
-            segment, segs, part, slot_of, offsets, pattern_ref,
+            base + segment, segs, part, slot_of, offsets, pattern_ref,
             (key_all, value_all), (key_buf.at[segment], value_buf.at[segment]),
         )
-        for segment in range(segs)
+        for segment in range(held)
     ]
 
-    for segment in range(segs):
+    for segment in range(held):
         place = lax.broadcasted_iota(jnp.int32, (1, many), 1)
-        scores = nt_dot(spread[segment], key_buf[segment])
+        scores = nt_dot(spread[base + segment], key_buf[segment])
         scores = jnp.where(place < counts[segment] * part, scores, NEG)
-        before = max_in[segment]
+        before = max_in[base + segment]
         top = jnp.max(tile_fold(scores, jnp.maximum), axis=1, keepdims=True)
         peak = jnp.maximum(before, jnp.broadcast_to(top, before.shape))
         max_buf[segment] = peak
         factor = jnp.exp(before - peak)
         weights = jnp.exp(scores - jnp.tile(peak, (1, many // 128)))
         row_total = jnp.sum(
-            total_in[segment] * factor + tile_fold(weights, jnp.add), axis=1, keepdims=True
+            total_in[base + segment] * factor + tile_fold(weights, jnp.add), axis=1, keepdims=True
         )
         total_buf[segment] = jnp.broadcast_to(row_total, before.shape)
-        acc[segment] = acc_in[segment] * jnp.tile(factor, (1, local // 128)) + mm(
+        acc[segment] = acc_in[base + segment] * jnp.tile(factor, (1, local // 128)) + mm(
             weights.astype(BF16), value_buf[segment]
         )
-    for segment in range(segs):
+    for segment in range(held):
         emit(
             segment, max_buf[segment], total_buf[segment], acc.at[segment], heads,
             full.at[segment], stat_full.at[segment], own_ref, own_stat_ref, sends,
@@ -542,9 +558,12 @@
     cross_out_other = swap_cores(cross_out)
     self_out_other = swap_cores(self_out)
 
-    part_outputs = [((segs, part, local), F32), ((segs, part, STATS), BF16)] + [
-        ((segs, part + STAT_ROWS, local), BF16)
-    ] * (readers - 1)
+
+    def part_outputs(held):
+        return [((held, part, local), F32), ((held, part, STATS), BF16)] + [
+            ((held, part + STAT_ROWS, local), BF16)
+        ] * (readers - 1)
+
     work = [pltpu.VMEM((segs, lat_rows, local), F32), pltpu.VMEM((segs, lat_rows, STATS), F32)]
     most = reads * length
     tiles = -(-most // CHUNK)
@@ -552,7 +571,7 @@
     produced = call(
         functools.partial(cross_kernel, readers),
         (band_start, coverage, present, latents, read_tokens, cross_query, cross_key, cross_value),
-        part_outputs,
+        part_outputs(segs),
         specs=[pl.BlockSpec(memory_space=pltpu.HBM)] * 8,
         scratch=[
             pltpu.SMEM(band_start.shape, jnp.int32),
@@ -584,23 +603,27 @@
         limit=60 * 1024 * 1024,
     )
 
-    def combine(parts):
-        own, own_stat, sends = parts[0], parts[1], parts[2:]
-        received = [to_reader(value, step + 1) for step, value in enumerate(sends)]
-        kept, level = call(
-            own_kernel,
-            (own.reshape(size, local), own_stat.reshape(size, STATS)),
-            [((size, local), F32), ((size, local), F32)],
-            estimate=cost(2 * size * STATS * local, 12 * size * local),
-        )
+    def combine(groups):
+        inputs = []
+        for parts in groups:
+            own, own_stat, sends = parts[0], parts[1], parts[2:]
+            rows = own.shape[0] * part
+            received = [to_reader(value, step + 1) for step, value in enumerate(sends)]
+            kept, level = call(
+                own_kernel,
+                (own.reshape(rows, local), own_stat.reshape(rows, STATS)),
+                [((rows, local), F32), ((rows, local), F32)],
+                estimate=cost(2 * rows * STATS * local, 12 * rows * local),
+            )
+            inputs += [kept, level] + received
         return call(
-            combine_kernel,
-            [kept, level] + received,
+            functools.partial(combine_kernel, 1 + readers),
+            inputs,
             [((size, local), BF16)],
             estimate=cost(8 * size * STATS * local, 8 * size * local),
         )[0]
 
-    attended = combine(produced)
+    attended = combine([produced])
     attended_other = swap_cores(attended)
     hidden, normed, query = call(
         hidden_kernel,
@@ -649,27 +672,35 @@
     )
     far = [step for step in steps if step > 1]
     far_blocks = [block for step in far for block in pair[step]]
-    produced = call(
-        functools.partial(far_kernel, readers, tuple(far), tuple(offsets)),
-        (pattern, self_key, self_value, *carried, *far_blocks),
-        part_outputs,
-        specs=[smem()] + [vmem()] * (6 + len(far_blocks)),
-        scratch=[
-            pltpu.VMEM((len(far_blocks) * size, local), BF16),
-            pltpu.VMEM((len(far_blocks) * size, local), BF16),
-            pltpu.VMEM((segs, far_keys, local), BF16),
-            pltpu.VMEM((segs, far_keys, local), BF16),
-            pltpu.VMEM((segs, spread_rows, 128), F32),
-            pltpu.VMEM((segs, spread_rows, 128), F32),
-            pltpu.VMEM((segs, spread_rows, local), F32),
-        ]
-        + work,
-        estimate=cost(
-            4 * segs * far_keys * local * spread_rows, 8 * segs * spread_rows * local
-        ),
-        limit=16 << 20,
-    )
-    mixed = combine(produced)
+    keys_shape = (len(far_blocks) * size, local)
+    groups, projected = [], None
+    half = segs // 2
+    for index, (base, held) in enumerate(((0, half), (half, segs - half))):
+        inputs = (pattern, *carried)
+        inputs += (self_key, self_value, *far_blocks) if index == 0 else projected
+        produced = call(
+            functools.partial(far_kernel, readers, tuple(far), tuple(offsets), base),
+            inputs,
+            part_outputs(held) + [(keys_shape, BF16)] * (2 if index == 0 else 0),
+            specs=[smem()] + [vmem()] * (len(inputs) - 1),
+            scratch=[
+                pltpu.VMEM((held, far_keys, local), BF16),
+                pltpu.VMEM((held, far_keys, local), BF16),
+                pltpu.VMEM((held, spread_rows, 128), F32),
+                pltpu.VMEM((held, spread_rows, 128), F32),
+                pltpu.VMEM((held, spread_rows, local), F32),
+                pltpu.VMEM((held, lat_rows, local), F32),
+                pltpu.VMEM((held, lat_rows, STATS), F32),
+            ],
+            estimate=cost(
+                4 * held * far_keys * local * spread_rows, 8 * held * spread_rows * local
+            ),
+            limit=16 << 20,
+        )
+        if index == 0:
+            projected = tuple(produced[1 + readers :])
+        groups.append(produced[: 1 + readers])
+    mixed = combine(groups)
     mixed_other = swap_cores(mixed)
     return call(
         out_kernel,

time: 56.4 us -> 57.3 us (1.016); the launches traced: 55.3 us -> 56.8 us
  Pallas kernels: 18.1 us -> 19.3 us
  waiting for transfers between devices: 18.4 us -> 19 us
    pallas_call x9 -> x11, Pallas kernels: 18.1 us -> 19.3 us  [call(): pl.pallas_call(kernel, out_shape=[jax.ShapeDtypeStruct(shape, kind) for s...]
    ppermute x3 -> x4, waiting for transfers between devices: 6.89 us -> 7.49 us  [to_reader(): lax.ppermute(value, 'read', [(i, (i + step) % readers) for i in range(rea...]
    ppermute x3 -> x4, starting transfers between devices: 8.1 us -> 8.12 us  [to_reader(): lax.ppermute(value, 'read', [(i, (i + step) % readers) for i in range(rea...]
  transfers between devices with their start and end apart: 11 -> 12, of which waited for: 7 -> 7; matrix products, arithmetic and copies ran while one was open for 0% -> 0% of each run, Pallas kernels for 7% -> 13%
where the time goes in v8:
time: 57.3 us; the launch traced here: 56.8 us
  Pallas kernels  19.3 us (34%)
  waiting for transfers between devices  19 us (33%)
  starting transfers between devices  16.6 us (29%)
  local copies, waits for them, and re-layouts  1.82 us (3%)
    pallas_call x11, Pallas kernels, call(): pl.pallas_call(kernel, out_shape=[jax.ShapeDtypeStruct(shape, kind) for s...  19.3 us
    ppermute x2, waiting for transfers between devices, both_ways(): return lax.ppermute(value, ('pos', 'head'), moves)  9.58 us
    ppermute x6, starting transfers between devices, swap_cores(): return lax.ppermute(value, 'head', [(0, 1), (1, 0)])  8.2 us
    ppermute x4, starting transfers between devices, to_reader(): lax.ppermute(value, 'read', [(i, (i + step) % readers) for i in range(rea...  8.12 us
    ppermute x4, waiting for transfers between devices, to_reader(): lax.ppermute(value, 'read', [(i, (i + step) % readers) for i in range(rea...  7.49 us
    ppermute x6, waiting for transfers between devices, swap_cores(): return lax.ppermute(value, 'head', [(0, 1), (1, 0)])  1.98 us
    unnamed x18, local copies, waits for them, and re-layouts  1.82 us
  transfers between devices with their start and end apart: 12, of which 7 were waited for; matrix products, arithmetic and copies ran while one was open for 0% of the time, Pallas kernels for 13%

profile of v8, /device:TPU:9, one launch (start us, length us, event | category | flops | bytes accessed | tf_op | source)
XLA Modules:
  0.0 56.8 jit_solution(15222564523465547388)
XLA Ops:
  0.0 10.5 %shard_map.136 = (f32[4,64,256]{2,1,0:T(8,128)}, bf16[4,64,128]{2,1,0:T(8,128)(2,1)}, bf16[4,80,256]{2,1,0:T(8,128)(2,1)}) custom-call(s32[4,4]{1,0:T(4,128)} %start_hbm.1, s32[4,4]{1,0:T(4,128)} %cov_hbm.1, s32[4,4]{1,0:T(4,128)} %present_hbm.1, bf16[4,128,512]{2,1,0:T(8,128)(2,1)} %lat_ref.1, bf16[4,4,512,512]{3,2,1,0:T(8,128)(2,1)} %tok_ref.1, ...), custom_call_target="tpu_custom_call" | custom-call | flops 8589934592 | bytes 8388608 | tf_op jit(solution)/shard_map/pallas_call | solution.py:506
  10.5 5.2 %collective-permute-start = (bf16[4,80,256]{2,1,0:T(8,128)(2,1)}, bf16[4,80,256]{2,1,0:T(8,128)(2,1)S(1)}, u32[]{:S(2)}, u32[]{:S(2)}) collective-permute-start(bf16[4,80,256]{2,1,0:T(8,128)(2,1)} %get-tuple-element.33), channel_id=1, source_target_pairs={{0,2},{2,0},{1,3},{3,1},{4,6},{6,4},{5,7},{7,5},{8,10},{10,8},{9,1... | collective-permute-start | bytes 491528 | tf_op jit(solution)/shard_map/ppermute | solution.py:523
  15.7 1.0 %collective-permute-start.2 = (bf16[256,512]{1,0:T(8,128)(2,1)S(1)}, bf16[256,512]{1,0:T(8,128)(2,1)S(1)}, u32[]{:S(2)}, u32[]{:S(2)}) collective-permute-start(bf16[256,512]{1,0:T(8,128)(2,1)S(1)} %copy-done.4), channel_id=1, source_target_pairs={{0,1},{1,0},{2,3},{3,2},{4,5},{5,4},{6,7},{7,6},{8,9},{9,8},{10,11... | collective-permute-start | bytes 786440 | tf_op jit(solution)/shard_map/ppermute | solution.py:518
  16.6 0.9 %copy-done.3 = f32[4,64,256]{2,1,0:T(8,128)S(1)} copy-done((f32[4,64,256]{2,1,0:T(8,128)S(1)}, f32[4,64,256]{2,1,0:T(8,128)}, u32[]{:S(2)}) %copy-start.3) | copy-done | bytes 262168
  17.6 0.8 %copy-done.7 = bf16[4,64,128]{2,1,0:T(8,128)(2,1)S(1)} copy-done((bf16[4,64,128]{2,1,0:T(8,128)(2,1)S(1)}, bf16[4,64,128]{2,1,0:T(8,128)(2,1)}, u32[]{:S(2)}) %copy-start.7) | copy-done | bytes 65560
  18.6 1.2 %collective-permute-done.refs_2_ = bf16[4,80,256]{2,1,0:T(8,128)(2,1)S(1)} collective-permute-done((bf16[4,80,256]{2,1,0:T(8,128)(2,1)}, bf16[4,80,256]{2,1,0:T(8,128)(2,1)S(1)}, u32[]{:S(2)}, u32[]{:S(2)}) %collective-permute-start) | collective-permute-done | bytes 163872 | tf_op jit(solution)/shard_map/ppermute | solution.py:523
  19.8 0.3 shard_map.138.own_ref
  20.1 1.3 %collective-permute-start.1 = (bf16[256,256]{1,0:T(8,128)(2,1)S(1)}, bf16[256,256]{1,0:T(8,128)(2,1)S(1)}, u32[]{:S(2)}, u32[]{:S(2)}) collective-permute-start(bf16[256,256]{1,0:T(8,128)(2,1)S(1)} %shard_map.138.own_ref), channel_id=1, source_target_pairs={{0,1},{1,0},{2,3},{3,2},{4,5},{5,4},{6,7},{7,6},{8,9},{9,8},{10,11... | collective-permute-start | bytes 393224 | tf_op jit(solution)/shard_map/ppermute | solution.py:518
  21.4 1.0 %collective-permute-done.1.other_ref = bf16[256,256]{1,0:T(8,128)(2,1)S(1)} collective-permute-done((bf16[256,256]{1,0:T(8,128)(2,1)S(1)}, bf16[256,256]{1,0:T(8,128)(2,1)S(1)}, u32[]{:S(2)}, u32[]{:S(2)}) %collective-permute-start.1) | collective-permute-done | bytes 131104 | tf_op jit(solution)/shard_map/ppermute | solution.py:518
  22.4 0.6 %shard_map.139 = (f32[256,512]{1,0:T(8,128)S(1)}, bf16[256,512]{1,0:T(8,128)(2,1)S(1)}, bf16[256,256]{1,0:T(8,128)(2,1)S(1)}) custom-call(bf16[4,128,512]{2,1,0:T(8,128)(2,1)S(1)} %copy-done, bf16[256,256]{1,0:T(8,128)(2,1)S(1)} %shard_map.138.own_ref, bf16[256,256]{1,0:T(8,128)(2,1)S(1)} %collective-permute-done.1.other_ref, ...), custom_call_target="tpu_custom_call" | custom-call | flops 201326592 | bytes 1048576 | tf_op jit(solution)/shard_map/pallas_call | solution.py:506
  23.3 5.3 %collective-permute-done.4.rest_3_ = bf16[256,512]{1,0:T(8,128)(2,1)S(1)} collective-permute-done((bf16[256,512]{1,0:T(8,128)(2,1)S(1)}, bf16[256,512]{1,0:T(8,128)(2,1)S(1)}, u32[]{:S(2)}, u32[]{:S(2)}) %collective-permute-start.4) | collective-permute-done | bytes 262176 | tf_op jit(solution)/shard_map/ppermute | solution.py:531
  28.6 1.2 %collective-permute-start.5 = (bf16[256,512]{1,0:T(8,128)(2,1)S(1)}, bf16[256,512]{1,0:T(8,128)(2,1)S(1)}, u32[]{:S(2)}, u32[]{:S(2)}) collective-permute-start(bf16[256,512]{1,0:T(8,128)(2,1)S(1)} %collective-permute-done.4.rest_3_), channel_id=1, source_target_pairs={{0,1},{1,0},{2,3},{3,2},{4,5},{5,4},{6,7},{7,6},{8,9},{9,8},{10,11... | collective-permute-start | bytes 786440 | tf_op jit(solution)/shard_map/ppermute | solution.py:518
  29.8 4.3 %collective-permute-done.6.rest_6_ = bf16[256,512]{1,0:T(8,128)(2,1)S(1)} collective-permute-done((bf16[256,512]{1,0:T(8,128)(2,1)S(1)}, bf16[256,512]{1,0:T(8,128)(2,1)S(1)}, u32[]{:S(2)}, u32[]{:S(2)}) %collective-permute-start.6) | collective-permute-done | bytes 262176 | tf_op jit(solution)/shard_map/ppermute | solution.py:531
  34.1 2.1 %collective-permute-start.7 = (bf16[256,512]{1,0:T(8,128)(2,1)S(1)}, bf16[256,512]{1,0:T(8,128)(2,1)S(1)}, u32[]{:S(2)}, u32[]{:S(2)}) collective-permute-start(bf16[256,512]{1,0:T(8,128)(2,1)S(1)} %collective-permute-done.6.rest_6_), channel_id=1, source_target_pairs={{0,1},{1,0},{2,3},{3,2},{4,5},{5,4},{6,7},{7,6},{8,9},{9,8},{10,11... | collective-permute-start | bytes 786440 | tf_op jit(solution)/shard_map/ppermute | solution.py:518
  36.2 1.5 %collective-permute-start.3 = (bf16[256,256]{1,0:T(8,128)(2,1)S(1)}, bf16[256,256]{1,0:T(8,128)(2,1)S(1)}, u32[]{:S(2)}, u32[]{:S(2)}) collective-permute-start(bf16[256,256]{1,0:T(8,128)(2,1)S(1)} %get-tuple-element.35.rest_0_), channel_id=1, source_target_pairs={{0,2},{2,0},{1,3},{3,1},{4,6},{6,4},{5,7},{7,5},{8,10},{10,8},{9,1... | collective-permute-start | bytes 393224 | tf_op jit(solution)/shard_map/ppermute | solution.py:523
  37.9 3.3 %collective-permute-done.3.rest_1_ = bf16[256,256]{1,0:T(8,128)(2,1)S(1)} collective-permute-done((bf16[256,256]{1,0:T(8,128)(2,1)S(1)}, bf16[256,256]{1,0:T(8,128)(2,1)S(1)}, u32[]{:S(2)}, u32[]{:S(2)}) %collective-permute-start.3) | collective-permute-done | bytes 131104 | tf_op jit(solution)/shard_map/ppermute | solution.py:523
  41.3 2.9 %shard_map.140 = (bf16[4,512,256]{2,1,0:T(8,128)(2,1)S(1)}, f32[4,512,128]{2,1,0:T(8,128)S(1)}, f32[4,512,128]{2,1,0:T(8,128)S(1)}, f32[4,512,256]{2,1,0:T(8,128)S(1)}) custom-call(s32[4,16]{1,0:T(4,128)S(1)} %copy-done.8, bf16[512,256]{1,0:T(8,128)(2,1)S(1)} %copy-done.1, bf16[512,256]{1,0:T(8,128)(2,1)S(1)} %copy-done.2, ...), custom_call_target="tpu_custom_call" | custom-call | flops 1073741824 | bytes 4194304 | tf_op jit(solution)/shard_map/pallas_call | solution.py:506
  44.2 1.8 %shard_map.141 = (f32[2,64,256]{2,1,0:T(8,128)S(1)}, bf16[2,64,128]{2,1,0:T(8,128)(2,1)S(1)}, bf16[2,80,256]{2,1,0:T(8,128)(2,1)S(1)}, bf16[512,256]{1,0:T(8,128)(2,1)S(1)}, bf16[512,256]{1,0:T(8,128)(2,1)S(1)}) custom-call(s32[4,16]{1,0:T(4,128)S(1)} %copy-done.8, bf16[4,512,256]{2,1,0:T(8,128)(2,1)S(1)} %get-tuple-element.37.rest_0_, ...), custom_call_target="tpu_custom_call" | custom-call | flops 134217728 | bytes 2097152 | tf_op jit(solution)/shard_map/pallas_call | solution.py:506
  45.9 1.5 %collective-permute-start.8 = (bf16[2,80,256]{2,1,0:T(8,128)(2,1)S(1)}, bf16[2,80,256]{2,1,0:T(8,128)(2,1)S(1)}, u32[]{:S(2)}, u32[]{:S(2)}) collective-permute-start(bf16[2,80,256]{2,1,0:T(8,128)(2,1)S(1)} %get-tuple-element.45), channel_id=1, source_target_pairs={{0,2},{2,0},{1,3},{3,1},{4,6},{6,4},{5,7},{7,5},{8,10},{10,8},{9,1... | collective-permute-start | bytes 245768 | tf_op jit(solution)/shard_map/ppermute | solution.py:523
  47.4 1.6 %shard_map.143 = (f32[2,64,256]{2,1,0:T(8,128)S(1)}, bf16[2,64,128]{2,1,0:T(8,128)(2,1)S(1)}, bf16[2,80,256]{2,1,0:T(8,128)(2,1)S(1)}) custom-call(s32[4,16]{1,0:T(4,128)S(1)} %copy-done.8, bf16[4,512,256]{2,1,0:T(8,128)(2,1)S(1)} %get-tuple-element.37.rest_0_, f32[4,512,128]{2,1,0:T(8,128)S(1)} %get-tuple-element.38.rest_1_, ...), custom_call_target="tpu_custom_call" | custom-call | flops 134217728 | bytes 2097152 | tf_op jit(solution)/shard_map/pallas_call | solution.py:506
  49.3 3.0 %collective-permute-done.9.refs_5_ = bf16[2,80,256]{2,1,0:T(8,128)(2,1)S(1)} collective-permute-done((bf16[2,80,256]{2,1,0:T(8,128)(2,1)S(1)}, bf16[2,80,256]{2,1,0:T(8,128)(2,1)S(1)}, u32[]{:S(2)}, u32[]{:S(2)}) %collective-permute-start.9) | collective-permute-done | bytes 81952 | tf_op jit(solution)/shard_map/ppermute | solution.py:523
  52.6 2.4 %collective-permute-start.10 = (bf16[256,256]{1,0:T(8,128)(2,1)S(1)}, bf16[256,256]{1,0:T(8,128)(2,1)S(1)}, u32[]{:S(2)}, u32[]{:S(2)}) collective-permute-start(bf16[256,256]{1,0:T(8,128)(2,1)S(1)} %shard_map.145.own_ref), channel_id=1, source_target_pairs={{0,1},{1,0},{2,3},{3,2},{4,5},{5,4},{6,7},{7,6},{8,9},{9,8},{10,11... | collective-permute-start | bytes 393224 | tf_op jit(solution)/shard_map/ppermute | solution.py:518
  55.0 1.0 %collective-permute-done.10.other_ref = bf16[256,256]{1,0:T(8,128)(2,1)S(1)} collective-permute-done((bf16[256,256]{1,0:T(8,128)(2,1)S(1)}, bf16[256,256]{1,0:T(8,128)(2,1)S(1)}, u32[]{:S(2)}, u32[]{:S(2)}) %collective-permute-start.10) | collective-permute-done | bytes 131104 | tf_op jit(solution)/shard_map/ppermute | solution.py:518
  55.9 0.9 %shard_map.146 = bf16[4,64,256]{2,1,0:T(8,128)(2,1)} custom-call(f32[256,512]{1,0:T(8,128)S(1)} %get-tuple-element.34.hid_ref, bf16[256,256]{1,0:T(8,128)(2,1)S(1)} %shard_map.145.own_ref, bf16[256,256]{1,0:T(8,128)(2,1)S(1)} %collective-permute-done.10.other_ref, bf16[256,512]{1,0:T(8,128)(2,1)S(1)} %copy-done.6, ...), custom_call_target="tpu_custom_call" | custom-call | flops 67108864 | bytes 1048576 | tf_op jit(solution)/shard_map/pallas_call | solution.py:506
  (29 shorter events, 1.3 us)
Async XLA Ops:
  0.0 22.4 %copy-start = (bf16[4,128,512]{2,1,0:T(8,128)(2,1)S(1)}, bf16[4,128,512]{2,1,0:T(8,128)(2,1)}, u32[]{:S(2)}) copy-start(bf16[4,128,512]{2,1,0:T(8,128)(2,1)} %lat_ref.1) | copy-start | bytes 1572868
  0.0 15.7 %copy-start.4 = (bf16[256,512]{1,0:T(8,128)(2,1)S(1)}, bf16[256,512]{1,0:T(8,128)(2,1)}, u32[]{:S(2)}) copy-start(bf16[256,512]{1,0:T(8,128)(2,1)} %wo_ref.2) | copy-start | bytes 786436
  0.0 22.4 %copy-start.5 = (bf16[512,256]{1,0:T(8,128)(2,1)S(1)}, bf16[512,256]{1,0:T(8,128)(2,1)}, u32[]{:S(2)}) copy-start(bf16[512,256]{1,0:T(8,128)(2,1)} %wq_ref.1) | copy-start | bytes 786436
  0.0 37.7 %copy-start.6 = (bf16[256,512]{1,0:T(8,128)(2,1)S(1)}, bf16[256,512]{1,0:T(8,128)(2,1)}, u32[]{:S(2)}) copy-start(bf16[256,512]{1,0:T(8,128)(2,1)} %wo_ref.3) | copy-start | bytes 786436
  0.0 41.2 %copy-start.8 = (s32[4,16]{1,0:T(4,128)S(1)}, s32[4,16]{1,0:T(4,128)}, u32[]{:S(2)}) copy-start(s32[4,16]{1,0:T(4,128)} %pattern_ref.5) | copy-start | bytes 772
  0.0 41.2 %copy-start.1 = (bf16[512,256]{1,0:T(8,128)(2,1)S(1)}, bf16[512,256]{1,0:T(8,128)(2,1)}, u32[]{:S(2)}) copy-start(bf16[512,256]{1,0:T(8,128)(2,1)} %rest_4_.1) | copy-start | bytes 786436
  0.0 41.2 %copy-start.2 = (bf16[512,256]{1,0:T(8,128)(2,1)S(1)}, bf16[512,256]{1,0:T(8,128)(2,1)}, u32[]{:S(2)}) copy-start(bf16[512,256]{1,0:T(8,128)(2,1)} %rest_5_.1) | copy-start | bytes 786436
  10.5 9.3 %collective-permute-start = (bf16[4,80,256]{2,1,0:T(8,128)(2,1)}, bf16[4,80,256]{2,1,0:T(8,128)(2,1)S(1)}, u32[]{:S(2)}, u32[]{:S(2)}) collective-permute-start(bf16[4,80,256]{2,1,0:T(8,128)(2,1)} %get-tuple-element.33), channel_id=1, source_target_pairs={{0,2},{2,0},{1,3},{3,1},{4,6},{6,4},{5,7},{7,5},{8,10},{10,8},{9,1... | collective-permute-start | bytes 491528 | tf_op jit(solution)/shard_map/ppermute | solution.py:523
  15.7 5.7 %collective-permute-start.2 = (bf16[256,512]{1,0:T(8,128)(2,1)S(1)}, bf16[256,512]{1,0:T(8,128)(2,1)S(1)}, u32[]{:S(2)}, u32[]{:S(2)}) collective-permute-start(bf16[256,512]{1,0:T(8,128)(2,1)S(1)} %copy-done.4), channel_id=1, source_target_pairs={{0,1},{1,0},{2,3},{3,2},{4,5},{5,4},{6,7},{7,6},{8,9},{9,8},{10,11... | collective-permute-start | bytes 786440 | tf_op jit(solution)/shard_map/ppermute | solution.py:518
  16.6 0.9 %copy-start.3 = (f32[4,64,256]{2,1,0:T(8,128)S(1)}, f32[4,64,256]{2,1,0:T(8,128)}, u32[]{:S(2)}) copy-start(f32[4,64,256]{2,1,0:T(8,128)} %get-tuple-element.29) | copy-start | bytes 786436
  17.6 0.8 %copy-start.7 = (bf16[4,64,128]{2,1,0:T(8,128)(2,1)S(1)}, bf16[4,64,128]{2,1,0:T(8,128)(2,1)}, u32[]{:S(2)}) copy-start(bf16[4,64,128]{2,1,0:T(8,128)(2,1)} %get-tuple-element.30) | copy-start | bytes 196612
  20.1 2.3 %collective-permute-start.1 = (bf16[256,256]{1,0:T(8,128)(2,1)S(1)}, bf16[256,256]{1,0:T(8,128)(2,1)S(1)}, u32[]{:S(2)}, u32[]{:S(2)}) collective-permute-start(bf16[256,256]{1,0:T(8,128)(2,1)S(1)} %shard_map.138.own_ref), channel_id=1, source_target_pairs={{0,1},{1,0},{2,3},{3,2},{4,5},{5,4},{6,7},{7,6},{8,9},{9,8},{10,11... | collective-permute-start | bytes 393224 | tf_op jit(solution)/shard_map/ppermute | solution.py:518
  23.1 5.5 %collective-permute-start.4 = (bf16[256,512]{1,0:T(8,128)(2,1)S(1)}, bf16[256,512]{1,0:T(8,128)(2,1)S(1)}, u32[]{:S(2)}, u32[]{:S(2)}) collective-permute-start(bf16[256,512]{1,0:T(8,128)(2,1)S(1)} %get-tuple-element.36.rest_2_), channel_id=1, source_target_pairs={{0,4},{4,8},{8,12},{12,13},{13,9},{9,5},{5,1},{1,0},{2,6},{6,10},{... | collective-permute-start | bytes 786440 | tf_op jit(solution)/shard_map/ppermute | solution.py:531
  28.6 5.5 %collective-permute-start.6 = (bf16[256,512]{1,0:T(8,128)(2,1)S(1)}, bf16[256,512]{1,0:T(8,128)(2,1)S(1)}, u32[]{:S(2)}, u32[]{:S(2)}) collective-permute-start(bf16[256,512]{1,0:T(8,128)(2,1)S(1)} %collective-permute-done.4.rest_3_), channel_id=1, source_target_pairs={{0,4},{4,8},{8,12},{12,13},{13,9},{9,5},{5,1},{1,0},{2,6},{6,10},{... | collective-permute-start | bytes 786440 | tf_op jit(solution)/shard_map/ppermute | solution.py:531
  28.6 12.6 %collective-permute-start.5 = (bf16[256,512]{1,0:T(8,128)(2,1)S(1)}, bf16[256,512]{1,0:T(8,128)(2,1)S(1)}, u32[]{:S(2)}, u32[]{:S(2)}) collective-permute-start(bf16[256,512]{1,0:T(8,128)(2,1)S(1)} %collective-permute-done.4.rest_3_), channel_id=1, source_target_pairs={{0,1},{1,0},{2,3},{3,2},{4,5},{5,4},{6,7},{7,6},{8,9},{9,8},{10,11... | collective-permute-start | bytes 786440 | tf_op jit(solution)/shard_map/ppermute | solution.py:518
  34.1 10.0 %collective-permute-start.7 = (bf16[256,512]{1,0:T(8,128)(2,1)S(1)}, bf16[256,512]{1,0:T(8,128)(2,1)S(1)}, u32[]{:S(2)}, u32[]{:S(2)}) collective-permute-start(bf16[256,512]{1,0:T(8,128)(2,1)S(1)} %collective-permute-done.6.rest_6_), channel_id=1, source_target_pairs={{0,1},{1,0},{2,3},{3,2},{4,5},{5,4},{6,7},{7,6},{8,9},{9,8},{10,11... | collective-permute-start | bytes 786440 | tf_op jit(solution)/shard_map/ppermute | solution.py:518
  36.2 5.1 %collective-permute-start.3 = (bf16[256,256]{1,0:T(8,128)(2,1)S(1)}, bf16[256,256]{1,0:T(8,128)(2,1)S(1)}, u32[]{:S(2)}, u32[]{:S(2)}) collective-permute-start(bf16[256,256]{1,0:T(8,128)(2,1)S(1)} %get-tuple-element.35.rest_0_), channel_id=1, source_target_pairs={{0,2},{2,0},{1,3},{3,1},{4,6},{6,4},{5,7},{7,5},{8,10},{10,8},{9,1... | collective-permute-start | bytes 393224 | tf_op jit(solution)/shard_map/ppermute | solution.py:523
  37.7 17.3 %collective-permute-start.11 = (bf16[256,512]{1,0:T(8,128)(2,1)S(1)}, bf16[256,512]{1,0:T(8,128)(2,1)S(1)}, u32[]{:S(2)}, u32[]{:S(2)}) collective-permute-start(bf16[256,512]{1,0:T(8,128)(2,1)S(1)} %copy-done.6), channel_id=1, source_target_pairs={{0,1},{1,0},{2,3},{3,2},{4,5},{5,4},{6,7},{7,6},{8,9},{9,8},{10,11... | collective-permute-start | bytes 786440 | tf_op jit(solution)/shard_map/ppermute | solution.py:518
  45.9 3.4 %collective-permute-start.8 = (bf16[2,80,256]{2,1,0:T(8,128)(2,1)S(1)}, bf16[2,80,256]{2,1,0:T(8,128)(2,1)S(1)}, u32[]{:S(2)}, u32[]{:S(2)}) collective-permute-start(bf16[2,80,256]{2,1,0:T(8,128)(2,1)S(1)} %get-tuple-element.45), channel_id=1, source_target_pairs={{0,2},{2,0},{1,3},{3,1},{4,6},{6,4},{5,7},{7,5},{8,10},{10,8},{9,1... | collective-permute-start | bytes 245768 | tf_op jit(solution)/shard_map/ppermute | solution.py:523
  49.0 3.3 %collective-permute-start.9 = (bf16[2,80,256]{2,1,0:T(8,128)(2,1)S(1)}, bf16[2,80,256]{2,1,0:T(8,128)(2,1)S(1)}, u32[]{:S(2)}, u32[]{:S(2)}) collective-permute-start(bf16[2,80,256]{2,1,0:T(8,128)(2,1)S(1)} %get-tuple-element.52), channel_id=1, source_target_pairs={{0,2},{2,0},{1,3},{3,1},{4,6},{6,4},{5,7},{7,5},{8,10},{10,8},{9,1... | collective-permute-start | bytes 245768 | tf_op jit(solution)/shard_map/ppermute | solution.py:523
  52.6 3.3 %collective-permute-start.10 = (bf16[256,256]{1,0:T(8,128)(2,1)S(1)}, bf16[256,256]{1,0:T(8,128)(2,1)S(1)}, u32[]{:S(2)}, u32[]{:S(2)}) collective-permute-start(bf16[256,256]{1,0:T(8,128)(2,1)S(1)} %shard_map.145.own_ref), channel_id=1, source_target_pairs={{0,1},{1,0},{2,3},{3,2},{4,5},{5,4},{6,7},{7,6},{8,9},{9,8},{10,11... | collective-permute-start | bytes 393224 | tf_op jit(solution)/shard_map/ppermute | solution.py:518
